TPU v7x, 512 devices: a whole 4x8x8 slice. The times are simulated.
512 devices in a mesh: rot: 32 (over y, x_hi, core), tag: 16 (over z, x_lo).
Axes of the slice: x: 4 (x_hi: 2, x_lo: 2; x = x_hi * 2 + x_lo), y: 8, z: 8, core: 2. Of those that a mesh axis runs over, the one named last changes fastest.
Arguments:
- user_factors: bfloat16 [262144, 512], P(('rot', 'tag')), may hold values from -1.1953125 to 1.1953125
- item_factors: bfloat16 [32768, 512], P('rot'), may hold values from -1.1953125 to 1.1953125
- tag_factors: bfloat16 [8192, 512], P('tag'), may hold values from -1.1953125 to 1.1953125
- rating_tiles: int32 [8192, 2], P(('rot', 'tag')), may hold values from 0 to 7, as said below
- rating_counts: int32 [512], P(('rot', 'tag')), may hold values from 1 to 16, as said below
- ratings: bfloat16 [8192, 128, 128], P(('rot', 'tag')), may hold values from -6 to 6
- tag_tiles: int32 [8192, 2], P(('rot', 'tag')), may hold values from 0 to 7, as said below
- tag_values: bfloat16 [8192, 128, 128], P(('rot', 'tag')), may hold values from -6 to 6
Outputs:
- new_users: bfloat16 [262144, 512], P(('rot', 'tag'))
- rotated_items: bfloat16 [32768, 512], P('rot')
- new_tags: bfloat16 [8192, 512], P('tag')
Inputs may be any that keep to these rules, and one draw needn't show every extreme that they name: `rating_tiles`: each device's 16 slots hold distinct tiles; column 0 is below 4, column 1 below 8. `rating_counts`: uneven over devices; some device has all 16 slots live. `tag_tiles`: each device has exactly 16 distinct tiles; column 0 is below 8, column 1 below 4.
All inputs are finite; a program needn't handle non-finite values.
Results may differ from a plain program's by a relative error of at most 0.0043.
Values may be sent and summed in bfloat16 or wider, within the bound.
No kernel may reach another device: no remote copies, remote signals or barrier semaphores. Data moves between devices by JAX's collectives and lax.ppermute only.
A program may use at most 64 MiB of HBM per device.

v0:
```python
import jax
import jax.numpy as jnp
from jax import lax
from jax.sharding import PartitionSpec as P

TILE = 128


def shifted(block, axis, distance):
    devices = range(lax.axis_size(axis))
    route = [((i - distance) % len(devices), i) for i in devices]
    return lax.ppermute(block, axis, route)


def spread_tiles(index, count, tiles):
    empty = jnp.zeros((count,) + tiles.shape[1:], jnp.float32)
    return empty.at[index].add(tiles)


def on_device(
    user_factors,
    item_factors,
    tag_factors,
    rating_tiles,
    rating_counts,
    ratings,
    tag_tiles,
    tag_values,
):
    user_count = user_factors.shape[0]
    item_count = item_factors.shape[0]
    tag_count = tag_factors.shape[0]
    rank = user_factors.shape[1]
    ublock = user_factors.reshape(user_count // TILE, TILE, rank)
    vblock = item_factors.reshape(item_count // TILE, TILE, rank)
    wblock = tag_factors.reshape(tag_count // TILE, TILE, rank)
    user_tiles = ublock[rating_tiles[:, 0]]
    item_tiles = vblock[rating_tiles[:, 1]]
    predicted = jnp.einsum(
        "sur,sir->sui", user_tiles, item_tiles, preferred_element_type=jnp.float32
    )
    live = (jnp.arange(rating_tiles.shape[0]) < rating_counts[0])[:, None, None]
    rating_err = jnp.where(live, predicted - ratings.astype(jnp.float32), 0.0).astype(jnp.bfloat16)
    user_part = jnp.einsum(
        "sui,sir->sur", rating_err, item_tiles, preferred_element_type=jnp.float32
    )
    item_part = jnp.einsum(
        "sui,sur->sir", rating_err, user_tiles, preferred_element_type=jnp.float32
    )
    item_rows = vblock[tag_tiles[:, 0]]
    tag_rows = wblock[tag_tiles[:, 1]]
    tag_err = (
        jnp.einsum("sir,sjr->sij", item_rows, tag_rows, preferred_element_type=jnp.float32)
        - tag_values.astype(jnp.float32)
    ).astype(jnp.bfloat16)
    item_from_tags = jnp.einsum(
        "sij,sjr->sir", tag_err, tag_rows, preferred_element_type=jnp.float32
    )
    tag_part = jnp.einsum("sij,sir->sjr", tag_err, item_rows, preferred_element_type=jnp.float32)
    user_grad = spread_tiles(rating_tiles[:, 0], user_count // TILE, user_part).reshape(
        user_count, rank
    )
    item_grad = spread_tiles(rating_tiles[:, 1], item_count // TILE, item_part)
    item_grad = item_grad.at[tag_tiles[:, 0]].add(item_from_tags).reshape(item_count, rank)
    tag_grad = spread_tiles(tag_tiles[:, 1], tag_count // TILE, tag_part).reshape(tag_count, rank)
    users32 = user_factors.astype(jnp.float32)
    new_users = (users32 - 0.04 * (user_grad + 0.05 * users32)).astype(jnp.bfloat16)
    total = lax.psum(item_grad, "tag")
    items32 = item_factors.astype(jnp.float32)
    new_items = (items32 - 0.04 * (total + 0.05 * items32)).astype(jnp.bfloat16)
    rotated_items = shifted(new_items, "rot", 1)
    tag_total = lax.psum(tag_grad, "rot")
    tags32 = tag_factors.astype(jnp.float32)
    new_tags = (tags32 - 0.04 * (tag_total + 0.05 * tags32)).astype(jnp.bfloat16)
    return (new_users, rotated_items, new_tags)


def solution(mesh):
    placed = (
        P(("rot", "tag"), None),
        P("rot", None),
        P("tag", None),
        P(("rot", "tag"), None),
        P(("rot", "tag")),
        P(("rot", "tag"), None, None),
        P(("rot", "tag"), None),
        P(("rot", "tag"), None, None),
    )
    return jax.shard_map(
        on_device,
        mesh=mesh,
        in_specs=placed,
        out_specs=(P(("rot", "tag"), None), P("rot", None), P("tag", None)),
        check_vma=False,
    )
```

profile of v0, /device:TPU:1, one launch (start us, length us, event | category | flops | bytes accessed | tf_op | source)
XLA Modules:
  0.0 487.2 jit_solution(15541563892529906015)
XLA Ops:
  7.2 0.0 all-reduce.3.cloned.1.call-start
  7.2 0.8 fusion.13
  8.6 0.0 copy-start.2
  8.7 3.2 gather_fusion
  11.8 0.0 copy-done.2
  11.8 0.7 gather_fusion.1
  12.5 0.0 copy-start.7
  12.5 0.0 copy-start.9
  12.5 3.2 fusion.4
  15.7 0.0 copy-done.7
  15.7 0.0 copy-done.9
  15.7 0.0 copy-start.11
  15.7 0.0 copy-start.13
  15.8 2.7 fusion.17
  18.5 0.0 copy-done.11
  18.5 0.0 copy-done.13
  18.5 0.7 gather_fusion.2
  19.2 0.0 copy-start.3
  19.2 3.4 gather_fusion.3
  22.6 0.0 copy-done.3
  22.6 0.0 copy-start.4
  22.6 2.5 fusion.5
  25.1 0.0 copy-done.4
  25.2 0.0 copy-start.10
  25.2 2.7 fusion.18
  27.9 0.0 copy-done.10
  27.9 0.2 broadcast_in_dim.16
  28.1 6.2 %scatter_fusion.1 = f32[8,128,512]{2,1,0:T(8,128)S(1)} fusion(f32[8,128,512]{2,1,0:T(8,128)S(1)} %broadcast_in_dim.16, s32[16]{0:T(128)S(1)} %get-tuple-element.5, f32[16,128,512]{2,1,0:T(8,128)} %fusion.17), kind=kCustom, calls=%fused_computation.5 | custom fusion | flops 1048576 | bytes 12582976 | tf_op jit(solution)/shard_map/scatter-add | solution.py:17
  34.3 6.2 %scatter_fusion.2 = f32[8,128,512]{2,1,0:T(8,128)S(1)} fusion(f32[8,128,512]{2,1,0:T(8,128)S(1)} %scatter_fusion.1, s32[16]{0:T(128)S(1)} %get-tuple-element.4, f32[16,128,512]{2,1,0:T(8,128)} %fusion.18), kind=kCustom, calls=%fused_computation.6 | custom fusion | flops 1048576 | bytes 12582976 | tf_op jit(solution)/shard_map/scatter-add | solution.py:64
  40.5 0.0 copy-start
  40.5 1.4 copy-done
  41.8 0.0 all-reduce.3.cloned.1.call-update
  41.9 0.0 all-reduce.5.cloned.1.call-start
  41.9 4.5 fusion.19
  46.4 0.1 broadcast.30.clone.1
  46.5 6.1 %scatter_fusion.3 = f32[4,128,512]{2,1,0:T(8,128)S(1)} fusion(f32[4,128,512]{2,1,0:T(8,128)S(1)} %broadcast.30.clone.1, s32[16]{0:T(128)S(1)} %get-tuple-element.3, f32[16,128,512]{2,1,0:T(8,128)} %fusion.19), kind=kCustom, calls=%fused_computation.7 | custom fusion | flops 1048576 | bytes 12582976 | tf_op jit(solution)/shard_map/scatter-add | solution.py:17
  52.6 0.0 copy-start.1
  52.6 1.0 copy-done.1
  53.6 0.0 all-reduce.5.cloned.1.call-update
  53.6 0.0 copy-start.8
  53.6 136.6 %all-reduce.3.cloned.1.call-done = f32[1024,512]{1,0:T(8,128)} async-done(((f32[1024,512]{1,0:T(8,128)}), f32[1024,512]{1,0:T(8,128)}) %all-reduce.3.cloned.1.call-update) | async-done | bytes 2097168 | tf_op jit(solution)/shard_map/psum | solution.py:68
  190.2 0.0 copy-start.12
  190.2 3.0 fusion.2
  193.2 14.7 %collective-permute-start = (bf16[1024,512]{1,0:T(8,128)(2,1)}, bf16[1024,512]{1,0:T(8,128)(2,1)}, u32[]{:S(2)}, u32[]{:S(2)}) collective-permute-start(bf16[1024,512]{1,0:T(8,128)(2,1)} %fusion.2), channel_id=1, source_target_pairs={{496,0},{0,16},{16,32},{32,48},{48,64},{64,80},{80,96},{96,112},{1... | collective-permute-start | bytes 3145736 | tf_op jit(solution)/shard_map/ppermute | solution.py:12
  207.9 0.0 copy-done.8
  207.9 0.0 copy-done.12
  207.9 2.6 fusion.16
  210.6 0.1 broadcast.30.clone
  210.7 0.0 copy-start.5
  210.7 6.1 %scatter_fusion = f32[4,128,512]{2,1,0:T(8,128)S(1)} fusion(f32[4,128,512]{2,1,0:T(8,128)S(1)} %broadcast.30.clone, s32[16]{0:T(128)S(1)} %get-tuple-element.6, f32[16,128,512]{2,1,0:T(8,128)} %fusion.16), kind=kCustom, calls=%fused_computation.4 | custom fusion | flops 1048576 | bytes 12582976 | tf_op jit(solution)/shard_map/scatter-add | solution.py:17
  216.8 0.0 copy-done.5
  216.9 0.0 copy-start.6
  216.9 1.0 fusion.8
  217.9 258.0 %all-reduce.5.cloned.1.call-done = f32[512,512]{1,0:T(8,128)} async-done(((f32[512,512]{1,0:T(8,128)}), f32[512,512]{1,0:T(8,128)}) %all-reduce.5.cloned.1.call-update) | async-done | bytes 1048592 | tf_op jit(solution)/shard_map/psum | solution.py:72
  475.9 0.0 copy-done.6
  475.9 2.2 fusion.11
  478.1 0.0 collective-permute-done
  478.1 2.3 copy.23
  (4 shorter events, 0.0 us)
Async XLA Ops:
  7.2 183.0 %all-reduce.3.cloned.1.call-start = ((), (), s32[]{:S(2)}) async-start(), calls=%async_computation | async-start | bytes 4194304 | tf_op jit(solution)/shard_map/psum | solution.py:68
  8.6 3.2 copy-start.2
  12.5 3.2 copy-start.7
  12.5 3.2 copy-start.9
  15.7 2.7 copy-start.11
  15.7 2.7 copy-start.13
  19.2 3.4 copy-start.3
  22.6 2.5 copy-start.4
  25.2 2.7 copy-start.10
  40.5 1.4 copy-start
  41.9 434.1 %all-reduce.5.cloned.1.call-start = ((), (), s32[]{:S(2)}) async-start(), calls=%async_computation.1 | async-start | bytes 2097152 | tf_op jit(solution)/shard_map/psum | solution.py:72
  52.6 1.0 copy-start.1
  53.6 154.3 %copy-start.8 = (bf16[16,128,512]{2,1,0:T(8,128)(2,1)S(1)}, bf16[16,128,512]{2,1,0:T(8,128)(2,1)}, u32[]{:S(2)}) copy-start(bf16[16,128,512]{2,1,0:T(8,128)(2,1)} %copy-done.7) | copy-start | bytes 6291460
  190.2 17.7 %copy-start.12 = (bf16[16,128,128]{2,1,0:T(8,128)(2,1)S(1)}, bf16[16,128,128]{2,1,0:T(8,128)(2,1)}, u32[]{:S(2)}) copy-start(bf16[16,128,128]{2,1,0:T(8,128)(2,1)} %copy-done.11) | copy-start | bytes 1572868
  193.2 284.9 %collective-permute-start = (bf16[1024,512]{1,0:T(8,128)(2,1)}, bf16[1024,512]{1,0:T(8,128)(2,1)}, u32[]{:S(2)}, u32[]{:S(2)}) collective-permute-start(bf16[1024,512]{1,0:T(8,128)(2,1)} %fusion.2), channel_id=1, source_target_pairs={{496,0},{0,16},{16,32},{32,48},{48,64},{64,80},{80,96},{96,112},{1... | collective-permute-start | bytes 3145736 | tf_op jit(solution)/shard_map/ppermute | solution.py:12
  210.7 6.2 %copy-start.5 = (bf16[512,512]{1,0:T(8,128)(2,1)S(1)}, bf16[512,512]{1,0:T(8,128)(2,1)}, u32[]{:S(2)}) copy-start(bf16[512,512]{1,0:T(8,128)(2,1)} %param.8) | copy-start | bytes 1572868
  216.9 259.0 %copy-start.6 = (bf16[512,512]{1,0:T(8,128)(2,1)S(1)}, bf16[512,512]{1,0:T(8,128)(2,1)}, u32[]{:S(2)}) copy-start(bf16[512,512]{1,0:T(8,128)(2,1)} %param.10) | copy-start | bytes 1572868
Sparse Core Ops, SparseCore 0:
  42.0 148.1 all-reduce.2
  193.1 282.7 all-reduce.4
where the time goes:
time: 488 us; the launch traced here: 487 us
  waiting for transfers between devices  395 us (81%)
  other arithmetic  31.6 us (6%)
  matrix products  18.2 us (4%)
  between operations  15 us (3%)
  starting transfers between devices  14.8 us (3%)
  local copies, waits for them, and re-layouts  13.1 us (3%)
    psum x1, waiting for transfers between devices, on_device(): tag_total = lax.psum(tag_grad, 'rot')  258 us
    psum x1, waiting for transfers between devices, on_device(): total = lax.psum(item_grad, 'tag')  137 us
    scatter-add x3, other arithmetic, spread_tiles(): return empty.at[index].add(tiles)  18.4 us
    ppermute x1, starting transfers between devices, shifted(): return lax.ppermute(block, axis, route)  14.7 us
  transfers between devices with their start and end apart: 3, of which 2 were waited for; matrix products, arithmetic and copies ran while one was open for 5% of the time, Pallas kernels for 0%

commit v1 on v0

v1 whole, which is shorter than its diff:
```python
import jax
import jax.numpy as jnp
from jax import lax
from jax.experimental import pallas as pl
from jax.experimental.pallas import tpu as pltpu
from jax.sharding import PartitionSpec as P

TILE = 128
F32 = jnp.float32
BF16 = jnp.bfloat16


def tile(index):
    return pl.ds(pl.multiple_of(index * TILE, TILE), TILE)


def dot_rows(left, right):
    return lax.dot_general(left, right, (((1,), (1,)), ((), ())), preferred_element_type=F32)


def grads_kernel(
    rt_ref, rc_ref, xt_ref, u_ref, v_ref, w_ref, r_ref, x_ref,
    item_ref, tag_ref, err_ref, err_t, tag_err, tag_err_t,
):
    err_ref[...] = jnp.zeros_like(err_ref)
    err_t[...] = jnp.zeros_like(err_t)
    tag_err[...] = jnp.zeros_like(tag_err)
    tag_err_t[...] = jnp.zeros_like(tag_err_t)
    count = rc_ref[0]
    for s in range(r_ref.shape[0]):
        a, c = tile(rt_ref[0, s]), tile(rt_ref[1, s])
        e = dot_rows(u_ref[a, :], v_ref[c, :]) - r_ref[s].astype(F32)
        e = jnp.where(s < count, e, 0.0)
        err_ref[a, c] = e.astype(BF16)
        err_t[c, a] = e.T.astype(BF16)
    for s in range(x_ref.shape[0]):
        a, c = tile(xt_ref[0, s]), tile(xt_ref[1, s])
        e = dot_rows(v_ref[a, :], w_ref[c, :]) - x_ref[s].astype(F32)
        tag_err[a, c] = e.astype(BF16)
        tag_err_t[c, a] = e.T.astype(BF16)
    step = 256
    for i in range(0, item_ref.shape[0], step):
        rows = pl.ds(i, step)
        part = jnp.dot(err_t[rows, :], u_ref[...], preferred_element_type=F32)
        part += jnp.dot(tag_err[rows, :], w_ref[...], preferred_element_type=F32)
        item_ref[rows, :] = part.astype(BF16)
    for i in range(0, tag_ref.shape[0], step):
        rows = pl.ds(i, step)
        part = jnp.dot(tag_err_t[rows, :], v_ref[...], preferred_element_type=F32)
        tag_ref[rows, :] = part.astype(BF16)


def users_kernel(err_ref, u_ref, v_ref, out_ref):
    step = 256
    for i in range(0, out_ref.shape[0], step):
        rows = pl.ds(i, step)
        grad = jnp.dot(err_ref[rows, :], v_ref[...], preferred_element_type=F32)
        old = u_ref[rows, :].astype(F32)
        out_ref[rows, :] = (old - 0.04 * (grad + 0.05 * old)).astype(BF16)


def whole():
    return pl.BlockSpec(memory_space=pltpu.VMEM)


def scalars():
    return pl.BlockSpec(memory_space=pltpu.SMEM)


def partials(rt, rc, xt, u, v, w, r, x):
    users, rank = u.shape
    items, tags = v.shape[0], w.shape[0]
    return pl.pallas_call(
        grads_kernel,
        out_shape=(
            jax.ShapeDtypeStruct((items, rank), BF16),
            jax.ShapeDtypeStruct((tags, rank), BF16),
            jax.ShapeDtypeStruct((users, items), BF16),
        ),
        in_specs=[scalars()] * 3 + [whole()] * 5,
        out_specs=(whole(),) * 3,
        scratch_shapes=[
            pltpu.VMEM((items, users), BF16),
            pltpu.VMEM((items, tags), BF16),
            pltpu.VMEM((tags, items), BF16),
        ],
        compiler_params=pltpu.CompilerParams(vmem_limit_bytes=24 << 20),
        cost_estimate=pl.CostEstimate(flops=3 << 30, bytes_accessed=6 << 20, transcendentals=0),
    )(rt, rc, xt, u, v, w, r, x)


def updated_users(err, u, v):
    return pl.pallas_call(
        users_kernel,
        out_shape=jax.ShapeDtypeStruct(u.shape, BF16),
        in_specs=[whole()] * 3,
        out_specs=whole(),
        compiler_params=pltpu.CompilerParams(vmem_limit_bytes=16 << 20),
        cost_estimate=pl.CostEstimate(flops=1 << 30, bytes_accessed=4 << 20, transcendentals=0),
    )(err, u, v)


def exchanged(pieces, axis):
    return lax.all_to_all(pieces, axis, 0, 0)


def stepped(old, pieces):
    total = jnp.sum(pieces.astype(F32), axis=0)
    old = old.astype(F32)
    return (old - 0.04 * (total + 0.05 * old)).astype(BF16)


def shard_of(block, axis):
    n = lax.axis_size(axis)
    size = block.shape[0] // n
    return lax.dynamic_slice_in_dim(block, lax.axis_index(axis) * size, size, 0)


def gathered(shard, axis):
    n = lax.axis_size(axis)
    copies = jnp.broadcast_to(shard, (n,) + shard.shape)
    return exchanged(copies, axis).reshape(n * shard.shape[0], shard.shape[1])


def on_device(u, v, w, rating_tiles, rating_counts, ratings, tag_tiles, tag_values):
    rank = u.shape[1]
    n_rot, n_tag = lax.axis_size("rot"), lax.axis_size("tag")
    item_part, tag_part, err = partials(
        rating_tiles.T, rating_counts, tag_tiles.T, u, v, w, ratings, tag_values
    )
    item_pieces = exchanged(item_part.reshape(n_tag, -1, rank), "tag")
    tag_pieces = exchanged(tag_part.reshape(n_rot, -1, rank), "rot")
    new_users = updated_users(err, u, v)
    item_shard = stepped(shard_of(v, "tag"), item_pieces)
    item_shard = lax.ppermute(item_shard, "rot", [(i, (i + 1) % n_rot) for i in range(n_rot)])
    tag_shard = stepped(shard_of(w, "rot"), tag_pieces)
    rotated_items = gathered(item_shard, "tag")
    new_tags = gathered(tag_shard, "rot")
    return (new_users, rotated_items, new_tags)


def solution(mesh):
    placed = (
        P(("rot", "tag"), None),
        P("rot", None),
        P("tag", None),
        P(("rot", "tag"), None),
        P(("rot", "tag")),
        P(("rot", "tag"), None, None),
        P(("rot", "tag"), None),
        P(("rot", "tag"), None, None),
    )
    return jax.shard_map(
        on_device,
        mesh=mesh,
        in_specs=placed,
        out_specs=(P(("rot", "tag"), None), P("rot", None), P("tag", None)),
        check_vma=False,
    )
```

time: 488 us -> 143 us (0.29)
  the two profiles are of different devices: /device:TPU:1 before, /device:TPU:4 now
where the time goes in v1:
time: 143 us; the launch traced here: 142 us
  waiting for transfers between devices  69.4 us (49%)
  blocking collectives  27.7 us (19%)
  starting transfers between devices  23.5 us (16%)
  local copies, waits for them, and re-layouts  12.8 us (9%)
  Pallas kernels  6.2 us (4%)
    all_to_all x3, waiting for transfers between devices, exchanged(): return lax.all_to_all(pieces, axis, 0, 0)  64 us
    all_to_all x1, blocking collectives, exchanged(): return lax.all_to_all(pieces, axis, 0, 0)  27.7 us
    all_to_all x3, starting transfers between devices, exchanged(): return lax.all_to_all(pieces, axis, 0, 0)  21.5 us
    unnamed x20, local copies, waits for them, and re-layouts  10.9 us
    ppermute x1, waiting for transfers between devices, on_device(): lax.ppermute(item_shard, 'rot', [(i, (i + 1) % n_rot) for i in range(n_ro...  5.36 us
    pallas_call x1, Pallas kernels, partials(): pl.pallas_call(grads_kernel, out_shape=(jax.ShapeDtypeStruct((items, rank...  4.63 us
  transfers between devices with their start and end apart: 4, of which 4 were waited for; matrix products, arithmetic and copies ran while one was open for 1% of the time, Pallas kernels for 1%

profile of v1, /device:TPU:4, one launch (start us, length us, event | category | flops | bytes accessed | tf_op | source)
XLA Modules:
  0.0 142.0 jit_solution(6948333833468522320)
XLA Ops:
  1.3 0.0 copy-start
  1.3 1.2 copy-done
  2.5 0.0 copy-start.2
  2.5 1.0 copy-done.2
  3.5 0.0 copy-start.3
  3.5 1.0 copy-done.3
  4.6 0.0 copy-start.4
  4.6 1.0 copy-done.4
  5.6 0.0 copy-start.5
  5.6 1.0 copy-done.5
  6.7 0.0 copy-start.7
  6.7 0.7 copy-done.7
  7.4 0.0 copy-start.8
  7.4 0.7 copy-done.8
  8.0 4.6 %shard_map.103 = (bf16[1024,512]{1,0:T(8,128)(2,1)}, bf16[512,512]{1,0:T(8,128)(2,1)S(1)}, bf16[512,1024]{1,0:T(8,128)(2,1)S(1)}) custom-call(s32[2,16]{1,0:T(2,128)S(1)} %bitcast.7, s32[1]{0:T(128)S(6)} %copy.13.rc_ref, s32[2,16]{1,0:T(2,128)S(1)} %bitcast.8, bf16[512,512]{1,0:T(8,128)(2,1)S(1)} %copy-done.5, bf16[1024,512]{1,0:T(8,128)(2,1)S(1)} %copy-done, ...), custom_call_target="tpu_custom_call" | custom-call | flops 3221225472 | bytes 6291456 | tf_op jit(solution)/shard_map/pallas_call | solution.py:73
  12.7 27.7 %all_to_all.20 = bf16[32,16,512]{2,1,0:T(8,128)(2,1)S(1)} all-to-all(bf16[32,16,512]{2,1,0:T(8,128)(2,1)S(1)} %bitcast.6), channel_id=1, replica_groups=mesh['rot'=32,'tag'=16] {'rot'}, dimensions={0} | all-to-all | bytes 1048576 | tf_op jit(solution)/shard_map/all_to_all | solution.py:104
  40.4 11.0 %all-to-all-start = ((bf16[16,64,512]{2,1,0:T(8,128)(2,1)}), bf16[16,64,512]{2,1,0:T(8,128)(2,1)S(1)}, u32[]{:S(2)}, u32[]{:S(2)}) async-start(bf16[16,64,512]{2,1,0:T(8,128)(2,1)} %bitcast.2), calls=%async_computation | async-start | bytes 2097152 | tf_op jit(solution)/shard_map/all_to_all | solution.py:104
  51.4 0.1 convert_reduce_fusion.1
  51.5 0.7 fusion.5
  52.3 26.9 %all-to-all-done = bf16[16,64,512]{2,1,0:T(8,128)(2,1)S(1)} async-done(((bf16[16,64,512]{2,1,0:T(8,128)(2,1)}), bf16[16,64,512]{2,1,0:T(8,128)(2,1)S(1)}, u32[]{:S(2)}, u32[]{:S(2)}) %all-to-all-start) | async-done | bytes 1048608 | tf_op jit(solution)/shard_map/all_to_all | solution.py:104
  79.2 0.9 broadcast_in_dim.7
  80.1 0.0 copy-start.1
  80.1 6.0 %all-to-all-start.3 = ((bf16[32,16,512]{2,1,0:T(8,128)(2,1)}), bf16[32,16,512]{2,1,0:T(8,128)(2,1)}, u32[]{:S(2)}, u32[]{:S(2)}) async-start(bf16[32,16,512]{2,1,0:T(8,128)(2,1)} %broadcast_in_dim.7), calls=%async_computation.3 | async-start | bytes 1048576 | tf_op jit(solution)/shard_map/all_to_all | solution.py:104
  86.1 0.1 convert_reduce_fusion
  86.2 0.0 copy-done.1
  86.3 2.1 %collective-permute-start = (bf16[64,512]{1,0:T(8,128)(2,1)S(1)}, bf16[64,512]{1,0:T(8,128)(2,1)S(1)}, u32[]{:S(2)}, u32[]{:S(2)}) collective-permute-start(bf16[64,512]{1,0:T(8,128)(2,1)S(1)} %fusion.2), channel_id=1, source_target_pairs={{0,16},{16,32},{32,48},{48,64},{64,80},{80,96},{96,112},{112,128},... | collective-permute-start | bytes 196616 | tf_op jit(solution)/shard_map/ppermute | solution.py:135
  88.3 5.4 %collective-permute-done = bf16[64,512]{1,0:T(8,128)(2,1)S(1)} collective-permute-done((bf16[64,512]{1,0:T(8,128)(2,1)S(1)}, bf16[64,512]{1,0:T(8,128)(2,1)S(1)}, u32[]{:S(2)}, u32[]{:S(2)}) %collective-permute-start) | collective-permute-done | bytes 65568 | tf_op jit(solution)/shard_map/ppermute | solution.py:135
  93.7 10.3 %all-to-all-done.3 = bf16[32,16,512]{2,1,0:T(8,128)(2,1)} async-done(((bf16[32,16,512]{2,1,0:T(8,128)(2,1)}), bf16[32,16,512]{2,1,0:T(8,128)(2,1)}, u32[]{:S(2)}, u32[]{:S(2)}) %all-to-all-start.3) | async-done | bytes 524320 | tf_op jit(solution)/shard_map/all_to_all | solution.py:104
  104.0 1.1 broadcast_in_dim.6
  105.1 0.0 copy-start.6
  105.1 4.5 %all-to-all-start.1 = ((bf16[16,64,512]{2,1,0:T(8,128)(2,1)}), bf16[16,64,512]{2,1,0:T(8,128)(2,1)}, u32[]{:S(2)}, u32[]{:S(2)}) async-start(bf16[16,64,512]{2,1,0:T(8,128)(2,1)} %broadcast_in_dim.6), calls=%async_computation.1 | async-start | bytes 2097152 | tf_op jit(solution)/shard_map/all_to_all | solution.py:104
  109.5 0.0 copy-done.6
  109.6 1.6 %shard_map.104 = bf16[512,512]{1,0:T(8,128)(2,1)} custom-call(bf16[512,1024]{1,0:T(8,128)(2,1)S(1)} %get-tuple-element.6.err_ref, bf16[512,512]{1,0:T(8,128)(2,1)S(1)} %copy-done.6, bf16[1024,512]{1,0:T(8,128)(2,1)S(1)} %copy-done.1), custom_call_target="tpu_custom_call" | custom-call | flops 1073741824 | bytes 4194304 | tf_op jit(solution)/shard_map/pallas_call | solution.py:93
  111.1 26.8 %all-to-all-done.1 = bf16[16,64,512]{2,1,0:T(8,128)(2,1)} async-done(((bf16[16,64,512]{2,1,0:T(8,128)(2,1)}), bf16[16,64,512]{2,1,0:T(8,128)(2,1)}, u32[]{:S(2)}, u32[]{:S(2)}) %all-to-all-start.1) | async-done | bytes 1048608 | tf_op jit(solution)/shard_map/all_to_all | solution.py:104
  137.9 2.3 %copy.14 = bf16[1024,512]{1,0:T(8,128)(2,1)} copy(bf16[1024,512]{1,0:T(8,128)(2,1)} %bitcast.3) | data formatting | bytes 2097152
  140.1 1.9 %copy.15 = bf16[512,512]{1,0:T(8,128)(2,1)} copy(bf16[512,512]{1,0:T(8,128)(2,1)} %bitcast.5) | data formatting | bytes 1048576
  (1 shorter events, 0.0 us)
Async XLA Ops:
  1.3 1.2 copy-start
  2.5 1.0 copy-start.2
  3.5 1.0 copy-start.3
  4.6 1.0 copy-start.4
  5.6 1.0 copy-start.5
  6.7 0.7 copy-start.7
  7.4 0.7 copy-start.8
  40.4 38.8 %all-to-all-start = ((bf16[16,64,512]{2,1,0:T(8,128)(2,1)}), bf16[16,64,512]{2,1,0:T(8,128)(2,1)S(1)}, u32[]{:S(2)}, u32[]{:S(2)}) async-start(bf16[16,64,512]{2,1,0:T(8,128)(2,1)} %bitcast.2), calls=%async_computation | async-start | bytes 2097152 | tf_op jit(solution)/shard_map/all_to_all | solution.py:104
  80.1 6.1 %copy-start.1 = (bf16[1024,512]{1,0:T(8,128)(2,1)S(1)}, bf16[1024,512]{1,0:T(8,128)(2,1)}, u32[]{:S(2)}) copy-start(bf16[1024,512]{1,0:T(8,128)(2,1)} %v_ref.3) | copy-start | bytes 3145732
  80.1 23.9 %all-to-all-start.3 = ((bf16[32,16,512]{2,1,0:T(8,128)(2,1)}), bf16[32,16,512]{2,1,0:T(8,128)(2,1)}, u32[]{:S(2)}, u32[]{:S(2)}) async-start(bf16[32,16,512]{2,1,0:T(8,128)(2,1)} %broadcast_in_dim.7), calls=%async_computation.3 | async-start | bytes 1048576 | tf_op jit(solution)/shard_map/all_to_all | solution.py:104
  86.3 7.4 %collective-permute-start = (bf16[64,512]{1,0:T(8,128)(2,1)S(1)}, bf16[64,512]{1,0:T(8,128)(2,1)S(1)}, u32[]{:S(2)}, u32[]{:S(2)}) collective-permute-start(bf16[64,512]{1,0:T(8,128)(2,1)S(1)} %fusion.2), channel_id=1, source_target_pairs={{0,16},{16,32},{32,48},{48,64},{64,80},{80,96},{96,112},{112,128},... | collective-permute-start | bytes 196616 | tf_op jit(solution)/shard_map/ppermute | solution.py:135
  105.1 4.5 %copy-start.6 = (bf16[512,512]{1,0:T(8,128)(2,1)S(1)}, bf16[512,512]{1,0:T(8,128)(2,1)}, u32[]{:S(2)}) copy-start(bf16[512,512]{1,0:T(8,128)(2,1)} %u_ref.3) | copy-start | bytes 1572868
  105.1 32.8 %all-to-all-start.1 = ((bf16[16,64,512]{2,1,0:T(8,128)(2,1)}), bf16[16,64,512]{2,1,0:T(8,128)(2,1)}, u32[]{:S(2)}, u32[]{:S(2)}) async-start(bf16[16,64,512]{2,1,0:T(8,128)(2,1)} %broadcast_in_dim.6), calls=%async_computation.1 | async-start | bytes 2097152 | tf_op jit(solution)/shard_map/all_to_all | solution.py:104

commit v2 on v1

v2 whole, which is shorter than its diff:
```python
import jax
import jax.numpy as jnp
from jax import lax
from jax.experimental import pallas as pl
from jax.experimental.pallas import tpu as pltpu
from jax.sharding import PartitionSpec as P

TILE = 128
F32 = jnp.float32
BF16 = jnp.bfloat16


def tile(index):
    return pl.ds(pl.multiple_of(index * TILE, TILE), TILE)


def dot_rows(left, right):
    return lax.dot_general(left, right, (((1,), (1,)), ((), ())), preferred_element_type=F32)


def grads_kernel(
    rt_ref, rc_ref, xt_ref, core_ref, u_hbm, v_hbm, w_hbm, r_hbm, x_hbm,
    item_ref, send_ref, own_ref, err_ref,
    u_ref, v_ref, w_ref, r_ref, x_ref, err_t, tag_err, tag_err_t, sems,
):
    copies = [
        pltpu.make_async_copy(src, dst, sems.at[i])
        for i, (src, dst) in enumerate(
            [(v_hbm, v_ref), (w_hbm, w_ref), (x_hbm, x_ref), (u_hbm, u_ref), (r_hbm, r_ref)]
        )
    ]
    for copy in copies:
        copy.start()
    err_ref[...] = jnp.zeros_like(err_ref)
    err_t[...] = jnp.zeros_like(err_t)
    tag_err[...] = jnp.zeros_like(tag_err)
    tag_err_t[...] = jnp.zeros_like(tag_err_t)
    for copy in copies[:3]:
        copy.wait()
    for s in range(x_ref.shape[0]):
        a, c = tile(xt_ref[0, s]), tile(xt_ref[1, s])
        e = dot_rows(v_ref[a, :], w_ref[c, :]) - x_ref[s].astype(F32)
        tag_err[a, c] = e.astype(BF16)
        tag_err_t[c, a] = e.T.astype(BF16)
    for copy in copies[3:]:
        copy.wait()
    count = rc_ref[0]
    for s in range(r_ref.shape[0]):
        a, c = tile(rt_ref[0, s]), tile(rt_ref[1, s])
        e = dot_rows(u_ref[a, :], v_ref[c, :]) - r_ref[s].astype(F32)
        e = jnp.where(s < count, e, 0.0)
        err_ref[a, c] = e.astype(BF16)
        err_t[c, a] = e.T.astype(BF16)
    step = 256
    for i in range(0, item_ref.shape[0], step):
        rows = pl.ds(i, step)
        part = jnp.dot(err_t[rows, :], u_ref[...], preferred_element_type=F32)
        part += jnp.dot(tag_err[rows, :], w_ref[...], preferred_element_type=F32)
        item_ref[rows, :] = part.astype(BF16)
    half = own_ref.shape[0]
    core = core_ref[0]
    mine, other = (pl.ds(pl.multiple_of(h * half, half), half) for h in (core, 1 - core))
    own_ref[...] = jnp.dot(tag_err_t[mine, :], v_ref[...], preferred_element_type=F32)
    part = jnp.dot(tag_err_t[other, :], v_ref[...], preferred_element_type=F32)
    send_ref[...] = part.astype(BF16)


def users_kernel(err_ref, u_ref, v_ref, out_ref):
    step = 256
    for i in range(0, out_ref.shape[0], step):
        rows = pl.ds(i, step)
        grad = jnp.dot(err_ref[rows, :], v_ref[...], preferred_element_type=F32)
        old = u_ref[rows, :].astype(F32)
        out_ref[rows, :] = (old - 0.04 * (grad + 0.05 * old)).astype(BF16)


def whole():
    return pl.BlockSpec(memory_space=pltpu.VMEM)


def scalars():
    return pl.BlockSpec(memory_space=pltpu.SMEM)


def in_hbm():
    return pl.BlockSpec(memory_space=pltpu.HBM)


def partials(rt, rc, xt, core, u, v, w, r, x):
    users, rank = u.shape
    items, tags = v.shape[0], w.shape[0]
    return pl.pallas_call(
        grads_kernel,
        out_shape=(
            jax.ShapeDtypeStruct((items, rank), BF16),
            jax.ShapeDtypeStruct((tags // 2, rank), BF16),
            jax.ShapeDtypeStruct((tags // 2, rank), F32),
            jax.ShapeDtypeStruct((users, items), BF16),
        ),
        in_specs=[scalars()] * 4 + [in_hbm()] * 5,
        out_specs=(whole(),) * 4,
        scratch_shapes=[pltpu.VMEM(a.shape, BF16) for a in (u, v, w, r, x)]
        + [
            pltpu.VMEM((items, users), BF16),
            pltpu.VMEM((items, tags), BF16),
            pltpu.VMEM((tags, items), BF16),
            pltpu.SemaphoreType.DMA((5,)),
        ],
        compiler_params=pltpu.CompilerParams(vmem_limit_bytes=24 << 20),
        cost_estimate=pl.CostEstimate(flops=3 << 30, bytes_accessed=6 << 20, transcendentals=0),
    )(rt, rc, xt, core, *(pltpu.with_memory_space_constraint(a, pltpu.HBM) for a in (u, v, w, r, x)))


def updated_users(err, u, v):
    return pl.pallas_call(
        users_kernel,
        out_shape=jax.ShapeDtypeStruct(u.shape, BF16),
        in_specs=[whole()] * 3,
        out_specs=whole(),
        compiler_params=pltpu.CompilerParams(vmem_limit_bytes=16 << 20),
        cost_estimate=pl.CostEstimate(flops=1 << 30, bytes_accessed=4 << 20, transcendentals=0),
    )(err, u, v)


def exchanged(pieces, axis):
    return lax.all_to_all(pieces, axis, 0, 0)


def updated(old, total):
    old = old.astype(F32)
    return (old - 0.04 * (total + 0.05 * old)).astype(BF16)


def part_of(block, index, size):
    return lax.dynamic_slice_in_dim(block, index * size, size, 0)


def swapped(block, mask):
    n = lax.axis_size("rot")
    return lax.ppermute(block, "rot", [(i, i ^ mask) for i in range(n)])


def joined(mine, other, bit):
    return jnp.where(
        bit == 0, jnp.concatenate([mine, other], 0), jnp.concatenate([other, mine], 0)
    )


def added(own, mask):
    own = lax.reduce_precision(own, 8, 7)
    return own + swapped(own.astype(BF16), mask).astype(F32)


def tag_sum_in_plane(send, own, x_hi):
    own = own + swapped(send, 1).astype(F32)
    size = own.shape[0] // 2
    send = part_of(own, 1 - x_hi, size).astype(BF16)
    own = part_of(own, x_hi, size) + swapped(send, 2).astype(F32)
    return added(own, 4)


def new_tag_rows(total, w, core, x_hi):
    shard = updated(part_of(w, core * 2 + x_hi, total.shape[0]), total)
    half = joined(shard, swapped(shard, 2), x_hi)
    return joined(half, swapped(half, 1), core)


def on_device(u, v, w, rating_tiles, rating_counts, ratings, tag_tiles, tag_values):
    rank = u.shape[1]
    n_rot, n_tag = lax.axis_size("rot"), lax.axis_size("tag")
    rot = lax.axis_index("rot")
    core, x_hi = rot & 1, (rot >> 1) & 1
    item_part, tag_send, tag_own, err = partials(
        rating_tiles.T, rating_counts, tag_tiles.T, core[None], u, v, w, ratings, tag_values
    )
    item_pieces = exchanged(item_part.reshape(n_tag, -1, rank), "tag")
    new_users = updated_users(err, u, v)
    tag_total = tag_sum_in_plane(tag_send, tag_own, x_hi)
    item_pieces, tag_total, new_users = lax.optimization_barrier(
        (item_pieces, tag_total, new_users)
    )
    shard = part_of(v, lax.axis_index("tag"), v.shape[0] // n_tag)
    shard = updated(shard, jnp.sum(item_pieces.astype(F32), axis=0))
    shard = lax.ppermute(shard, "rot", [(i, (i + 1) % n_rot) for i in range(n_rot)])
    tag_total = added(tag_total, 8)
    shard, tag_total = lax.optimization_barrier((shard, tag_total))
    copies = jnp.broadcast_to(shard, (n_tag,) + shard.shape)
    rotated_items = exchanged(copies, "tag").reshape(v.shape)
    new_tags = new_tag_rows(added(tag_total, 16), w, core, x_hi)
    return (new_users, rotated_items, new_tags)


def solution(mesh):
    placed = (
        P(("rot", "tag"), None),
        P("rot", None),
        P("tag", None),
        P(("rot", "tag"), None),
        P(("rot", "tag")),
        P(("rot", "tag"), None, None),
        P(("rot", "tag"), None),
        P(("rot", "tag"), None, None),
    )
    return jax.shard_map(
        on_device,
        mesh=mesh,
        in_specs=placed,
        out_specs=(P(("rot", "tag"), None), P("rot", None), P("tag", None)),
        check_vma=False,
    )
```

time: 143 us -> 101 us (0.71)
  the two profiles are of different devices: /device:TPU:4 before, /device:TPU:1 now
where the time goes in v2:
time: 101 us
  starting transfers between devices  60.3 us (60%)
  waiting for transfers between devices  22.4 us (22%)
  Pallas kernels  7.62 us (8%)
  other arithmetic  4.62 us (5%)
  local copies, waits for them, and re-layouts  4.21 us (4%)
  between operations  1.51 us (1%)
    ppermute x7, starting transfers between devices, swapped(): return lax.ppermute(block, 'rot', [(i, i ^ mask) for i in range(n)])  35.2 us
    ppermute x7, waiting for transfers between devices, swapped(): return lax.ppermute(block, 'rot', [(i, i ^ mask) for i in range(n)])  16.7 us
    all_to_all x2, starting transfers between devices, exchanged(): return lax.all_to_all(pieces, axis, 0, 0)  16.2 us
    ppermute x1, starting transfers between devices, on_device(): lax.ppermute(shard, 'rot', [(i, (i + 1) % n_rot) for i in range(n_rot)])  8.86 us
    pallas_call x1, Pallas kernels, partials(): pl.pallas_call(grads_kernel, out_shape=(jax.ShapeDtypeStruct((items, rank...  6.05 us
    all_to_all x2, waiting for transfers between devices, exchanged(): return lax.all_to_all(pieces, axis, 0, 0)  4.5 us
    unnamed x13, local copies, waits for them, and re-layouts  3.12 us
  transfers between devices with their start and end apart: 10, of which 8 were waited for; matrix products, arithmetic and copies ran while one was open for 5% of the time, Pallas kernels for 2%

profile of v2, /device:TPU:1, one launch (start us, length us, event | category | flops | bytes accessed | tf_op | source)
XLA Modules:
  0.0 100.7 jit_solution(15518408198087211681)
XLA Ops:
  1.3 0.0 copy-start.2
  1.3 0.7 copy-done.2
  2.0 0.0 copy-start.3
  2.0 0.7 copy-done.3
  2.6 6.0 %shard_map.103 = (bf16[1024,512]{1,0:T(8,128)(2,1)}, bf16[256,512]{1,0:T(8,128)(2,1)S(1)}, f32[256,512]{1,0:T(8,128)S(1)}, bf16[512,1024]{1,0:T(8,128)(2,1)S(1)}) custom-call(s32[2,16]{1,0:T(2,128)S(1)} %bitcast.5, s32[1]{0:T(128)S(6)} %copy.12.rc_ref, s32[2,16]{1,0:T(2,128)S(1)} %bitcast.6, s32[1]{0:T(128)} %bitcast.2.core_ref, bf16[512,512]{1,0:T(8,128)(2,1)} %u_ref.1, ...), custom_call_target="tpu_custom_call" | custom-call | flops 3221225472 | bytes 6291456 | tf_op jit(solution)/shard_map/pallas_call | solution.py:92
  8.7 12.0 %all-to-all-start = ((bf16[16,64,512]{2,1,0:T(8,128)(2,1)}), bf16[16,64,512]{2,1,0:T(8,128)(2,1)}, u32[]{:S(2)}, u32[]{:S(2)}) async-start(bf16[16,64,512]{2,1,0:T(8,128)(2,1)} %bitcast.3), calls=%async_computation | async-start | bytes 2097152 | tf_op jit(solution)/shard_map/all_to_all | solution.py:126
  20.7 2.9 %collective-permute-start = (bf16[256,512]{1,0:T(8,128)(2,1)S(1)}, bf16[256,512]{1,0:T(8,128)(2,1)S(1)}, u32[]{:S(2)}, u32[]{:S(2)}) collective-permute-start(bf16[256,512]{1,0:T(8,128)(2,1)S(1)} %get-tuple-element.14), channel_id=1, source_target_pairs={{0,16},{16,0},{32,48},{48,32},{64,80},{80,64},{96,112},{112,96},{1... | collective-permute-start | bytes 786440 | tf_op jit(solution)/shard_map/ppermute | solution.py:140
  23.5 1.1 %collective-permute-done = bf16[256,512]{1,0:T(8,128)(2,1)S(1)} collective-permute-done((bf16[256,512]{1,0:T(8,128)(2,1)S(1)}, bf16[256,512]{1,0:T(8,128)(2,1)S(1)}, u32[]{:S(2)}, u32[]{:S(2)}) %collective-permute-start) | collective-permute-done | bytes 262176 | tf_op jit(solution)/shard_map/ppermute | solution.py:140
  24.7 0.0 copy-start
  24.7 0.0 copy-start.1
  24.7 0.1 convert_add_fusion
  24.8 0.0 copy-start.4
  24.8 0.8 copy-done.4
  25.6 4.4 %collective-permute-start.1 = (bf16[128,512]{1,0:T(8,128)(2,1)S(1)}, bf16[128,512]{1,0:T(8,128)(2,1)S(1)}, u32[]{:S(2)}, u32[]{:S(2)}) collective-permute-start(bf16[128,512]{1,0:T(8,128)(2,1)S(1)} %dynamic-slice_convert_fusion), channel_id=1, source_target_pairs={{0,32},{16,48},{32,0},{48,16},{64,96},{80,112},{96,64},{112,80},{1... | collective-permute-start | bytes 393224 | tf_op jit(solution)/shard_map/ppermute | solution.py:140
  29.9 4.4 %collective-permute-done.1 = bf16[128,512]{1,0:T(8,128)(2,1)S(1)} collective-permute-done((bf16[128,512]{1,0:T(8,128)(2,1)S(1)}, bf16[128,512]{1,0:T(8,128)(2,1)S(1)}, u32[]{:S(2)}, u32[]{:S(2)}) %collective-permute-start.1) | collective-permute-done | bytes 131104 | tf_op jit(solution)/shard_map/ppermute | solution.py:140
  34.4 1.0 fusion.3
  35.4 3.2 %collective-permute-start.2 = (bf16[128,512]{1,0:T(8,128)(2,1)S(1)}, bf16[128,512]{1,0:T(8,128)(2,1)S(1)}, u32[]{:S(2)}, u32[]{:S(2)}) collective-permute-start(bf16[128,512]{1,0:T(8,128)(2,1)S(1)} %fusion.3), channel_id=1, source_target_pairs={{0,64},{16,80},{32,96},{48,112},{64,0},{80,16},{96,32},{112,48},{1... | collective-permute-start | bytes 393224 | tf_op jit(solution)/shard_map/ppermute | solution.py:140
  38.6 0.0 copy-done
  38.6 0.0 copy-done.1
  38.6 0.0 copy-start.5
  38.6 1.6 %shard_map.104 = bf16[512,512]{1,0:T(8,128)(2,1)} custom-call(bf16[512,1024]{1,0:T(8,128)(2,1)S(1)} %get-tuple-element.15.err_ref, bf16[512,512]{1,0:T(8,128)(2,1)S(1)} %copy-done.1, bf16[1024,512]{1,0:T(8,128)(2,1)S(1)} %copy-done), custom_call_target="tpu_custom_call" | custom-call | flops 1073741824 | bytes 4194304 | tf_op jit(solution)/shard_map/pallas_call | solution.py:115
  40.2 1.3 %collective-permute-done.2 = bf16[128,512]{1,0:T(8,128)(2,1)S(1)} collective-permute-done((bf16[128,512]{1,0:T(8,128)(2,1)S(1)}, bf16[128,512]{1,0:T(8,128)(2,1)S(1)}, u32[]{:S(2)}, u32[]{:S(2)}) %collective-permute-start.2) | collective-permute-done | bytes 131104 | tf_op jit(solution)/shard_map/ppermute | solution.py:140
  41.5 0.0 copy-done.5
  41.5 0.1 convert_add_fusion.2
  41.5 4.5 %all-to-all-done = bf16[16,64,512]{2,1,0:T(8,128)(2,1)} async-done(((bf16[16,64,512]{2,1,0:T(8,128)(2,1)}), bf16[16,64,512]{2,1,0:T(8,128)(2,1)}, u32[]{:S(2)}, u32[]{:S(2)}) %all-to-all-start) | async-done | bytes 1048608 | tf_op jit(solution)/shard_map/all_to_all | solution.py:126
  46.1 4.2 %collective-permute-start.4 = (bf16[128,512]{1,0:T(8,128)(2,1)S(1)}, bf16[128,512]{1,0:T(8,128)(2,1)S(1)}, u32[]{:S(2)}, u32[]{:S(2)}) collective-permute-start(bf16[128,512]{1,0:T(8,128)(2,1)S(1)} %reduce-precision_convert_fusion.1), channel_id=1, source_target_pairs={{0,128},{16,144},{32,160},{48,176},{64,192},{80,208},{96,224},{112... | collective-permute-start | bytes 393224 | tf_op jit(solution)/shard_map/ppermute | solution.py:140
  50.3 1.4 %convert_reduce_fusion = f32[64,512]{1,0:T(8,128)S(1)} fusion(bf16[16,64,512]{2,1,0:T(8,128)(2,1)} %all-to-all-done), kind=kLoop, calls=%fused_computation | loop fusion | flops 1015808 | bytes 1179648 | tf_op jit(solution)/shard_map/reduce_sum | solution.py:183
  51.7 8.9 %collective-permute-start.3 = (bf16[64,512]{1,0:T(8,128)(2,1)S(1)}, bf16[64,512]{1,0:T(8,128)(2,1)S(1)}, u32[]{:S(2)}, u32[]{:S(2)}) collective-permute-start(bf16[64,512]{1,0:T(8,128)(2,1)S(1)} %fusion.6), channel_id=1, source_target_pairs={{0,16},{16,32},{32,48},{48,64},{64,80},{80,96},{96,112},{112,128},... | collective-permute-start | bytes 196616 | tf_op jit(solution)/shard_map/ppermute | solution.py:184
  60.6 0.0 collective-permute-done.4
  60.6 1.3 %collective-permute-done.3 = bf16[64,512]{1,0:T(8,128)(2,1)S(1)} collective-permute-done((bf16[64,512]{1,0:T(8,128)(2,1)S(1)}, bf16[64,512]{1,0:T(8,128)(2,1)S(1)}, u32[]{:S(2)}, u32[]{:S(2)}) %collective-permute-start.3) | collective-permute-done | bytes 65568 | tf_op jit(solution)/shard_map/ppermute | solution.py:184
  61.9 1.1 %broadcast_in_dim.7 = bf16[16,64,512]{2,1,0:T(8,128)(2,1)} broadcast(bf16[64,512]{1,0:T(8,128)(2,1)S(1)} %collective-permute-done.3), dimensions={1,2} | broadcast | bytes 1114112 | tf_op jit(solution)/shard_map/broadcast_in_dim | solution.py:187
  62.9 4.3 %all-to-all-start.1 = ((bf16[16,64,512]{2,1,0:T(8,128)(2,1)}), bf16[16,64,512]{2,1,0:T(8,128)(2,1)S(1)}, u32[]{:S(2)}, u32[]{:S(2)}) async-start(bf16[16,64,512]{2,1,0:T(8,128)(2,1)} %broadcast_in_dim.7), calls=%async_computation.1 | async-start | bytes 2097152 | tf_op jit(solution)/shard_map/all_to_all | solution.py:126
  67.3 5.7 %collective-permute-start.5 = (bf16[128,512]{1,0:T(8,128)(2,1)S(1)}, bf16[128,512]{1,0:T(8,128)(2,1)S(1)}, u32[]{:S(2)}, u32[]{:S(2)}) collective-permute-start(bf16[128,512]{1,0:T(8,128)(2,1)S(1)} %reduce-precision_convert_fusion), channel_id=1, source_target_pairs={{0,256},{16,272},{32,288},{48,304},{64,320},{80,336},{96,352},{112... | collective-permute-start | bytes 393224 | tf_op jit(solution)/shard_map/ppermute | solution.py:140
  72.9 3.9 %collective-permute-done.5 = bf16[128,512]{1,0:T(8,128)(2,1)S(1)} collective-permute-done((bf16[128,512]{1,0:T(8,128)(2,1)S(1)}, bf16[128,512]{1,0:T(8,128)(2,1)S(1)}, u32[]{:S(2)}, u32[]{:S(2)}) %collective-permute-start.5) | collective-permute-done | bytes 131104 | tf_op jit(solution)/shard_map/ppermute | solution.py:140
  76.9 1.0 fusion.2
  77.9 3.1 %collective-permute-start.6 = (bf16[128,512]{1,0:T(8,128)(2,1)S(1)}, bf16[128,512]{1,0:T(8,128)(2,1)S(1)}, u32[]{:S(2)}, u32[]{:S(2)}) collective-permute-start(bf16[128,512]{1,0:T(8,128)(2,1)S(1)} %fusion.2), channel_id=1, source_target_pairs={{0,32},{16,48},{32,0},{48,16},{64,96},{80,112},{96,64},{112,80},{1... | collective-permute-start | bytes 393224 | tf_op jit(solution)/shard_map/ppermute | solution.py:140
  81.0 4.7 %collective-permute-done.6 = bf16[128,512]{1,0:T(8,128)(2,1)S(1)} collective-permute-done((bf16[128,512]{1,0:T(8,128)(2,1)S(1)}, bf16[128,512]{1,0:T(8,128)(2,1)S(1)}, u32[]{:S(2)}, u32[]{:S(2)}) %collective-permute-start.6) | collective-permute-done | bytes 131104 | tf_op jit(solution)/shard_map/ppermute | solution.py:140
  85.7 0.1 maximum_select_fusion.1
  85.8 11.8 %collective-permute-start.7 = (bf16[256,512]{1,0:T(8,128)(2,1)S(1)}, bf16[256,512]{1,0:T(8,128)(2,1)S(1)}, u32[]{:S(2)}, u32[]{:S(2)}) collective-permute-start(bf16[256,512]{1,0:T(8,128)(2,1)S(1)} %maximum_select_fusion.1), channel_id=1, source_target_pairs={{0,16},{16,0},{32,48},{48,32},{64,80},{80,64},{96,112},{112,96},{1... | collective-permute-start | bytes 786440 | tf_op jit(solution)/shard_map/ppermute | solution.py:140
  97.6 1.1 %collective-permute-done.7 = bf16[256,512]{1,0:T(8,128)(2,1)S(1)} collective-permute-done((bf16[256,512]{1,0:T(8,128)(2,1)S(1)}, bf16[256,512]{1,0:T(8,128)(2,1)S(1)}, u32[]{:S(2)}, u32[]{:S(2)}) %collective-permute-start.7) | collective-permute-done | bytes 262176 | tf_op jit(solution)/shard_map/ppermute | solution.py:140
  98.7 1.0 maximum_select_fusion
  99.7 0.0 all-to-all-done.1
  99.7 1.0 copy.13
  (5 shorter events, 0.1 us)
Async XLA Ops:
  1.3 0.7 copy-start.2
  2.0 0.7 copy-start.3
  8.7 37.3 %all-to-all-start = ((bf16[16,64,512]{2,1,0:T(8,128)(2,1)}), bf16[16,64,512]{2,1,0:T(8,128)(2,1)}, u32[]{:S(2)}, u32[]{:S(2)}) async-start(bf16[16,64,512]{2,1,0:T(8,128)(2,1)} %bitcast.3), calls=%async_computation | async-start | bytes 2097152 | tf_op jit(solution)/shard_map/all_to_all | solution.py:126
  20.7 4.0 %collective-permute-start = (bf16[256,512]{1,0:T(8,128)(2,1)S(1)}, bf16[256,512]{1,0:T(8,128)(2,1)S(1)}, u32[]{:S(2)}, u32[]{:S(2)}) collective-permute-start(bf16[256,512]{1,0:T(8,128)(2,1)S(1)} %get-tuple-element.14), channel_id=1, source_target_pairs={{0,16},{16,0},{32,48},{48,32},{64,80},{80,64},{96,112},{112,96},{1... | collective-permute-start | bytes 786440 | tf_op jit(solution)/shard_map/ppermute | solution.py:140
  24.7 13.9 %copy-start = (bf16[1024,512]{1,0:T(8,128)(2,1)S(1)}, bf16[1024,512]{1,0:T(8,128)(2,1)}, u32[]{:S(2)}) copy-start(bf16[1024,512]{1,0:T(8,128)(2,1)} %v_ref.1) | copy-start | bytes 3145732
  24.7 13.9 %copy-start.1 = (bf16[512,512]{1,0:T(8,128)(2,1)S(1)}, bf16[512,512]{1,0:T(8,128)(2,1)}, u32[]{:S(2)}) copy-start(bf16[512,512]{1,0:T(8,128)(2,1)} %u_ref.1) | copy-start | bytes 1572868
  24.8 0.8 copy-start.4
  25.6 8.8 %collective-permute-start.1 = (bf16[128,512]{1,0:T(8,128)(2,1)S(1)}, bf16[128,512]{1,0:T(8,128)(2,1)S(1)}, u32[]{:S(2)}, u32[]{:S(2)}) collective-permute-start(bf16[128,512]{1,0:T(8,128)(2,1)S(1)} %dynamic-slice_convert_fusion), channel_id=1, source_target_pairs={{0,32},{16,48},{32,0},{48,16},{64,96},{80,112},{96,64},{112,80},{1... | collective-permute-start | bytes 393224 | tf_op jit(solution)/shard_map/ppermute | solution.py:140
  35.4 6.1 %collective-permute-start.2 = (bf16[128,512]{1,0:T(8,128)(2,1)S(1)}, bf16[128,512]{1,0:T(8,128)(2,1)S(1)}, u32[]{:S(2)}, u32[]{:S(2)}) collective-permute-start(bf16[128,512]{1,0:T(8,128)(2,1)S(1)} %fusion.3), channel_id=1, source_target_pairs={{0,64},{16,80},{32,96},{48,112},{64,0},{80,16},{96,32},{112,48},{1... | collective-permute-start | bytes 393224 | tf_op jit(solution)/shard_map/ppermute | solution.py:140
  38.6 2.9 %copy-start.5 = (f32[256,512]{1,0:T(8,128)S(1)}, f32[256,512]{1,0:T(8,128)}, u32[]{:S(2)}) copy-start(f32[256,512]{1,0:T(8,128)} %copy-done.4) | copy-start | bytes 1572868
  46.1 14.5 %collective-permute-start.4 = (bf16[128,512]{1,0:T(8,128)(2,1)S(1)}, bf16[128,512]{1,0:T(8,128)(2,1)S(1)}, u32[]{:S(2)}, u32[]{:S(2)}) collective-permute-start(bf16[128,512]{1,0:T(8,128)(2,1)S(1)} %reduce-precision_convert_fusion.1), channel_id=1, source_target_pairs={{0,128},{16,144},{32,160},{48,176},{64,192},{80,208},{96,224},{112... | collective-permute-start | bytes 393224 | tf_op jit(solution)/shard_map/ppermute | solution.py:140
  51.7 10.2 %collective-permute-start.3 = (bf16[64,512]{1,0:T(8,128)(2,1)S(1)}, bf16[64,512]{1,0:T(8,128)(2,1)S(1)}, u32[]{:S(2)}, u32[]{:S(2)}) collective-permute-start(bf16[64,512]{1,0:T(8,128)(2,1)S(1)} %fusion.6), channel_id=1, source_target_pairs={{0,16},{16,32},{32,48},{48,64},{64,80},{80,96},{96,112},{112,128},... | collective-permute-start | bytes 196616 | tf_op jit(solution)/shard_map/ppermute | solution.py:184
  62.9 36.8 %all-to-all-start.1 = ((bf16[16,64,512]{2,1,0:T(8,128)(2,1)}), bf16[16,64,512]{2,1,0:T(8,128)(2,1)S(1)}, u32[]{:S(2)}, u32[]{:S(2)}) async-start(bf16[16,64,512]{2,1,0:T(8,128)(2,1)} %broadcast_in_dim.7), calls=%async_computation.1 | async-start | bytes 2097152 | tf_op jit(solution)/shard_map/all_to_all | solution.py:126
  67.3 9.6 %collective-permute-start.5 = (bf16[128,512]{1,0:T(8,128)(2,1)S(1)}, bf16[128,512]{1,0:T(8,128)(2,1)S(1)}, u32[]{:S(2)}, u32[]{:S(2)}) collective-permute-start(bf16[128,512]{1,0:T(8,128)(2,1)S(1)} %reduce-precision_convert_fusion), channel_id=1, source_target_pairs={{0,256},{16,272},{32,288},{48,304},{64,320},{80,336},{96,352},{112... | collective-permute-start | bytes 393224 | tf_op jit(solution)/shard_map/ppermute | solution.py:140
  77.9 7.9 %collective-permute-start.6 = (bf16[128,512]{1,0:T(8,128)(2,1)S(1)}, bf16[128,512]{1,0:T(8,128)(2,1)S(1)}, u32[]{:S(2)}, u32[]{:S(2)}) collective-permute-start(bf16[128,512]{1,0:T(8,128)(2,1)S(1)} %fusion.2), channel_id=1, source_target_pairs={{0,32},{16,48},{32,0},{48,16},{64,96},{80,112},{96,64},{112,80},{1... | collective-permute-start | bytes 393224 | tf_op jit(solution)/shard_map/ppermute | solution.py:140
  85.8 12.9 %collective-permute-start.7 = (bf16[256,512]{1,0:T(8,128)(2,1)S(1)}, bf16[256,512]{1,0:T(8,128)(2,1)S(1)}, u32[]{:S(2)}, u32[]{:S(2)}) collective-permute-start(bf16[256,512]{1,0:T(8,128)(2,1)S(1)} %maximum_select_fusion.1), channel_id=1, source_target_pairs={{0,16},{16,0},{32,48},{48,32},{64,80},{80,64},{96,112},{112,96},{1... | collective-permute-start | bytes 786440 | tf_op jit(solution)/shard_map/ppermute | solution.py:140

commit v3 on v2

v3 whole, which is shorter than its diff:
```python
import jax
import jax.numpy as jnp
from jax import lax
from jax.experimental import pallas as pl
from jax.experimental.pallas import tpu as pltpu
from jax.sharding import PartitionSpec as P

TILE = 128
F32 = jnp.float32
BF16 = jnp.bfloat16


def tile(index):
    return pl.ds(pl.multiple_of(index * TILE, TILE), TILE)


def dot_rows(left, right):
    return lax.dot_general(left, right, (((1,), (1,)), ((), ())), preferred_element_type=F32)


def errors_kernel(
    rt_ref, rc_ref, xt_ref, u_hbm, v_hbm, w_hbm, r_hbm, x_hbm,
    item_a_ref, err_ref, err_t_b, tag_err_b, tag_err_t,
    u_ref, v_ref, w_ref, r_ref, x_ref, err_t, tag_err, sems,
):
    copies = [
        pltpu.make_async_copy(src, dst, sems.at[i])
        for i, (src, dst) in enumerate(
            [(v_hbm, v_ref), (w_hbm, w_ref), (x_hbm, x_ref), (u_hbm, u_ref), (r_hbm, r_ref)]
        )
    ]
    for copy in copies:
        copy.start()
    for ref in (err_ref, err_t, tag_err, tag_err_t):
        ref[...] = jnp.zeros_like(ref)
    for copy in copies[:3]:
        copy.wait()
    for s in range(x_ref.shape[0]):
        a, c = tile(xt_ref[0, s]), tile(xt_ref[1, s])
        e = dot_rows(v_ref[a, :], w_ref[c, :]) - x_ref[s].astype(F32)
        tag_err[a, c] = e.astype(BF16)
        tag_err_t[c, a] = e.T.astype(BF16)
    for copy in copies[3:]:
        copy.wait()
    count = rc_ref[0]
    for s in range(r_ref.shape[0]):
        a, c = tile(rt_ref[0, s]), tile(rt_ref[1, s])
        e = dot_rows(u_ref[a, :], v_ref[c, :]) - r_ref[s].astype(F32)
        e = jnp.where(s < count, e, 0.0)
        err_ref[a, c] = e.astype(BF16)
        err_t[c, a] = e.T.astype(BF16)
    half = item_a_ref.shape[0]
    step = 256
    for i in range(0, half, step):
        rows = pl.ds(i, step)
        part = jnp.dot(err_t[rows, :], u_ref[...], preferred_element_type=F32)
        part += jnp.dot(tag_err[rows, :], w_ref[...], preferred_element_type=F32)
        item_a_ref[rows, :] = part.astype(BF16)
    err_t_b[...] = err_t[half:, :]
    tag_err_b[...] = tag_err[half:, :]


def second_kernel(
    core_ref, x_lo_ref, err_t, tag_err, tag_err_t, u_ref, v_ref, w_ref,
    item_own, item_send, tag_own, tag_send,
):
    def halves(index, size):
        return (pl.ds(pl.multiple_of(h * size, size), size) for h in (index, 1 - index))

    mine, other = halves(core_ref[0], tag_own.shape[0])
    tag_own[...] = jnp.dot(tag_err_t[mine, :], v_ref[...], preferred_element_type=F32)
    part = jnp.dot(tag_err_t[other, :], v_ref[...], preferred_element_type=F32)
    tag_send[...] = part.astype(BF16)
    mine, other = halves(x_lo_ref[0], item_own.shape[0])
    part = jnp.dot(err_t[other, :], u_ref[...], preferred_element_type=F32)
    part += jnp.dot(tag_err[other, :], w_ref[...], preferred_element_type=F32)
    item_send[...] = part.astype(BF16)
    part = jnp.dot(err_t[mine, :], u_ref[...], preferred_element_type=F32)
    part += jnp.dot(tag_err[mine, :], w_ref[...], preferred_element_type=F32)
    item_own[...] = part


def users_kernel(err_ref, u_ref, v_ref, out_ref):
    step = 256
    for i in range(0, out_ref.shape[0], step):
        rows = pl.ds(i, step)
        grad = jnp.dot(err_ref[rows, :], v_ref[...], preferred_element_type=F32)
        old = u_ref[rows, :].astype(F32)
        out_ref[rows, :] = (old - 0.04 * (grad + 0.05 * old)).astype(BF16)


def whole():
    return pl.BlockSpec(memory_space=pltpu.VMEM)


def scalars():
    return pl.BlockSpec(memory_space=pltpu.SMEM)


def in_hbm():
    return pl.BlockSpec(memory_space=pltpu.HBM)


def like(*dims, dtype=BF16):
    return jax.ShapeDtypeStruct(dims, dtype)


def limits(mib):
    return pltpu.CompilerParams(vmem_limit_bytes=mib << 20)


def cost(flops, moved):
    return pl.CostEstimate(flops=flops, bytes_accessed=moved, transcendentals=0)


def errors(rt, rc, xt, u, v, w, r, x):
    users, rank = u.shape
    items, tags = v.shape[0], w.shape[0]
    half = items // 2
    return pl.pallas_call(
        errors_kernel,
        out_shape=(
            like(half, rank),
            like(users, items),
            like(half, users),
            like(half, tags),
            like(tags, items),
        ),
        in_specs=[scalars()] * 3 + [in_hbm()] * 5,
        out_specs=(whole(),) * 5,
        scratch_shapes=[pltpu.VMEM(a.shape, BF16) for a in (u, v, w, r, x)]
        + [
            pltpu.VMEM((items, users), BF16),
            pltpu.VMEM((items, tags), BF16),
            pltpu.SemaphoreType.DMA((5,)),
        ],
        compiler_params=limits(24),
        cost_estimate=cost(2 << 30, 6 << 20),
    )(rt, rc, xt, *(pltpu.with_memory_space_constraint(a, pltpu.HBM) for a in (u, v, w, r, x)))


def second_parts(core, x_lo, err_t, tag_err, tag_err_t, u, v, w):
    rank = u.shape[1]
    items, tags = err_t.shape[0] // 2, w.shape[0] // 2
    return pl.pallas_call(
        second_kernel,
        out_shape=(
            like(items, rank, dtype=F32),
            like(items, rank),
            like(tags, rank, dtype=F32),
            like(tags, rank),
        ),
        in_specs=[scalars()] * 2 + [whole()] * 6,
        out_specs=(whole(),) * 4,
        compiler_params=limits(16),
        cost_estimate=cost(1 << 30, 6 << 20),
    )(core, x_lo, err_t, tag_err, tag_err_t, u, v, w)


def updated_users(err, u, v):
    return pl.pallas_call(
        users_kernel,
        out_shape=like(*u.shape),
        in_specs=[whole()] * 3,
        out_specs=whole(),
        compiler_params=limits(16),
        cost_estimate=cost(1 << 30, 4 << 20),
    )(err, u, v)


def updated(old, total):
    old = old.astype(F32)
    return (old - 0.04 * (total + 0.05 * old)).astype(BF16)


def rows_from(block, start, size):
    return lax.dynamic_slice_in_dim(block, start, size, 0)


def swapped(block, mask, axis="rot"):
    n = lax.axis_size(axis)
    return lax.ppermute(block, axis, [(i, i ^ mask) for i in range(n)])


def rotated(block):
    n = lax.axis_size("rot")
    return lax.ppermute(block, "rot", [(i, (i + 1) % n) for i in range(n)])


def joined(mine, other, bit):
    return jnp.where(
        bit == 0, jnp.concatenate([mine, other], 0), jnp.concatenate([other, mine], 0)
    )


def added(own, mask):
    own = lax.reduce_precision(own, 8, 7)
    return own + swapped(own.astype(BF16), mask).astype(F32)


def tag_sum_in_plane(send, own, x_hi):
    own = own + swapped(send, 1).astype(F32)
    size = own.shape[0] // 2
    send = rows_from(own, (1 - x_hi) * size, size).astype(BF16)
    return rows_from(own, x_hi * size, size) + swapped(send, 2).astype(F32)


def new_tag_rows(total, w, core, x_hi):
    size = total.shape[0]
    shard = updated(rows_from(w, (core * 2 + x_hi) * size, size), total)
    half = joined(shard, swapped(shard, 2), x_hi)
    return joined(half, swapped(half, 1), core)


def total_of(pieces):
    return jnp.sum(pieces.astype(F32), axis=0)


def gathered(shard):
    copies = jnp.broadcast_to(shard, (lax.axis_size("tag"),) + shard.shape)
    return lax.all_to_all(copies, "tag", 0, 0)


def on_device(u, v, w, rating_tiles, rating_counts, ratings, tag_tiles, tag_values):
    items, rank = v.shape
    n_tag = lax.axis_size("tag")
    rot, tag = lax.axis_index("rot"), lax.axis_index("tag")
    core, x_hi = rot & 1, (rot >> 1) & 1
    x_lo, z = tag & 1, tag >> 1
    half, size = items // 2, items // 2 // n_tag
    columns = [[x + 2 * k for k in range(n_tag // 2)] for x in range(2)]

    item_a, err, err_t_b, tag_err_b, tag_err_t = errors(
        rating_tiles.T, rating_counts, tag_tiles.T, u, v, w, ratings, tag_values
    )
    pieces_a = lax.all_to_all(item_a.reshape(n_tag, size, rank), "tag", 0, 0)
    own_b, send_b, tag_own, tag_send = second_parts(
        core[None], x_lo[None], err_t_b, tag_err_b, tag_err_t, u, v, w
    )
    new_users = updated_users(err, u, v)
    tag_total = tag_sum_in_plane(tag_send, tag_own, x_hi)
    pair_b = (own_b + swapped(send_b, 1, "tag").astype(F32)).astype(BF16)
    pieces_a, pair_b, tag_total, new_users = lax.optimization_barrier(
        (pieces_a, pair_b, tag_total, new_users)
    )
    pieces_b = lax.all_to_all(
        pair_b.reshape(n_tag // 2, size, rank), "tag", 0, 0, axis_index_groups=columns
    )
    shard_a = rotated(updated(rows_from(v, tag * size, size), total_of(pieces_a)))
    tag_total = added(tag_total, 4)
    pieces_b, shard_a, tag_total = lax.optimization_barrier((pieces_b, shard_a, tag_total))
    new_a = gathered(shard_a)
    place = half + x_lo * (half // 2) + z * size
    shard_b = rotated(updated(rows_from(v, place, size), total_of(pieces_b)))
    tag_total = added(tag_total, 8)
    new_a, shard_b, tag_total = lax.optimization_barrier((new_a, shard_b, tag_total))
    new_b = gathered(shard_b)
    new_tags = new_tag_rows(added(tag_total, 16), w, core, x_hi)
    new_b = jnp.swapaxes(new_b.reshape(n_tag // 2, 2, size, rank), 0, 1)
    rotated_items = jnp.concatenate([new_a.reshape(half, rank), new_b.reshape(half, rank)], 0)
    return (new_users, rotated_items, new_tags)


def solution(mesh):
    placed = (
        P(("rot", "tag"), None),
        P("rot", None),
        P("tag", None),
        P(("rot", "tag"), None),
        P(("rot", "tag")),
        P(("rot", "tag"), None, None),
        P(("rot", "tag"), None),
        P(("rot", "tag"), None, None),
    )
    return jax.shard_map(
        on_device,
        mesh=mesh,
        in_specs=placed,
        out_specs=(P(("rot", "tag"), None), P("rot", None), P("tag", None)),
        check_vma=False,
    )
```

time: 101 us -> 115 us (1.14)
  starting transfers between devices: 60.3 us -> 81.3 us
  waiting for transfers between devices: 22.4 us -> 12.1 us
  other arithmetic: 4.62 us -> 6.29 us
    ppermute x8 -> x10, starting transfers between devices: 44 us -> 56.1 us  [the longest x8 44.9 us: swapped(): return lax.ppermute(block, axis, [(i, i ^ mask) for i in range(n)])]
    all_to_all x2 -> x4, starting transfers between devices: 16.2 us -> 25.2 us  [the longest x2 13.2 us: gathered(): return lax.all_to_all(copies, 'tag', 0, 0)]
    ppermute x8 -> x10, waiting for transfers between devices: 17.9 us -> 12.1 us  [the longest x8 10.2 us: swapped(): return lax.ppermute(block, axis, [(i, i ^ mask) for i in range(n)])]
    all_to_all x2 -> x4, waiting for transfers between devices: 4.5 us -> 0.03 us  [the longest x1 0.03 us: on_device(): lax.all_to_all(pair_b.reshape(n_tag // 2, size, rank), 'tag', 0, 0, axis_...]
    convert_element_type x0 -> x1, other arithmetic: none -> 1.72 us  [on_device(): pair_b = (own_b + swapped(send_b, 1, 'tag').astype(F32)).astype(BF16)]
    pallas_call x2 -> x3, Pallas kernels: 7.62 us -> 8.5 us  [the longest x1 5.21 us: errors(): pl.pallas_call(errors_kernel, out_shape=(like(half, rank), like(users, it...]
    unnamed x13 -> x14, local copies, waits for them, and re-layouts: 3.12 us -> 2.59 us
  transfers between devices with their start and end apart: 10 -> 14, of which waited for: 8 -> 5; matrix products, arithmetic and copies ran while one was open for 5% -> 5% of each run, Pallas kernels for 2% -> 1%
where the time goes in v3:
time: 115 us; the launch traced here: 114 us
  starting transfers between devices  81.3 us (71%)
  waiting for transfers between devices  12.1 us (11%)
  Pallas kernels  8.5 us (7%)
  other arithmetic  6.29 us (5%)
  local copies, waits for them, and re-layouts  4.34 us (4%)
  between operations  1.62 us (1%)
    ppermute x8, starting transfers between devices, swapped(): return lax.ppermute(block, axis, [(i, i ^ mask) for i in range(n)])  44.9 us
    all_to_all x2, starting transfers between devices, gathered(): return lax.all_to_all(copies, 'tag', 0, 0)  13.2 us
    ppermute x2, starting transfers between devices, rotated(): return lax.ppermute(block, 'rot', [(i, (i + 1) % n) for i in range(n)])  11.2 us
    ppermute x8, waiting for transfers between devices, swapped(): return lax.ppermute(block, axis, [(i, i ^ mask) for i in range(n)])  10.2 us
    all_to_all x1, starting transfers between devices, on_device(): lax.all_to_all(pair_b.reshape(n_tag // 2, size, rank), 'tag', 0, 0, axis_...  6.21 us
    all_to_all x1, starting transfers between devices, on_device(): pieces_a = lax.all_to_all(item_a.reshape(n_tag, size, rank), 'tag', 0, 0)  5.76 us
    pallas_call x1, Pallas kernels, errors(): pl.pallas_call(errors_kernel, out_shape=(like(half, rank), like(users, it...  5.21 us
    unnamed x14, local copies, waits for them, and re-layouts  2.59 us
  transfers between devices with their start and end apart: 14, of which 5 were waited for; matrix products, arithmetic and copies ran while one was open for 5% of the time, Pallas kernels for 1%

profile of v3, /device:TPU:1, one launch (start us, length us, event | category | flops | bytes accessed | tf_op | source)
XLA Modules:
  0.0 114.1 jit_solution(4603081915613794479)
XLA Ops:
  1.3 0.0 copy-start.3
  1.3 0.7 copy-done.3
  2.0 0.0 copy-start.4
  2.0 0.7 copy-done.4
  2.6 0.0 copy-start
  2.6 0.0 copy-start.1
  2.6 0.0 copy-start.2
  2.7 5.2 %shard_map.103 = (bf16[512,512]{1,0:T(8,128)(2,1)}, bf16[512,1024]{1,0:T(8,128)(2,1)S(1)}, bf16[512,512]{1,0:T(8,128)(2,1)S(1)}, bf16[512,512]{1,0:T(8,128)(2,1)S(1)}, bf16[512,1024]{1,0:T(8,128)(2,1)S(1)}) custom-call(s32[2,16]{1,0:T(2,128)S(1)} %bitcast.11, s32[1]{0:T(128)S(6)} %copy.12.rc_ref, s32[2,16]{1,0:T(2,128)S(1)} %bitcast.12, ...), custom_call_target="tpu_custom_call" | custom-call | flops 2147483648 | bytes 6291456 | tf_op jit(solution)/shard_map/pallas_call | solution.py:120
  7.9 0.0 copy-start.5
  7.9 0.0 copy-done
  7.9 0.0 copy-done.1
  7.9 0.0 copy-done.2
  7.9 1.7 %shard_map.104 = (f32[256,512]{1,0:T(8,128)S(1)}, bf16[256,512]{1,0:T(8,128)(2,1)S(1)}, f32[256,512]{1,0:T(8,128)S(1)}, bf16[256,512]{1,0:T(8,128)(2,1)}) custom-call(s32[1]{0:T(128)} %bitcast.3.core_ref, s32[1]{0:T(128)} %bitcast.4.x_lo_ref, bf16[512,512]{1,0:T(8,128)(2,1)S(1)} %get-tuple-element.23.err_t, bf16[512,512]{1,0:T(8,128)(2,1)S(1)} %get-tuple-element.24.tag_err, ...), custom_call_target="tpu_custom_call" | custom-call | flops 1073741824 | bytes 6291456 | tf_op jit(solution)/shard_map/pallas_call | solution.py:145
  9.6 0.0 copy-done.5
  9.6 8.8 %collective-permute-start.1 = (bf16[256,512]{1,0:T(8,128)(2,1)}, bf16[256,512]{1,0:T(8,128)(2,1)}, u32[]{:S(2)}, u32[]{:S(2)}) collective-permute-start(bf16[256,512]{1,0:T(8,128)(2,1)} %get-tuple-element.29), channel_id=1, source_target_pairs={{0,16},{16,0},{32,48},{48,32},{64,80},{80,64},{96,112},{112,96},{1... | collective-permute-start | bytes 786440 | tf_op jit(solution)/shard_map/ppermute | solution.py:182
  18.4 5.8 %all-to-all-start = ((bf16[16,32,512]{2,1,0:T(8,128)(2,1)}), bf16[16,32,512]{2,1,0:T(8,128)(2,1)}, u32[]{:S(2)}, u32[]{:S(2)}) async-start(bf16[16,32,512]{2,1,0:T(8,128)(2,1)} %bitcast.2), calls=%async_computation | async-start | bytes 1048576 | tf_op jit(solution)/shard_map/all_to_all | solution.py:236
  24.2 3.2 %collective-permute-start = (bf16[256,512]{1,0:T(8,128)(2,1)S(1)}, bf16[256,512]{1,0:T(8,128)(2,1)}, u32[]{:S(2)}, u32[]{:S(2)}) collective-permute-start(bf16[256,512]{1,0:T(8,128)(2,1)S(1)} %get-tuple-element.27), channel_id=1, source_target_pairs={{0,1},{1,0},{2,3},{3,2},{4,5},{5,4},{6,7},{7,6},{8,9},{9,8},{10,11... | collective-permute-start | bytes 786440 | tf_op jit(solution)/shard_map/ppermute | solution.py:182
  27.4 0.0 copy-start.6
  27.4 1.2 %copy-done.6 = bf16[512,1024]{1,0:T(8,128)(2,1)S(1)} copy-done((bf16[512,1024]{1,0:T(8,128)(2,1)S(1)}, bf16[512,1024]{1,0:T(8,128)(2,1)}, u32[]{:S(2)}) %copy-start.6) | copy-done | bytes 1048600
  28.6 1.6 %shard_map.105 = bf16[512,512]{1,0:T(8,128)(2,1)} custom-call(bf16[512,1024]{1,0:T(8,128)(2,1)S(1)} %copy-done.6, bf16[512,512]{1,0:T(8,128)(2,1)S(1)} %copy-done.2, bf16[1024,512]{1,0:T(8,128)(2,1)S(1)} %copy-done), custom_call_target="tpu_custom_call" | custom-call | flops 1073741824 | bytes 4194304 | tf_op jit(solution)/shard_map/pallas_call | solution.py:161
  30.2 0.0 collective-permute-done.1
  30.2 1.0 convert_add_fusion
  31.3 4.4 %collective-permute-start.2 = (bf16[128,512]{1,0:T(8,128)(2,1)S(1)}, bf16[128,512]{1,0:T(8,128)(2,1)S(1)}, u32[]{:S(2)}, u32[]{:S(2)}) collective-permute-start(bf16[128,512]{1,0:T(8,128)(2,1)S(1)} %dynamic-slice_convert_fusion), channel_id=1, source_target_pairs={{0,32},{16,48},{32,0},{48,16},{64,96},{80,112},{96,64},{112,80},{1... | collective-permute-start | bytes 393224 | tf_op jit(solution)/shard_map/ppermute | solution.py:182
  35.6 0.0 collective-permute-done
  35.7 1.7 %add_convert_fusion = bf16[256,512]{1,0:T(8,128)(2,1)} fusion(f32[256,512]{1,0:T(8,128)S(1)} %get-tuple-element.26, bf16[256,512]{1,0:T(8,128)(2,1)} %collective-permute-done), kind=kLoop, calls=%fused_computation.5 | loop fusion | flops 393216 | bytes 1048576 | tf_op jit(solution)/shard_map/convert_element_type | solution.py:242
  37.4 6.0 %collective-permute-done.2 = bf16[128,512]{1,0:T(8,128)(2,1)S(1)} collective-permute-done((bf16[128,512]{1,0:T(8,128)(2,1)S(1)}, bf16[128,512]{1,0:T(8,128)(2,1)S(1)}, u32[]{:S(2)}, u32[]{:S(2)}) %collective-permute-start.2) | collective-permute-done | bytes 131104 | tf_op jit(solution)/shard_map/ppermute | solution.py:182
  43.4 0.0 all-to-all-done
  43.5 6.2 %all-to-all-start.1 = ((bf16[8,32,512]{2,1,0:T(8,128)(2,1)}), bf16[8,32,512]{2,1,0:T(8,128)(2,1)S(1)}, u32[]{:S(2)}, u32[]{:S(2)}) async-start(bf16[8,32,512]{2,1,0:T(8,128)(2,1)} %bitcast.5), calls=%async_computation.1 | async-start | bytes 524288 | tf_op jit(solution)/shard_map/all_to_all | solution.py:246
  49.7 1.1 convert_reduce_fusion
  50.8 3.2 %collective-permute-start.4 = (bf16[128,512]{1,0:T(8,128)(2,1)S(1)}, bf16[128,512]{1,0:T(8,128)(2,1)S(1)}, u32[]{:S(2)}, u32[]{:S(2)}) collective-permute-start(bf16[128,512]{1,0:T(8,128)(2,1)S(1)} %reduce-precision_convert_fusion.2), channel_id=1, source_target_pairs={{0,64},{16,80},{32,96},{48,112},{64,0},{80,16},{96,32},{112,48},{1... | collective-permute-start | bytes 393224 | tf_op jit(solution)/shard_map/ppermute | solution.py:182
  54.1 4.3 %collective-permute-start.3 = (bf16[32,512]{1,0:T(8,128)(2,1)S(1)}, bf16[32,512]{1,0:T(8,128)(2,1)S(1)}, u32[]{:S(2)}, u32[]{:S(2)}) collective-permute-start(bf16[32,512]{1,0:T(8,128)(2,1)S(1)} %fusion.5), channel_id=1, source_target_pairs={{0,16},{16,32},{32,48},{48,64},{64,80},{80,96},{96,112},{112,128},... | collective-permute-start | bytes 98312 | tf_op jit(solution)/shard_map/ppermute | solution.py:187
  58.4 0.0 collective-permute-done.4
  58.4 1.0 collective-permute-done.3
  59.4 0.0 all-to-all-done.1
  59.4 0.8 broadcast_in_dim.14
  60.2 7.2 %all-to-all-start.2 = ((bf16[16,32,512]{2,1,0:T(8,128)(2,1)}), bf16[16,32,512]{2,1,0:T(8,128)(2,1)S(1)}, u32[]{:S(2)}, u32[]{:S(2)}) async-start(bf16[16,32,512]{2,1,0:T(8,128)(2,1)} %broadcast_in_dim.14), calls=%async_computation.2 | async-start | bytes 1048576 | tf_op jit(solution)/shard_map/all_to_all | solution.py:221
  67.5 4.2 %collective-permute-start.6 = (bf16[128,512]{1,0:T(8,128)(2,1)S(1)}, bf16[128,512]{1,0:T(8,128)(2,1)S(1)}, u32[]{:S(2)}, u32[]{:S(2)}) collective-permute-start(bf16[128,512]{1,0:T(8,128)(2,1)S(1)} %reduce-precision_convert_fusion.1), channel_id=1, source_target_pairs={{0,128},{16,144},{32,160},{48,176},{64,192},{80,208},{96,224},{112... | collective-permute-start | bytes 393224 | tf_op jit(solution)/shard_map/ppermute | solution.py:182
  71.7 6.9 %collective-permute-start.5 = (bf16[32,512]{1,0:T(8,128)(2,1)S(1)}, bf16[32,512]{1,0:T(8,128)(2,1)S(1)}, u32[]{:S(2)}, u32[]{:S(2)}) collective-permute-start(bf16[32,512]{1,0:T(8,128)(2,1)S(1)} %fusion.8), channel_id=1, source_target_pairs={{0,16},{16,32},{32,48},{48,64},{64,80},{80,96},{96,112},{112,128},... | collective-permute-start | bytes 98312 | tf_op jit(solution)/shard_map/ppermute | solution.py:187
  78.6 0.0 collective-permute-done.6
  78.7 1.0 collective-permute-done.5
  79.6 0.0 all-to-all-done.2
  79.7 6.4 %collective-permute-start.7 = (bf16[128,512]{1,0:T(8,128)(2,1)S(1)}, bf16[128,512]{1,0:T(8,128)(2,1)S(1)}, u32[]{:S(2)}, u32[]{:S(2)}) collective-permute-start(bf16[128,512]{1,0:T(8,128)(2,1)S(1)} %reduce-precision_convert_fusion), channel_id=1, source_target_pairs={{0,256},{16,272},{32,288},{48,304},{64,320},{80,336},{96,352},{112... | collective-permute-start | bytes 393224 | tf_op jit(solution)/shard_map/ppermute | solution.py:182
  86.1 0.8 broadcast_in_dim.15
  86.9 6.0 %all-to-all-start.3 = ((bf16[16,32,512]{2,1,0:T(8,128)(2,1)}), bf16[16,32,512]{2,1,0:T(8,128)(2,1)S(1)}, u32[]{:S(2)}, u32[]{:S(2)}) async-start(bf16[16,32,512]{2,1,0:T(8,128)(2,1)} %broadcast_in_dim.15), calls=%async_computation.3 | async-start | bytes 1048576 | tf_op jit(solution)/shard_map/all_to_all | solution.py:221
  93.0 0.0 collective-permute-done.7
  93.0 0.1 fusion.2
  93.1 6.4 %collective-permute-start.8 = (bf16[128,512]{1,0:T(8,128)(2,1)S(1)}, bf16[128,512]{1,0:T(8,128)(2,1)S(1)}, u32[]{:S(2)}, u32[]{:S(2)}) collective-permute-start(bf16[128,512]{1,0:T(8,128)(2,1)S(1)} %fusion.2), channel_id=1, source_target_pairs={{0,32},{16,48},{32,0},{48,16},{64,96},{80,112},{96,64},{112,80},{1... | collective-permute-start | bytes 393224 | tf_op jit(solution)/shard_map/ppermute | solution.py:182
  99.5 3.0 %collective-permute-done.8 = bf16[128,512]{1,0:T(8,128)(2,1)S(1)} collective-permute-done((bf16[128,512]{1,0:T(8,128)(2,1)S(1)}, bf16[128,512]{1,0:T(8,128)(2,1)S(1)}, u32[]{:S(2)}, u32[]{:S(2)}) %collective-permute-start.8) | collective-permute-done | bytes 131104 | tf_op jit(solution)/shard_map/ppermute | solution.py:182
  102.5 0.1 maximum_select_fusion.1
  102.5 8.3 %collective-permute-start.9 = (bf16[256,512]{1,0:T(8,128)(2,1)S(1)}, bf16[256,512]{1,0:T(8,128)(2,1)S(1)}, u32[]{:S(2)}, u32[]{:S(2)}) collective-permute-start(bf16[256,512]{1,0:T(8,128)(2,1)S(1)} %maximum_select_fusion.1), channel_id=1, source_target_pairs={{0,16},{16,0},{32,48},{48,32},{64,80},{80,64},{96,112},{112,96},{1... | collective-permute-start | bytes 786440 | tf_op jit(solution)/shard_map/ppermute | solution.py:182
  110.9 1.1 collective-permute-done.9
  112.0 1.0 maximum_select_fusion
  113.0 0.0 all-to-all-done.3
  113.1 1.0 pad_maximum_fusion
  (11 shorter events, 0.3 us)
Async XLA Ops:
  1.3 0.7 copy-start.3
  2.0 0.7 copy-start.4
  2.6 5.2 %copy-start = (bf16[1024,512]{1,0:T(8,128)(2,1)S(1)}, bf16[1024,512]{1,0:T(8,128)(2,1)}, u32[]{:S(2)}) copy-start(bf16[1024,512]{1,0:T(8,128)(2,1)} %v_ref.3) | copy-start | bytes 3145732
  2.6 5.3 %copy-start.1 = (bf16[512,512]{1,0:T(8,128)(2,1)S(1)}, bf16[512,512]{1,0:T(8,128)(2,1)}, u32[]{:S(2)}) copy-start(bf16[512,512]{1,0:T(8,128)(2,1)} %w_ref.1) | copy-start | bytes 1572868
  2.6 5.3 %copy-start.2 = (bf16[512,512]{1,0:T(8,128)(2,1)S(1)}, bf16[512,512]{1,0:T(8,128)(2,1)}, u32[]{:S(2)}) copy-start(bf16[512,512]{1,0:T(8,128)(2,1)} %u_ref.3) | copy-start | bytes 1572868
  7.9 1.8 %copy-start.5 = (bf16[512,1024]{1,0:T(8,128)(2,1)}, bf16[512,1024]{1,0:T(8,128)(2,1)S(1)}, u32[]{:S(2)}) copy-start(bf16[512,1024]{1,0:T(8,128)(2,1)S(1)} %get-tuple-element.30.err_ref) | copy-start | bytes 3145732
  9.6 20.6 %collective-permute-start.1 = (bf16[256,512]{1,0:T(8,128)(2,1)}, bf16[256,512]{1,0:T(8,128)(2,1)}, u32[]{:S(2)}, u32[]{:S(2)}) collective-permute-start(bf16[256,512]{1,0:T(8,128)(2,1)} %get-tuple-element.29), channel_id=1, source_target_pairs={{0,16},{16,0},{32,48},{48,32},{64,80},{80,64},{96,112},{112,96},{1... | collective-permute-start | bytes 786440 | tf_op jit(solution)/shard_map/ppermute | solution.py:182
  18.4 25.0 %all-to-all-start = ((bf16[16,32,512]{2,1,0:T(8,128)(2,1)}), bf16[16,32,512]{2,1,0:T(8,128)(2,1)}, u32[]{:S(2)}, u32[]{:S(2)}) async-start(bf16[16,32,512]{2,1,0:T(8,128)(2,1)} %bitcast.2), calls=%async_computation | async-start | bytes 1048576 | tf_op jit(solution)/shard_map/all_to_all | solution.py:236
  24.2 11.5 %collective-permute-start = (bf16[256,512]{1,0:T(8,128)(2,1)S(1)}, bf16[256,512]{1,0:T(8,128)(2,1)}, u32[]{:S(2)}, u32[]{:S(2)}) collective-permute-start(bf16[256,512]{1,0:T(8,128)(2,1)S(1)} %get-tuple-element.27), channel_id=1, source_target_pairs={{0,1},{1,0},{2,3},{3,2},{4,5},{5,4},{6,7},{7,6},{8,9},{9,8},{10,11... | collective-permute-start | bytes 786440 | tf_op jit(solution)/shard_map/ppermute | solution.py:182
  27.4 1.2 %copy-start.6 = (bf16[512,1024]{1,0:T(8,128)(2,1)S(1)}, bf16[512,1024]{1,0:T(8,128)(2,1)}, u32[]{:S(2)}) copy-start(bf16[512,1024]{1,0:T(8,128)(2,1)} %copy-done.5) | copy-start | bytes 3145732
  31.3 12.1 %collective-permute-start.2 = (bf16[128,512]{1,0:T(8,128)(2,1)S(1)}, bf16[128,512]{1,0:T(8,128)(2,1)S(1)}, u32[]{:S(2)}, u32[]{:S(2)}) collective-permute-start(bf16[128,512]{1,0:T(8,128)(2,1)S(1)} %dynamic-slice_convert_fusion), channel_id=1, source_target_pairs={{0,32},{16,48},{32,0},{48,16},{64,96},{80,112},{96,64},{112,80},{1... | collective-permute-start | bytes 393224 | tf_op jit(solution)/shard_map/ppermute | solution.py:182
  43.5 15.9 %all-to-all-start.1 = ((bf16[8,32,512]{2,1,0:T(8,128)(2,1)}), bf16[8,32,512]{2,1,0:T(8,128)(2,1)S(1)}, u32[]{:S(2)}, u32[]{:S(2)}) async-start(bf16[8,32,512]{2,1,0:T(8,128)(2,1)} %bitcast.5), calls=%async_computation.1 | async-start | bytes 524288 | tf_op jit(solution)/shard_map/all_to_all | solution.py:246
  50.8 7.6 %collective-permute-start.4 = (bf16[128,512]{1,0:T(8,128)(2,1)S(1)}, bf16[128,512]{1,0:T(8,128)(2,1)S(1)}, u32[]{:S(2)}, u32[]{:S(2)}) collective-permute-start(bf16[128,512]{1,0:T(8,128)(2,1)S(1)} %reduce-precision_convert_fusion.2), channel_id=1, source_target_pairs={{0,64},{16,80},{32,96},{48,112},{64,0},{80,16},{96,32},{112,48},{1... | collective-permute-start | bytes 393224 | tf_op jit(solution)/shard_map/ppermute | solution.py:182
  54.1 5.3 %collective-permute-start.3 = (bf16[32,512]{1,0:T(8,128)(2,1)S(1)}, bf16[32,512]{1,0:T(8,128)(2,1)S(1)}, u32[]{:S(2)}, u32[]{:S(2)}) collective-permute-start(bf16[32,512]{1,0:T(8,128)(2,1)S(1)} %fusion.5), channel_id=1, source_target_pairs={{0,16},{16,32},{32,48},{48,64},{64,80},{80,96},{96,112},{112,128},... | collective-permute-start | bytes 98312 | tf_op jit(solution)/shard_map/ppermute | solution.py:187
  60.2 19.4 %all-to-all-start.2 = ((bf16[16,32,512]{2,1,0:T(8,128)(2,1)}), bf16[16,32,512]{2,1,0:T(8,128)(2,1)S(1)}, u32[]{:S(2)}, u32[]{:S(2)}) async-start(bf16[16,32,512]{2,1,0:T(8,128)(2,1)} %broadcast_in_dim.14), calls=%async_computation.2 | async-start | bytes 1048576 | tf_op jit(solution)/shard_map/all_to_all | solution.py:221
  67.5 11.2 %collective-permute-start.6 = (bf16[128,512]{1,0:T(8,128)(2,1)S(1)}, bf16[128,512]{1,0:T(8,128)(2,1)S(1)}, u32[]{:S(2)}, u32[]{:S(2)}) collective-permute-start(bf16[128,512]{1,0:T(8,128)(2,1)S(1)} %reduce-precision_convert_fusion.1), channel_id=1, source_target_pairs={{0,128},{16,144},{32,160},{48,176},{64,192},{80,208},{96,224},{112... | collective-permute-start | bytes 393224 | tf_op jit(solution)/shard_map/ppermute | solution.py:182
  71.7 7.9 %collective-permute-start.5 = (bf16[32,512]{1,0:T(8,128)(2,1)S(1)}, bf16[32,512]{1,0:T(8,128)(2,1)S(1)}, u32[]{:S(2)}, u32[]{:S(2)}) collective-permute-start(bf16[32,512]{1,0:T(8,128)(2,1)S(1)} %fusion.8), channel_id=1, source_target_pairs={{0,16},{16,32},{32,48},{48,64},{64,80},{80,96},{96,112},{112,128},... | collective-permute-start | bytes 98312 | tf_op jit(solution)/shard_map/ppermute | solution.py:187
  79.7 13.3 %collective-permute-start.7 = (bf16[128,512]{1,0:T(8,128)(2,1)S(1)}, bf16[128,512]{1,0:T(8,128)(2,1)S(1)}, u32[]{:S(2)}, u32[]{:S(2)}) collective-permute-start(bf16[128,512]{1,0:T(8,128)(2,1)S(1)} %reduce-precision_convert_fusion), channel_id=1, source_target_pairs={{0,256},{16,272},{32,288},{48,304},{64,320},{80,336},{96,352},{112... | collective-permute-start | bytes 393224 | tf_op jit(solution)/shard_map/ppermute | solution.py:182
  86.9 26.1 %all-to-all-start.3 = ((bf16[16,32,512]{2,1,0:T(8,128)(2,1)}), bf16[16,32,512]{2,1,0:T(8,128)(2,1)S(1)}, u32[]{:S(2)}, u32[]{:S(2)}) async-start(bf16[16,32,512]{2,1,0:T(8,128)(2,1)} %broadcast_in_dim.15), calls=%async_computation.3 | async-start | bytes 1048576 | tf_op jit(solution)/shard_map/all_to_all | solution.py:221
  93.1 9.4 %collective-permute-start.8 = (bf16[128,512]{1,0:T(8,128)(2,1)S(1)}, bf16[128,512]{1,0:T(8,128)(2,1)S(1)}, u32[]{:S(2)}, u32[]{:S(2)}) collective-permute-start(bf16[128,512]{1,0:T(8,128)(2,1)S(1)} %fusion.2), channel_id=1, source_target_pairs={{0,32},{16,48},{32,0},{48,16},{64,96},{80,112},{96,64},{112,80},{1... | collective-permute-start | bytes 393224 | tf_op jit(solution)/shard_map/ppermute | solution.py:182
  102.5 9.5 %collective-permute-start.9 = (bf16[256,512]{1,0:T(8,128)(2,1)S(1)}, bf16[256,512]{1,0:T(8,128)(2,1)S(1)}, u32[]{:S(2)}, u32[]{:S(2)}) collective-permute-start(bf16[256,512]{1,0:T(8,128)(2,1)S(1)} %maximum_select_fusion.1), channel_id=1, source_target_pairs={{0,16},{16,0},{32,48},{48,32},{64,80},{80,64},{96,112},{112,96},{1... | collective-permute-start | bytes 786440 | tf_op jit(solution)/shard_map/ppermute | solution.py:182

commit v4 on v2

--- a/solution.py
+++ b/solution.py
@@ -19,14 +19,17 @@
 
 
 def grads_kernel(
-    rt_ref, rc_ref, xt_ref, core_ref, u_hbm, v_hbm, w_hbm, r_hbm, x_hbm,
+    rc_ref, core_ref, xt_hbm, rt_hbm, u_hbm, v_hbm, w_hbm, r_hbm, x_hbm,
     item_ref, send_ref, own_ref, err_ref,
-    u_ref, v_ref, w_ref, r_ref, x_ref, err_t, tag_err, tag_err_t, sems,
+    xt_ref, rt_ref, u_ref, v_ref, w_ref, r_ref, x_ref, err_t, tag_err, tag_err_t, sems,
 ):
     copies = [
         pltpu.make_async_copy(src, dst, sems.at[i])
         for i, (src, dst) in enumerate(
-            [(v_hbm, v_ref), (w_hbm, w_ref), (x_hbm, x_ref), (u_hbm, u_ref), (r_hbm, r_ref)]
+            [
+                (xt_hbm, xt_ref), (v_hbm, v_ref), (w_hbm, w_ref), (x_hbm, x_ref),
+                (rt_hbm, rt_ref), (u_hbm, u_ref), (r_hbm, r_ref),
+            ]
         )
     ]
     for copy in copies:
@@ -35,14 +38,14 @@
     err_t[...] = jnp.zeros_like(err_t)
     tag_err[...] = jnp.zeros_like(tag_err)
     tag_err_t[...] = jnp.zeros_like(tag_err_t)
-    for copy in copies[:3]:
+    for copy in copies[:4]:
         copy.wait()
     for s in range(x_ref.shape[0]):
         a, c = tile(xt_ref[0, s]), tile(xt_ref[1, s])
         e = dot_rows(v_ref[a, :], w_ref[c, :]) - x_ref[s].astype(F32)
         tag_err[a, c] = e.astype(BF16)
         tag_err_t[c, a] = e.T.astype(BF16)
-    for copy in copies[3:]:
+    for copy in copies[4:]:
         copy.wait()
     count = rc_ref[0]
     for s in range(r_ref.shape[0]):
@@ -74,6 +77,15 @@
         out_ref[rows, :] = (old - 0.04 * (grad + 0.05 * old)).astype(BF16)
 
 
+def split_kernel(bit_ref, own_ref, arrived_ref, keep_ref, send_ref):
+    size = keep_ref.shape[0]
+    mine, other = (
+        pl.ds(pl.multiple_of(h * size, size), size) for h in (bit_ref[0], 1 - bit_ref[0])
+    )
+    keep_ref[...] = own_ref[mine, :] + arrived_ref[mine, :].astype(F32)
+    send_ref[...] = (own_ref[other, :] + arrived_ref[other, :].astype(F32)).astype(BF16)
+
+
 def whole():
     return pl.BlockSpec(memory_space=pltpu.VMEM)
 
@@ -97,18 +109,19 @@
             jax.ShapeDtypeStruct((tags // 2, rank), F32),
             jax.ShapeDtypeStruct((users, items), BF16),
         ),
-        in_specs=[scalars()] * 4 + [in_hbm()] * 5,
+        in_specs=[scalars()] * 2 + [in_hbm()] * 7,
         out_specs=(whole(),) * 4,
-        scratch_shapes=[pltpu.VMEM(a.shape, BF16) for a in (u, v, w, r, x)]
+        scratch_shapes=[pltpu.SMEM(a.shape, a.dtype) for a in (xt, rt)]
+        + [pltpu.VMEM(a.shape, BF16) for a in (u, v, w, r, x)]
         + [
             pltpu.VMEM((items, users), BF16),
             pltpu.VMEM((items, tags), BF16),
             pltpu.VMEM((tags, items), BF16),
-            pltpu.SemaphoreType.DMA((5,)),
+            pltpu.SemaphoreType.DMA((7,)),
         ],
         compiler_params=pltpu.CompilerParams(vmem_limit_bytes=24 << 20),
         cost_estimate=pl.CostEstimate(flops=3 << 30, bytes_accessed=6 << 20, transcendentals=0),
-    )(rt, rc, xt, core, *(pltpu.with_memory_space_constraint(a, pltpu.HBM) for a in (u, v, w, r, x)))
+    )(rc, core, *(pltpu.with_memory_space_constraint(a, pltpu.HBM) for a in (xt, rt, u, v, w, r, x)))
 
 
 def updated_users(err, u, v):
@@ -122,6 +135,21 @@
     )(err, u, v)
 
 
+def split_sum(bit, own, arrived):
+    size, rank = own.shape[0] // 2, own.shape[1]
+    return pl.pallas_call(
+        split_kernel,
+        out_shape=(
+            jax.ShapeDtypeStruct((size, rank), F32),
+            jax.ShapeDtypeStruct((size, rank), BF16),
+        ),
+        in_specs=[scalars(), whole(), whole()],
+        out_specs=(whole(),) * 2,
+        compiler_params=pltpu.CompilerParams(vmem_limit_bytes=4 << 20),
+        cost_estimate=pl.CostEstimate(flops=1 << 18, bytes_accessed=1 << 20, transcendentals=0),
+    )(bit, own, arrived)
+
+
 def exchanged(pieces, axis):
     return lax.all_to_all(pieces, axis, 0, 0)
 
@@ -152,11 +180,8 @@
 
 
 def tag_sum_in_plane(send, own, x_hi):
-    own = own + swapped(send, 1).astype(F32)
-    size = own.shape[0] // 2
-    send = part_of(own, 1 - x_hi, size).astype(BF16)
-    own = part_of(own, x_hi, size) + swapped(send, 2).astype(F32)
-    return added(own, 4)
+    own, send = split_sum(x_hi[None], own, swapped(send, 1))
+    return added(own + swapped(send, 2).astype(F32), 4)
 
 
 def new_tag_rows(total, w, core, x_hi):
@@ -174,16 +199,14 @@
         rating_tiles.T, rating_counts, tag_tiles.T, core[None], u, v, w, ratings, tag_values
     )
     item_pieces = exchanged(item_part.reshape(n_tag, -1, rank), "tag")
-    new_users = updated_users(err, u, v)
     tag_total = tag_sum_in_plane(tag_send, tag_own, x_hi)
-    item_pieces, tag_total, new_users = lax.optimization_barrier(
-        (item_pieces, tag_total, new_users)
-    )
+    item_pieces, _ = lax.optimization_barrier((item_pieces, tag_total))
     shard = part_of(v, lax.axis_index("tag"), v.shape[0] // n_tag)
     shard = updated(shard, jnp.sum(item_pieces.astype(F32), axis=0))
     shard = lax.ppermute(shard, "rot", [(i, (i + 1) % n_rot) for i in range(n_rot)])
     tag_total = added(tag_total, 8)
-    shard, tag_total = lax.optimization_barrier((shard, tag_total))
+    shard, err, _ = lax.optimization_barrier((shard, err, tag_total))
+    new_users = updated_users(err, u, v)
     copies = jnp.broadcast_to(shard, (n_tag,) + shard.shape)
     rotated_items = exchanged(copies, "tag").reshape(v.shape)
     new_tags = new_tag_rows(added(tag_total, 16), w, core, x_hi)

time: 101 us -> 99.9 us (0.989)
  the two profiles are of different devices: /device:TPU:1 before, /device:TPU:15 now
where the time goes in v4:
time: 99.9 us; the launch traced here: 99.3 us
  starting transfers between devices  55.5 us (56%)
  waiting for transfers between devices  28.3 us (28%)
  Pallas kernels  7.14 us (7%)
  other arithmetic  3.57 us (4%)
  local copies, waits for them, and re-layouts  3.35 us (3%)
  between operations  1.45 us (1%)
    ppermute x7, starting transfers between devices, swapped(): return lax.ppermute(block, 'rot', [(i, i ^ mask) for i in range(n)])  31 us
    ppermute x7, waiting for transfers between devices, swapped(): return lax.ppermute(block, 'rot', [(i, i ^ mask) for i in range(n)])  26.2 us
    all_to_all x2, starting transfers between devices, exchanged(): return lax.all_to_all(pieces, axis, 0, 0)  16.3 us
    ppermute x1, starting transfers between devices, on_device(): lax.ppermute(shard, 'rot', [(i, (i + 1) % n_rot) for i in range(n_rot)])  8.2 us
    pallas_call x1, Pallas kernels, partials(): pl.pallas_call(grads_kernel, out_shape=(jax.ShapeDtypeStruct((items, rank...  5.53 us
    unnamed x5, local copies, waits for them, and re-layouts  2.27 us
  transfers between devices with their start and end apart: 10, of which 8 were waited for; matrix products, arithmetic and copies ran while one was open for 4% of the time, Pallas kernels for 2%

profile of v4, /device:TPU:15, one launch (start us, length us, event | category | flops | bytes accessed | tf_op | source)
XLA Modules:
  0.0 99.3 jit_solution(7587598202589372873)
XLA Ops:
  1.3 5.5 %shard_map.103 = (bf16[1024,512]{1,0:T(8,128)(2,1)}, bf16[256,512]{1,0:T(8,128)(2,1)S(1)}, f32[256,512]{1,0:T(8,128)S(1)}, bf16[512,1024]{1,0:T(8,128)(2,1)S(1)}) custom-call(s32[1]{0:T(128)S(6)} %copy.12.rc_ref, s32[1]{0:T(128)} %bitcast.core_ref, s32[2,16]{1,0:T(2,128)} %bitcast.6, s32[2,16]{1,0:T(2,128)} %bitcast.7, bf16[512,512]{1,0:T(8,128)(2,1)} %u_ref.1, ...), custom_call_target="tpu_custom_call" | custom-call | flops 3221225472 | bytes 6291456 | tf_op jit(solution)/shard_map/pallas_call | solution.py:104
  6.8 11.2 %all-to-all-start = ((bf16[16,64,512]{2,1,0:T(8,128)(2,1)}), bf16[16,64,512]{2,1,0:T(8,128)(2,1)}, u32[]{:S(2)}, u32[]{:S(2)}) async-start(bf16[16,64,512]{2,1,0:T(8,128)(2,1)} %bitcast.3), calls=%async_computation | async-start | bytes 2097152 | tf_op jit(solution)/shard_map/all_to_all | solution.py:154
  18.1 3.1 %collective-permute-start = (bf16[256,512]{1,0:T(8,128)(2,1)S(1)}, bf16[256,512]{1,0:T(8,128)(2,1)S(1)}, u32[]{:S(2)}, u32[]{:S(2)}) collective-permute-start(bf16[256,512]{1,0:T(8,128)(2,1)S(1)} %get-tuple-element.14), channel_id=1, source_target_pairs={{0,16},{16,0},{32,48},{48,32},{64,80},{80,64},{96,112},{112,96},{1... | collective-permute-start | bytes 786440 | tf_op jit(solution)/shard_map/ppermute | solution.py:168
  21.2 1.1 %collective-permute-done.arrived_ref = bf16[256,512]{1,0:T(8,128)(2,1)S(1)} collective-permute-done((bf16[256,512]{1,0:T(8,128)(2,1)S(1)}, bf16[256,512]{1,0:T(8,128)(2,1)S(1)}, u32[]{:S(2)}, u32[]{:S(2)}) %collective-permute-start) | collective-permute-done | bytes 262176 | tf_op jit(solution)/shard_map/ppermute | solution.py:168
  22.4 3.0 %collective-permute-start.1 = (bf16[128,512]{1,0:T(8,128)(2,1)S(1)}, bf16[128,512]{1,0:T(8,128)(2,1)S(1)}, u32[]{:S(2)}, u32[]{:S(2)}) collective-permute-start(bf16[128,512]{1,0:T(8,128)(2,1)S(1)} %get-tuple-element.16), channel_id=1, source_target_pairs={{0,32},{16,48},{32,0},{48,16},{64,96},{80,112},{96,64},{112,80},{1... | collective-permute-start | bytes 393224 | tf_op jit(solution)/shard_map/ppermute | solution.py:168
  25.4 5.6 %collective-permute-done.1 = bf16[128,512]{1,0:T(8,128)(2,1)S(1)} collective-permute-done((bf16[128,512]{1,0:T(8,128)(2,1)S(1)}, bf16[128,512]{1,0:T(8,128)(2,1)S(1)}, u32[]{:S(2)}, u32[]{:S(2)}) %collective-permute-start.1) | collective-permute-done | bytes 131104 | tf_op jit(solution)/shard_map/ppermute | solution.py:168
  31.1 2.1 %collective-permute-start.2 = (bf16[128,512]{1,0:T(8,128)(2,1)S(1)}, bf16[128,512]{1,0:T(8,128)(2,1)S(1)}, u32[]{:S(2)}, u32[]{:S(2)}) collective-permute-start(bf16[128,512]{1,0:T(8,128)(2,1)S(1)} %fusion.3), channel_id=1, source_target_pairs={{0,64},{16,80},{32,96},{48,112},{64,0},{80,16},{96,32},{112,48},{1... | collective-permute-start | bytes 393224 | tf_op jit(solution)/shard_map/ppermute | solution.py:168
  33.2 0.0 copy-start
  33.2 4.0 %collective-permute-done.2 = bf16[128,512]{1,0:T(8,128)(2,1)S(1)} collective-permute-done((bf16[128,512]{1,0:T(8,128)(2,1)S(1)}, bf16[128,512]{1,0:T(8,128)(2,1)S(1)}, u32[]{:S(2)}, u32[]{:S(2)}) %collective-permute-start.2) | collective-permute-done | bytes 131104 | tf_op jit(solution)/shard_map/ppermute | solution.py:168
  37.2 0.1 reduce-precision_convert_fusion.1
  37.3 4.2 %collective-permute-start.4 = (bf16[128,512]{1,0:T(8,128)(2,1)S(1)}, bf16[128,512]{1,0:T(8,128)(2,1)S(1)}, u32[]{:S(2)}, u32[]{:S(2)}) collective-permute-start(bf16[128,512]{1,0:T(8,128)(2,1)S(1)} %get-tuple-element.23), channel_id=1, source_target_pairs={{0,128},{16,144},{32,160},{48,176},{64,192},{80,208},{96,224},{112... | collective-permute-start | bytes 393224 | tf_op jit(solution)/shard_map/ppermute | solution.py:168
  41.5 0.8 all-to-all-done
  42.3 1.4 %convert_reduce_fusion = f32[64,512]{1,0:T(8,128)S(1)} fusion(bf16[16,64,512]{2,1,0:T(8,128)(2,1)} %all-to-all-done), kind=kLoop, calls=%fused_computation | loop fusion | flops 1015808 | bytes 1179648 | tf_op jit(solution)/shard_map/reduce_sum | solution.py:205
  43.7 0.0 copy-done
  43.8 8.2 %collective-permute-start.3 = (bf16[64,512]{1,0:T(8,128)(2,1)S(1)}, bf16[64,512]{1,0:T(8,128)(2,1)S(1)}, u32[]{:S(2)}, u32[]{:S(2)}) collective-permute-start(bf16[64,512]{1,0:T(8,128)(2,1)S(1)} %fusion.6), channel_id=1, source_target_pairs={{0,16},{16,32},{32,48},{48,64},{64,80},{80,96},{96,112},{112,128},... | collective-permute-start | bytes 196616 | tf_op jit(solution)/shard_map/ppermute | solution.py:206
  52.0 0.0 collective-permute-done.4
  52.0 1.3 %collective-permute-done.3 = bf16[64,512]{1,0:T(8,128)(2,1)S(1)} collective-permute-done((bf16[64,512]{1,0:T(8,128)(2,1)S(1)}, bf16[64,512]{1,0:T(8,128)(2,1)S(1)}, u32[]{:S(2)}, u32[]{:S(2)}) %collective-permute-start.3) | collective-permute-done | bytes 65568 | tf_op jit(solution)/shard_map/ppermute | solution.py:206
  53.3 1.1 %broadcast_in_dim.11 = bf16[16,64,512]{2,1,0:T(8,128)(2,1)} broadcast(bf16[64,512]{1,0:T(8,128)(2,1)S(1)} %collective-permute-done.3), dimensions={1,2} | broadcast | bytes 1114112 | tf_op jit(solution)/shard_map/broadcast_in_dim | solution.py:210
  54.4 5.1 %all-to-all-start.1 = ((bf16[16,64,512]{2,1,0:T(8,128)(2,1)}), bf16[16,64,512]{2,1,0:T(8,128)(2,1)}, u32[]{:S(2)}, u32[]{:S(2)}) async-start(bf16[16,64,512]{2,1,0:T(8,128)(2,1)} %broadcast_in_dim.11), calls=%async_computation.1 | async-start | bytes 2097152 | tf_op jit(solution)/shard_map/all_to_all | solution.py:154
  59.5 5.3 %collective-permute-start.5 = (bf16[128,512]{1,0:T(8,128)(2,1)S(1)}, bf16[128,512]{1,0:T(8,128)(2,1)S(1)}, u32[]{:S(2)}, u32[]{:S(2)}) collective-permute-start(bf16[128,512]{1,0:T(8,128)(2,1)S(1)} %get-tuple-element.21), channel_id=1, source_target_pairs={{0,256},{16,272},{32,288},{48,304},{64,320},{80,336},{96,352},{112... | collective-permute-start | bytes 393224 | tf_op jit(solution)/shard_map/ppermute | solution.py:168
  64.8 0.0 copy-start.1
  64.8 4.4 %collective-permute-done.5 = bf16[128,512]{1,0:T(8,128)(2,1)S(1)} collective-permute-done((bf16[128,512]{1,0:T(8,128)(2,1)S(1)}, bf16[128,512]{1,0:T(8,128)(2,1)S(1)}, u32[]{:S(2)}, u32[]{:S(2)}) %collective-permute-start.5) | collective-permute-done | bytes 131104 | tf_op jit(solution)/shard_map/ppermute | solution.py:168
  69.2 1.0 fusion.2
  70.2 10.1 %collective-permute-start.6 = (bf16[128,512]{1,0:T(8,128)(2,1)S(1)}, bf16[128,512]{1,0:T(8,128)(2,1)S(1)}, u32[]{:S(2)}, u32[]{:S(2)}) collective-permute-start(bf16[128,512]{1,0:T(8,128)(2,1)S(1)} %fusion.2), channel_id=1, source_target_pairs={{0,32},{16,48},{32,0},{48,16},{64,96},{80,112},{96,64},{112,80},{1... | collective-permute-start | bytes 393224 | tf_op jit(solution)/shard_map/ppermute | solution.py:168
  80.3 9.9 %collective-permute-done.6 = bf16[128,512]{1,0:T(8,128)(2,1)S(1)} collective-permute-done((bf16[128,512]{1,0:T(8,128)(2,1)S(1)}, bf16[128,512]{1,0:T(8,128)(2,1)S(1)}, u32[]{:S(2)}, u32[]{:S(2)}) %collective-permute-start.6) | collective-permute-done | bytes 131104 | tf_op jit(solution)/shard_map/ppermute | solution.py:168
  90.2 0.1 maximum_select_fusion.1
  90.2 3.1 %collective-permute-start.7 = (bf16[256,512]{1,0:T(8,128)(2,1)S(1)}, bf16[256,512]{1,0:T(8,128)(2,1)S(1)}, u32[]{:S(2)}, u32[]{:S(2)}) collective-permute-start(bf16[256,512]{1,0:T(8,128)(2,1)S(1)} %maximum_select_fusion.1), channel_id=1, source_target_pairs={{0,16},{16,0},{32,48},{48,32},{64,80},{80,64},{96,112},{112,96},{1... | collective-permute-start | bytes 786440 | tf_op jit(solution)/shard_map/ppermute | solution.py:168
  93.3 1.1 %collective-permute-done.7 = bf16[256,512]{1,0:T(8,128)(2,1)S(1)} collective-permute-done((bf16[256,512]{1,0:T(8,128)(2,1)S(1)}, bf16[256,512]{1,0:T(8,128)(2,1)S(1)}, u32[]{:S(2)}, u32[]{:S(2)}) %collective-permute-start.7) | collective-permute-done | bytes 262176 | tf_op jit(solution)/shard_map/ppermute | solution.py:168
  94.5 1.0 %maximum_select_fusion = bf16[512,512]{1,0:T(8,128)(2,1)} fusion(bf16[256,512]{1,0:T(8,128)(2,1)S(1)} %collective-permute-done.7, bf16[256,512]{1,0:T(8,128)(2,1)S(1)} %maximum_select_fusion.1, pred[]{:T(512)S(6)} %eq.6), kind=kLoop, calls=%fused_computation.1 | loop fusion | flops 2359296 | bytes 1048577 | tf_op jit(solution)/shard_map/jit(_where)/select_n | solution.py:172
  95.5 0.0 copy-done.1
  95.5 1.6 %shard_map.105 = bf16[512,512]{1,0:T(8,128)(2,1)} custom-call(bf16[512,1024]{1,0:T(8,128)(2,1)S(1)} %get-tuple-element.19.err_ref, bf16[512,512]{1,0:T(8,128)(2,1)S(1)} %copy-done.1, bf16[1024,512]{1,0:T(8,128)(2,1)S(1)} %copy-done), custom_call_target="tpu_custom_call" | custom-call | flops 1073741824 | bytes 4194304 | tf_op jit(solution)/shard_map/pallas_call | solution.py:128
  97.0 0.0 all-to-all-done.1
  97.0 2.3 %copy.13 = bf16[1024,512]{1,0:T(8,128)(2,1)} copy(bf16[1024,512]{1,0:T(8,128)(2,1)} %bitcast.5) | data formatting | bytes 2097152
  (4 shorter events, 0.1 us)
Async XLA Ops:
  6.8 35.5 %all-to-all-start = ((bf16[16,64,512]{2,1,0:T(8,128)(2,1)}), bf16[16,64,512]{2,1,0:T(8,128)(2,1)}, u32[]{:S(2)}, u32[]{:S(2)}) async-start(bf16[16,64,512]{2,1,0:T(8,128)(2,1)} %bitcast.3), calls=%async_computation | async-start | bytes 2097152 | tf_op jit(solution)/shard_map/all_to_all | solution.py:154
  18.1 4.3 %collective-permute-start = (bf16[256,512]{1,0:T(8,128)(2,1)S(1)}, bf16[256,512]{1,0:T(8,128)(2,1)S(1)}, u32[]{:S(2)}, u32[]{:S(2)}) collective-permute-start(bf16[256,512]{1,0:T(8,128)(2,1)S(1)} %get-tuple-element.14), channel_id=1, source_target_pairs={{0,16},{16,0},{32,48},{48,32},{64,80},{80,64},{96,112},{112,96},{1... | collective-permute-start | bytes 786440 | tf_op jit(solution)/shard_map/ppermute | solution.py:168
  22.4 8.7 %collective-permute-start.1 = (bf16[128,512]{1,0:T(8,128)(2,1)S(1)}, bf16[128,512]{1,0:T(8,128)(2,1)S(1)}, u32[]{:S(2)}, u32[]{:S(2)}) collective-permute-start(bf16[128,512]{1,0:T(8,128)(2,1)S(1)} %get-tuple-element.16), channel_id=1, source_target_pairs={{0,32},{16,48},{32,0},{48,16},{64,96},{80,112},{96,64},{112,80},{1... | collective-permute-start | bytes 393224 | tf_op jit(solution)/shard_map/ppermute | solution.py:168
  31.1 6.1 %collective-permute-start.2 = (bf16[128,512]{1,0:T(8,128)(2,1)S(1)}, bf16[128,512]{1,0:T(8,128)(2,1)S(1)}, u32[]{:S(2)}, u32[]{:S(2)}) collective-permute-start(bf16[128,512]{1,0:T(8,128)(2,1)S(1)} %fusion.3), channel_id=1, source_target_pairs={{0,64},{16,80},{32,96},{48,112},{64,0},{80,16},{96,32},{112,48},{1... | collective-permute-start | bytes 393224 | tf_op jit(solution)/shard_map/ppermute | solution.py:168
  33.2 10.5 %copy-start = (bf16[1024,512]{1,0:T(8,128)(2,1)S(1)}, bf16[1024,512]{1,0:T(8,128)(2,1)}, u32[]{:S(2)}) copy-start(bf16[1024,512]{1,0:T(8,128)(2,1)} %v_ref.1) | copy-start | bytes 3145732
  37.3 14.7 %collective-permute-start.4 = (bf16[128,512]{1,0:T(8,128)(2,1)S(1)}, bf16[128,512]{1,0:T(8,128)(2,1)S(1)}, u32[]{:S(2)}, u32[]{:S(2)}) collective-permute-start(bf16[128,512]{1,0:T(8,128)(2,1)S(1)} %get-tuple-element.23), channel_id=1, source_target_pairs={{0,128},{16,144},{32,160},{48,176},{64,192},{80,208},{96,224},{112... | collective-permute-start | bytes 393224 | tf_op jit(solution)/shard_map/ppermute | solution.py:168
  43.8 9.5 %collective-permute-start.3 = (bf16[64,512]{1,0:T(8,128)(2,1)S(1)}, bf16[64,512]{1,0:T(8,128)(2,1)S(1)}, u32[]{:S(2)}, u32[]{:S(2)}) collective-permute-start(bf16[64,512]{1,0:T(8,128)(2,1)S(1)} %fusion.6), channel_id=1, source_target_pairs={{0,16},{16,32},{32,48},{48,64},{64,80},{80,96},{96,112},{112,128},... | collective-permute-start | bytes 196616 | tf_op jit(solution)/shard_map/ppermute | solution.py:206
  54.4 42.7 %all-to-all-start.1 = ((bf16[16,64,512]{2,1,0:T(8,128)(2,1)}), bf16[16,64,512]{2,1,0:T(8,128)(2,1)}, u32[]{:S(2)}, u32[]{:S(2)}) async-start(bf16[16,64,512]{2,1,0:T(8,128)(2,1)} %broadcast_in_dim.11), calls=%async_computation.1 | async-start | bytes 2097152 | tf_op jit(solution)/shard_map/all_to_all | solution.py:154
  59.5 9.7 %collective-permute-start.5 = (bf16[128,512]{1,0:T(8,128)(2,1)S(1)}, bf16[128,512]{1,0:T(8,128)(2,1)S(1)}, u32[]{:S(2)}, u32[]{:S(2)}) collective-permute-start(bf16[128,512]{1,0:T(8,128)(2,1)S(1)} %get-tuple-element.21), channel_id=1, source_target_pairs={{0,256},{16,272},{32,288},{48,304},{64,320},{80,336},{96,352},{112... | collective-permute-start | bytes 393224 | tf_op jit(solution)/shard_map/ppermute | solution.py:168
  64.8 30.7 %copy-start.1 = (bf16[512,512]{1,0:T(8,128)(2,1)S(1)}, bf16[512,512]{1,0:T(8,128)(2,1)}, u32[]{:S(2)}) copy-start(bf16[512,512]{1,0:T(8,128)(2,1)} %u_ref.1) | copy-start | bytes 1572868
  70.2 20.0 %collective-permute-start.6 = (bf16[128,512]{1,0:T(8,128)(2,1)S(1)}, bf16[128,512]{1,0:T(8,128)(2,1)S(1)}, u32[]{:S(2)}, u32[]{:S(2)}) collective-permute-start(bf16[128,512]{1,0:T(8,128)(2,1)S(1)} %fusion.2), channel_id=1, source_target_pairs={{0,32},{16,48},{32,0},{48,16},{64,96},{80,112},{96,64},{112,80},{1... | collective-permute-start | bytes 393224 | tf_op jit(solution)/shard_map/ppermute | solution.py:168
  90.2 4.2 %collective-permute-start.7 = (bf16[256,512]{1,0:T(8,128)(2,1)S(1)}, bf16[256,512]{1,0:T(8,128)(2,1)S(1)}, u32[]{:S(2)}, u32[]{:S(2)}) collective-permute-start(bf16[256,512]{1,0:T(8,128)(2,1)S(1)} %maximum_select_fusion.1), channel_id=1, source_target_pairs={{0,16},{16,0},{32,48},{48,32},{64,80},{80,64},{96,112},{112,96},{1... | collective-permute-start | bytes 786440 | tf_op jit(solution)/shard_map/ppermute | solution.py:168

commit v5 on v4

--- a/solution.py
+++ b/solution.py
@@ -130,7 +130,7 @@
         out_shape=jax.ShapeDtypeStruct(u.shape, BF16),
         in_specs=[whole()] * 3,
         out_specs=whole(),
-        compiler_params=pltpu.CompilerParams(vmem_limit_bytes=16 << 20),
+        compiler_params=pltpu.CompilerParams(vmem_limit_bytes=8 << 20),
         cost_estimate=pl.CostEstimate(flops=1 << 30, bytes_accessed=4 << 20, transcendentals=0),
     )(err, u, v)
 
@@ -181,7 +181,8 @@
 
 def tag_sum_in_plane(send, own, x_hi):
     own, send = split_sum(x_hi[None], own, swapped(send, 1))
-    return added(own + swapped(send, 2).astype(F32), 4)
+    own = added(own + swapped(send, 2).astype(F32), 4)
+    return added(own, 8)
 
 
 def new_tag_rows(total, w, core, x_hi):
@@ -200,16 +201,16 @@
     )
     item_pieces = exchanged(item_part.reshape(n_tag, -1, rank), "tag")
     tag_total = tag_sum_in_plane(tag_send, tag_own, x_hi)
-    item_pieces, _ = lax.optimization_barrier((item_pieces, tag_total))
+    item_pieces, tag_total = lax.optimization_barrier((item_pieces, tag_total))
     shard = part_of(v, lax.axis_index("tag"), v.shape[0] // n_tag)
     shard = updated(shard, jnp.sum(item_pieces.astype(F32), axis=0))
     shard = lax.ppermute(shard, "rot", [(i, (i + 1) % n_rot) for i in range(n_rot)])
-    tag_total = added(tag_total, 8)
-    shard, err, _ = lax.optimization_barrier((shard, err, tag_total))
+    tag_total = added(tag_total, 16)
+    shard, err, tag_total = lax.optimization_barrier((shard, err, tag_total))
     new_users = updated_users(err, u, v)
     copies = jnp.broadcast_to(shard, (n_tag,) + shard.shape)
     rotated_items = exchanged(copies, "tag").reshape(v.shape)
-    new_tags = new_tag_rows(added(tag_total, 16), w, core, x_hi)
+    new_tags = new_tag_rows(tag_total, w, core, x_hi)
     return (new_users, rotated_items, new_tags)
 
 

time: 99.9 us -> 105 us (1.051)
  the two profiles are of different devices: /device:TPU:15 before, /device:TPU:8 now
where the time goes in v5:
time: 105 us; the launch traced here: 104 us
  starting transfers between devices  49.6 us (47%)
  waiting for transfers between devices  38.9 us (37%)
  Pallas kernels  7.14 us (7%)
  other arithmetic  3.7 us (4%)
  local copies, waits for them, and re-layouts  3.35 us (3%)
  between operations  1.49 us (1%)
    ppermute x7, starting transfers between devices, swapped(): return lax.ppermute(block, 'rot', [(i, i ^ mask) for i in range(n)])  27.9 us
    ppermute x7, waiting for transfers between devices, swapped(): return lax.ppermute(block, 'rot', [(i, i ^ mask) for i in range(n)])  20.3 us
    all_to_all x2, starting transfers between devices, exchanged(): return lax.all_to_all(pieces, axis, 0, 0)  19.7 us
    all_to_all x2, waiting for transfers between devices, exchanged(): return lax.all_to_all(pieces, axis, 0, 0)  13.3 us
    pallas_call x1, Pallas kernels, partials(): pl.pallas_call(grads_kernel, out_shape=(jax.ShapeDtypeStruct((items, rank...  5.53 us
    ppermute x1, waiting for transfers between devices, on_device(): lax.ppermute(shard, 'rot', [(i, (i + 1) % n_rot) for i in range(n_rot)])  5.24 us
    unnamed x5, local copies, waits for them, and re-layouts  2.27 us
  transfers between devices with their start and end apart: 10, of which 8 were waited for; matrix products, arithmetic and copies ran while one was open for 4% of the time, Pallas kernels for 2%

profile of v5, /device:TPU:8, one launch (start us, length us, event | category | flops | bytes accessed | tf_op | source)
XLA Modules:
  0.0 104.1 jit_solution(16626979527910821348)
XLA Ops:
  1.3 5.5 %shard_map.103 = (bf16[1024,512]{1,0:T(8,128)(2,1)}, bf16[256,512]{1,0:T(8,128)(2,1)S(1)}, f32[256,512]{1,0:T(8,128)S(1)}, bf16[512,1024]{1,0:T(8,128)(2,1)S(1)}) custom-call(s32[1]{0:T(128)S(6)} %copy.12.rc_ref, s32[1]{0:T(128)} %bitcast.core_ref, s32[2,16]{1,0:T(2,128)} %bitcast.6, s32[2,16]{1,0:T(2,128)} %bitcast.7, bf16[512,512]{1,0:T(8,128)(2,1)} %u_ref.1, ...), custom_call_target="tpu_custom_call" | custom-call | flops 3221225472 | bytes 6291456 | tf_op jit(solution)/shard_map/pallas_call | solution.py:104
  6.8 11.4 %all-to-all-start = ((bf16[16,64,512]{2,1,0:T(8,128)(2,1)}), bf16[16,64,512]{2,1,0:T(8,128)(2,1)}, u32[]{:S(2)}, u32[]{:S(2)}) async-start(bf16[16,64,512]{2,1,0:T(8,128)(2,1)} %bitcast.3), calls=%async_computation | async-start | bytes 2097152 | tf_op jit(solution)/shard_map/all_to_all | solution.py:154
  18.2 1.9 %collective-permute-start = (bf16[256,512]{1,0:T(8,128)(2,1)S(1)}, bf16[256,512]{1,0:T(8,128)(2,1)S(1)}, u32[]{:S(2)}, u32[]{:S(2)}) collective-permute-start(bf16[256,512]{1,0:T(8,128)(2,1)S(1)} %get-tuple-element.16), channel_id=1, source_target_pairs={{0,16},{16,0},{32,48},{48,32},{64,80},{80,64},{96,112},{112,96},{1... | collective-permute-start | bytes 786440 | tf_op jit(solution)/shard_map/ppermute | solution.py:168
  20.2 1.5 %collective-permute-done.arrived_ref = bf16[256,512]{1,0:T(8,128)(2,1)S(1)} collective-permute-done((bf16[256,512]{1,0:T(8,128)(2,1)S(1)}, bf16[256,512]{1,0:T(8,128)(2,1)S(1)}, u32[]{:S(2)}, u32[]{:S(2)}) %collective-permute-start) | collective-permute-done | bytes 262176 | tf_op jit(solution)/shard_map/ppermute | solution.py:168
  21.7 4.6 %collective-permute-start.1 = (bf16[128,512]{1,0:T(8,128)(2,1)S(1)}, bf16[128,512]{1,0:T(8,128)(2,1)S(1)}, u32[]{:S(2)}, u32[]{:S(2)}) collective-permute-start(bf16[128,512]{1,0:T(8,128)(2,1)S(1)} %get-tuple-element.18), channel_id=1, source_target_pairs={{0,32},{16,48},{32,0},{48,16},{64,96},{80,112},{96,64},{112,80},{1... | collective-permute-start | bytes 393224 | tf_op jit(solution)/shard_map/ppermute | solution.py:168
  26.4 4.9 %collective-permute-done.1 = bf16[128,512]{1,0:T(8,128)(2,1)S(1)} collective-permute-done((bf16[128,512]{1,0:T(8,128)(2,1)S(1)}, bf16[128,512]{1,0:T(8,128)(2,1)S(1)}, u32[]{:S(2)}, u32[]{:S(2)}) %collective-permute-start.1) | collective-permute-done | bytes 131104 | tf_op jit(solution)/shard_map/ppermute | solution.py:168
  31.3 2.4 %collective-permute-start.2 = (bf16[128,512]{1,0:T(8,128)(2,1)S(1)}, bf16[128,512]{1,0:T(8,128)(2,1)S(1)}, u32[]{:S(2)}, u32[]{:S(2)}) collective-permute-start(bf16[128,512]{1,0:T(8,128)(2,1)S(1)} %fusion.3), channel_id=1, source_target_pairs={{0,64},{16,80},{32,96},{48,112},{64,0},{80,16},{96,32},{112,48},{1... | collective-permute-start | bytes 393224 | tf_op jit(solution)/shard_map/ppermute | solution.py:168
  33.7 4.5 %collective-permute-done.2 = bf16[128,512]{1,0:T(8,128)(2,1)S(1)} collective-permute-done((bf16[128,512]{1,0:T(8,128)(2,1)S(1)}, bf16[128,512]{1,0:T(8,128)(2,1)S(1)}, u32[]{:S(2)}, u32[]{:S(2)}) %collective-permute-start.2) | collective-permute-done | bytes 131104 | tf_op jit(solution)/shard_map/ppermute | solution.py:168
  38.2 0.1 fusion.7
  38.2 4.5 %collective-permute-start.3 = (bf16[128,512]{1,0:T(8,128)(2,1)S(1)}, bf16[128,512]{1,0:T(8,128)(2,1)S(1)}, u32[]{:S(2)}, u32[]{:S(2)}) collective-permute-start(bf16[128,512]{1,0:T(8,128)(2,1)S(1)} %fusion.7), channel_id=1, source_target_pairs={{0,128},{16,144},{32,160},{48,176},{64,192},{80,208},{96,224},{112... | collective-permute-start | bytes 393224 | tf_op jit(solution)/shard_map/ppermute | solution.py:168
  42.7 0.0 copy-start
  42.8 4.2 %collective-permute-done.3 = bf16[128,512]{1,0:T(8,128)(2,1)S(1)} collective-permute-done((bf16[128,512]{1,0:T(8,128)(2,1)S(1)}, bf16[128,512]{1,0:T(8,128)(2,1)S(1)}, u32[]{:S(2)}, u32[]{:S(2)}) %collective-permute-start.3) | collective-permute-done | bytes 131104 | tf_op jit(solution)/shard_map/ppermute | solution.py:168
  47.0 0.1 convert_add_fusion.1
  47.1 0.0 all-to-all-done
  47.1 6.7 %collective-permute-start.5 = (bf16[128,512]{1,0:T(8,128)(2,1)S(1)}, bf16[128,512]{1,0:T(8,128)(2,1)S(1)}, u32[]{:S(2)}, u32[]{:S(2)}) collective-permute-start(bf16[128,512]{1,0:T(8,128)(2,1)S(1)} %reduce-precision_convert_fusion), channel_id=1, source_target_pairs={{0,256},{16,272},{32,288},{48,304},{64,320},{80,336},{96,352},{112... | collective-permute-start | bytes 393224 | tf_op jit(solution)/shard_map/ppermute | solution.py:168
  53.8 1.4 %convert_reduce_fusion = f32[64,512]{1,0:T(8,128)S(1)} fusion(bf16[16,64,512]{2,1,0:T(8,128)(2,1)} %all-to-all-done), kind=kLoop, calls=%fused_computation | loop fusion | flops 1015808 | bytes 1179648 | tf_op jit(solution)/shard_map/reduce_sum | solution.py:206
  55.2 0.0 copy-done
  55.3 1.9 %collective-permute-start.4 = (bf16[64,512]{1,0:T(8,128)(2,1)S(1)}, bf16[64,512]{1,0:T(8,128)(2,1)S(1)}, u32[]{:S(2)}, u32[]{:S(2)}) collective-permute-start(bf16[64,512]{1,0:T(8,128)(2,1)S(1)} %fusion.6), channel_id=1, source_target_pairs={{0,16},{16,32},{32,48},{48,64},{64,80},{80,96},{96,112},{112,128},... | collective-permute-start | bytes 196616 | tf_op jit(solution)/shard_map/ppermute | solution.py:207
  57.2 0.8 collective-permute-done.5
  58.0 5.2 %collective-permute-done.4 = bf16[64,512]{1,0:T(8,128)(2,1)S(1)} collective-permute-done((bf16[64,512]{1,0:T(8,128)(2,1)S(1)}, bf16[64,512]{1,0:T(8,128)(2,1)S(1)}, u32[]{:S(2)}, u32[]{:S(2)}) %collective-permute-start.4) | collective-permute-done | bytes 65568 | tf_op jit(solution)/shard_map/ppermute | solution.py:207
  63.3 1.1 %broadcast_in_dim.11 = bf16[16,64,512]{2,1,0:T(8,128)(2,1)} broadcast(bf16[64,512]{1,0:T(8,128)(2,1)S(1)} %collective-permute-done.4), dimensions={1,2} | broadcast | bytes 1114112 | tf_op jit(solution)/shard_map/broadcast_in_dim | solution.py:211
  64.3 8.3 %all-to-all-start.1 = ((bf16[16,64,512]{2,1,0:T(8,128)(2,1)}), bf16[16,64,512]{2,1,0:T(8,128)(2,1)}, u32[]{:S(2)}, u32[]{:S(2)}) async-start(bf16[16,64,512]{2,1,0:T(8,128)(2,1)} %broadcast_in_dim.11), calls=%async_computation.1 | async-start | bytes 2097152 | tf_op jit(solution)/shard_map/all_to_all | solution.py:154
  72.6 0.0 copy-start.1
  72.6 1.0 fusion.2
  73.7 5.9 %collective-permute-start.6 = (bf16[128,512]{1,0:T(8,128)(2,1)S(1)}, bf16[128,512]{1,0:T(8,128)(2,1)S(1)}, u32[]{:S(2)}, u32[]{:S(2)}) collective-permute-start(bf16[128,512]{1,0:T(8,128)(2,1)S(1)} %fusion.2), channel_id=1, source_target_pairs={{0,32},{16,48},{32,0},{48,16},{64,96},{80,112},{96,64},{112,80},{1... | collective-permute-start | bytes 393224 | tf_op jit(solution)/shard_map/ppermute | solution.py:168
  79.6 4.3 %collective-permute-done.6 = bf16[128,512]{1,0:T(8,128)(2,1)S(1)} collective-permute-done((bf16[128,512]{1,0:T(8,128)(2,1)S(1)}, bf16[128,512]{1,0:T(8,128)(2,1)S(1)}, u32[]{:S(2)}, u32[]{:S(2)}) %collective-permute-start.6) | collective-permute-done | bytes 131104 | tf_op jit(solution)/shard_map/ppermute | solution.py:168
  83.9 0.1 maximum_select_fusion.1
  84.0 1.9 %collective-permute-start.7 = (bf16[256,512]{1,0:T(8,128)(2,1)S(1)}, bf16[256,512]{1,0:T(8,128)(2,1)S(1)}, u32[]{:S(2)}, u32[]{:S(2)}) collective-permute-start(bf16[256,512]{1,0:T(8,128)(2,1)S(1)} %maximum_select_fusion.1), channel_id=1, source_target_pairs={{0,16},{16,0},{32,48},{48,32},{64,80},{80,64},{96,112},{112,96},{1... | collective-permute-start | bytes 786440 | tf_op jit(solution)/shard_map/ppermute | solution.py:168
  85.9 0.0 copy-done.1
  85.9 1.6 %shard_map.105 = bf16[512,512]{1,0:T(8,128)(2,1)} custom-call(bf16[512,1024]{1,0:T(8,128)(2,1)S(1)} %get-tuple-element.22.err_ref, bf16[512,512]{1,0:T(8,128)(2,1)S(1)} %copy-done.1, bf16[1024,512]{1,0:T(8,128)(2,1)S(1)} %copy-done), custom_call_target="tpu_custom_call" | custom-call | flops 1073741824 | bytes 4194304 | tf_op jit(solution)/shard_map/pallas_call | solution.py:128
  87.5 0.0 collective-permute-done.7
  87.5 1.0 maximum_select_fusion
  88.5 13.3 %all-to-all-done.1 = bf16[16,64,512]{2,1,0:T(8,128)(2,1)} async-done(((bf16[16,64,512]{2,1,0:T(8,128)(2,1)}), bf16[16,64,512]{2,1,0:T(8,128)(2,1)}, u32[]{:S(2)}, u32[]{:S(2)}) %all-to-all-start.1) | async-done | bytes 1048608 | tf_op jit(solution)/shard_map/all_to_all | solution.py:154
  101.8 2.3 %copy.13 = bf16[1024,512]{1,0:T(8,128)(2,1)} copy(bf16[1024,512]{1,0:T(8,128)(2,1)} %bitcast.5) | data formatting | bytes 2097152
  (5 shorter events, 0.2 us)
Async XLA Ops:
  6.8 40.3 %all-to-all-start = ((bf16[16,64,512]{2,1,0:T(8,128)(2,1)}), bf16[16,64,512]{2,1,0:T(8,128)(2,1)}, u32[]{:S(2)}, u32[]{:S(2)}) async-start(bf16[16,64,512]{2,1,0:T(8,128)(2,1)} %bitcast.3), calls=%async_computation | async-start | bytes 2097152 | tf_op jit(solution)/shard_map/all_to_all | solution.py:154
  18.2 3.4 %collective-permute-start = (bf16[256,512]{1,0:T(8,128)(2,1)S(1)}, bf16[256,512]{1,0:T(8,128)(2,1)S(1)}, u32[]{:S(2)}, u32[]{:S(2)}) collective-permute-start(bf16[256,512]{1,0:T(8,128)(2,1)S(1)} %get-tuple-element.16), channel_id=1, source_target_pairs={{0,16},{16,0},{32,48},{48,32},{64,80},{80,64},{96,112},{112,96},{1... | collective-permute-start | bytes 786440 | tf_op jit(solution)/shard_map/ppermute | solution.py:168
  21.7 9.6 %collective-permute-start.1 = (bf16[128,512]{1,0:T(8,128)(2,1)S(1)}, bf16[128,512]{1,0:T(8,128)(2,1)S(1)}, u32[]{:S(2)}, u32[]{:S(2)}) collective-permute-start(bf16[128,512]{1,0:T(8,128)(2,1)S(1)} %get-tuple-element.18), channel_id=1, source_target_pairs={{0,32},{16,48},{32,0},{48,16},{64,96},{80,112},{96,64},{112,80},{1... | collective-permute-start | bytes 393224 | tf_op jit(solution)/shard_map/ppermute | solution.py:168
  31.3 6.9 %collective-permute-start.2 = (bf16[128,512]{1,0:T(8,128)(2,1)S(1)}, bf16[128,512]{1,0:T(8,128)(2,1)S(1)}, u32[]{:S(2)}, u32[]{:S(2)}) collective-permute-start(bf16[128,512]{1,0:T(8,128)(2,1)S(1)} %fusion.3), channel_id=1, source_target_pairs={{0,64},{16,80},{32,96},{48,112},{64,0},{80,16},{96,32},{112,48},{1... | collective-permute-start | bytes 393224 | tf_op jit(solution)/shard_map/ppermute | solution.py:168
  38.2 8.8 %collective-permute-start.3 = (bf16[128,512]{1,0:T(8,128)(2,1)S(1)}, bf16[128,512]{1,0:T(8,128)(2,1)S(1)}, u32[]{:S(2)}, u32[]{:S(2)}) collective-permute-start(bf16[128,512]{1,0:T(8,128)(2,1)S(1)} %fusion.7), channel_id=1, source_target_pairs={{0,128},{16,144},{32,160},{48,176},{64,192},{80,208},{96,224},{112... | collective-permute-start | bytes 393224 | tf_op jit(solution)/shard_map/ppermute | solution.py:168
  42.7 12.5 %copy-start = (bf16[1024,512]{1,0:T(8,128)(2,1)S(1)}, bf16[1024,512]{1,0:T(8,128)(2,1)}, u32[]{:S(2)}) copy-start(bf16[1024,512]{1,0:T(8,128)(2,1)} %v_ref.1) | copy-start | bytes 3145732
  47.1 10.9 %collective-permute-start.5 = (bf16[128,512]{1,0:T(8,128)(2,1)S(1)}, bf16[128,512]{1,0:T(8,128)(2,1)S(1)}, u32[]{:S(2)}, u32[]{:S(2)}) collective-permute-start(bf16[128,512]{1,0:T(8,128)(2,1)S(1)} %reduce-precision_convert_fusion), channel_id=1, source_target_pairs={{0,256},{16,272},{32,288},{48,304},{64,320},{80,336},{96,352},{112... | collective-permute-start | bytes 393224 | tf_op jit(solution)/shard_map/ppermute | solution.py:168
  55.3 8.0 %collective-permute-start.4 = (bf16[64,512]{1,0:T(8,128)(2,1)S(1)}, bf16[64,512]{1,0:T(8,128)(2,1)S(1)}, u32[]{:S(2)}, u32[]{:S(2)}) collective-permute-start(bf16[64,512]{1,0:T(8,128)(2,1)S(1)} %fusion.6), channel_id=1, source_target_pairs={{0,16},{16,32},{32,48},{48,64},{64,80},{80,96},{96,112},{112,128},... | collective-permute-start | bytes 196616 | tf_op jit(solution)/shard_map/ppermute | solution.py:207
  64.3 37.5 %all-to-all-start.1 = ((bf16[16,64,512]{2,1,0:T(8,128)(2,1)}), bf16[16,64,512]{2,1,0:T(8,128)(2,1)}, u32[]{:S(2)}, u32[]{:S(2)}) async-start(bf16[16,64,512]{2,1,0:T(8,128)(2,1)} %broadcast_in_dim.11), calls=%async_computation.1 | async-start | bytes 2097152 | tf_op jit(solution)/shard_map/all_to_all | solution.py:154
  72.6 13.3 %copy-start.1 = (bf16[512,512]{1,0:T(8,128)(2,1)S(1)}, bf16[512,512]{1,0:T(8,128)(2,1)}, u32[]{:S(2)}) copy-start(bf16[512,512]{1,0:T(8,128)(2,1)} %u_ref.1) | copy-start | bytes 1572868
  73.7 10.2 %collective-permute-start.6 = (bf16[128,512]{1,0:T(8,128)(2,1)S(1)}, bf16[128,512]{1,0:T(8,128)(2,1)S(1)}, u32[]{:S(2)}, u32[]{:S(2)}) collective-permute-start(bf16[128,512]{1,0:T(8,128)(2,1)S(1)} %fusion.2), channel_id=1, source_target_pairs={{0,32},{16,48},{32,0},{48,16},{64,96},{80,112},{96,64},{112,80},{1... | collective-permute-start | bytes 393224 | tf_op jit(solution)/shard_map/ppermute | solution.py:168
  84.0 3.5 %collective-permute-start.7 = (bf16[256,512]{1,0:T(8,128)(2,1)S(1)}, bf16[256,512]{1,0:T(8,128)(2,1)S(1)}, u32[]{:S(2)}, u32[]{:S(2)}) collective-permute-start(bf16[256,512]{1,0:T(8,128)(2,1)S(1)} %maximum_select_fusion.1), channel_id=1, source_target_pairs={{0,16},{16,0},{32,48},{48,32},{64,80},{80,64},{96,112},{112,96},{1... | collective-permute-start | bytes 786440 | tf_op jit(solution)/shard_map/ppermute | solution.py:168

commit v6 on v4

--- a/solution.py
+++ b/solution.py
@@ -18,10 +18,14 @@
     return lax.dot_general(left, right, (((1,), (1,)), ((), ())), preferred_element_type=F32)
 
 
+def dot_cols(left, right):
+    return lax.dot_general(left, right, (((0,), (0,)), ((), ())), preferred_element_type=F32)
+
+
 def grads_kernel(
     rc_ref, core_ref, xt_hbm, rt_hbm, u_hbm, v_hbm, w_hbm, r_hbm, x_hbm,
     item_ref, send_ref, own_ref, err_ref,
-    xt_ref, rt_ref, u_ref, v_ref, w_ref, r_ref, x_ref, err_t, tag_err, tag_err_t, sems,
+    xt_ref, rt_ref, u_ref, v_ref, w_ref, r_ref, x_ref, tag_err, sems,
 ):
     copies = [
         pltpu.make_async_copy(src, dst, sems.at[i])
@@ -35,16 +39,13 @@
     for copy in copies:
         copy.start()
     err_ref[...] = jnp.zeros_like(err_ref)
-    err_t[...] = jnp.zeros_like(err_t)
     tag_err[...] = jnp.zeros_like(tag_err)
-    tag_err_t[...] = jnp.zeros_like(tag_err_t)
     for copy in copies[:4]:
         copy.wait()
     for s in range(x_ref.shape[0]):
         a, c = tile(xt_ref[0, s]), tile(xt_ref[1, s])
         e = dot_rows(v_ref[a, :], w_ref[c, :]) - x_ref[s].astype(F32)
         tag_err[a, c] = e.astype(BF16)
-        tag_err_t[c, a] = e.T.astype(BF16)
     for copy in copies[4:]:
         copy.wait()
     count = rc_ref[0]
@@ -53,18 +54,17 @@
         e = dot_rows(u_ref[a, :], v_ref[c, :]) - r_ref[s].astype(F32)
         e = jnp.where(s < count, e, 0.0)
         err_ref[a, c] = e.astype(BF16)
-        err_t[c, a] = e.T.astype(BF16)
     step = 256
     for i in range(0, item_ref.shape[0], step):
         rows = pl.ds(i, step)
-        part = jnp.dot(err_t[rows, :], u_ref[...], preferred_element_type=F32)
+        part = dot_cols(err_ref[:, rows], u_ref[...])
         part += jnp.dot(tag_err[rows, :], w_ref[...], preferred_element_type=F32)
         item_ref[rows, :] = part.astype(BF16)
     half = own_ref.shape[0]
     core = core_ref[0]
     mine, other = (pl.ds(pl.multiple_of(h * half, half), half) for h in (core, 1 - core))
-    own_ref[...] = jnp.dot(tag_err_t[mine, :], v_ref[...], preferred_element_type=F32)
-    part = jnp.dot(tag_err_t[other, :], v_ref[...], preferred_element_type=F32)
+    own_ref[...] = dot_cols(tag_err[:, mine], v_ref[...])
+    part = dot_cols(tag_err[:, other], v_ref[...])
     send_ref[...] = part.astype(BF16)
 
 
@@ -84,6 +84,51 @@
     )
     keep_ref[...] = own_ref[mine, :] + arrived_ref[mine, :].astype(F32)
     send_ref[...] = (own_ref[other, :] + arrived_ref[other, :].astype(F32)).astype(BF16)
+
+
+def item_kernel(tag_ref, v_hbm, pieces_hbm, out_ref, old_ref, pieces_ref, sems):
+    count, size = pieces_ref.shape[:2]
+    group = count // 4
+    start = pl.multiple_of(tag_ref[0] * size, size)
+    copies = [
+        pltpu.make_async_copy(
+            pieces_hbm.at[pl.ds(g * group, group)], pieces_ref.at[pl.ds(g * group, group)], sems.at[g]
+        )
+        for g in range(4)
+    ]
+    copies.append(pltpu.make_async_copy(v_hbm.at[pl.ds(start, size)], old_ref, sems.at[4]))
+    for copy in copies:
+        copy.start()
+    total = jnp.zeros(out_ref.shape, F32)
+    for g in range(4):
+        copies[g].wait()
+        for k in range(g * group, (g + 1) * group):
+            total += pieces_ref[k].astype(F32)
+    copies[4].wait()
+    old = old_ref[...].astype(F32)
+    out_ref[...] = (old - 0.04 * (total + 0.05 * old)).astype(BF16)
+
+
+def spread_kernel(shard_ref, out_hbm, sems):
+    copies = [
+        pltpu.make_async_copy(shard_ref, out_hbm.at[k], sems.at[k])
+        for k in range(out_hbm.shape[0])
+    ]
+    for copy in copies:
+        copy.start()
+    for copy in copies:
+        copy.wait()
+
+
+def place_kernel(in_ref, out_ref, sems):
+    copies = [
+        pltpu.make_async_copy(in_ref.at[k], out_ref.at[k], sems.at[k])
+        for k in range(out_ref.shape[0])
+    ]
+    for copy in copies:
+        copy.start()
+    for copy in copies:
+        copy.wait()
 
 
 def whole():
@@ -114,12 +159,10 @@
         scratch_shapes=[pltpu.SMEM(a.shape, a.dtype) for a in (xt, rt)]
         + [pltpu.VMEM(a.shape, BF16) for a in (u, v, w, r, x)]
         + [
-            pltpu.VMEM((items, users), BF16),
             pltpu.VMEM((items, tags), BF16),
-            pltpu.VMEM((tags, items), BF16),
             pltpu.SemaphoreType.DMA((7,)),
         ],
-        compiler_params=pltpu.CompilerParams(vmem_limit_bytes=24 << 20),
+        compiler_params=pltpu.CompilerParams(vmem_limit_bytes=14 << 20),
         cost_estimate=pl.CostEstimate(flops=3 << 30, bytes_accessed=6 << 20, transcendentals=0),
     )(rc, core, *(pltpu.with_memory_space_constraint(a, pltpu.HBM) for a in (xt, rt, u, v, w, r, x)))
 
@@ -130,7 +173,7 @@
         out_shape=jax.ShapeDtypeStruct(u.shape, BF16),
         in_specs=[whole()] * 3,
         out_specs=whole(),
-        compiler_params=pltpu.CompilerParams(vmem_limit_bytes=16 << 20),
+        compiler_params=pltpu.CompilerParams(vmem_limit_bytes=6 << 20),
         cost_estimate=pl.CostEstimate(flops=1 << 30, bytes_accessed=4 << 20, transcendentals=0),
     )(err, u, v)
 
@@ -150,6 +193,47 @@
     )(bit, own, arrived)
 
 
+def updated_items(tag, v, pieces):
+    count, size, rank = pieces.shape
+    return pl.pallas_call(
+        item_kernel,
+        out_shape=jax.ShapeDtypeStruct((size, rank), BF16),
+        in_specs=[scalars(), in_hbm(), in_hbm()],
+        out_specs=whole(),
+        scratch_shapes=[
+            pltpu.VMEM((size, rank), BF16),
+            pltpu.VMEM(pieces.shape, BF16),
+            pltpu.SemaphoreType.DMA((5,)),
+        ],
+        compiler_params=pltpu.CompilerParams(vmem_limit_bytes=4 << 20),
+        cost_estimate=pl.CostEstimate(flops=1 << 19, bytes_accessed=1 << 20, transcendentals=0),
+    )(tag, *(pltpu.with_memory_space_constraint(a, pltpu.HBM) for a in (v, pieces)))
+
+
+def spread(shard, count):
+    return pl.pallas_call(
+        spread_kernel,
+        out_shape=jax.ShapeDtypeStruct((count,) + shard.shape, BF16),
+        in_specs=[whole()],
+        out_specs=in_hbm(),
+        scratch_shapes=[pltpu.SemaphoreType.DMA((count,))],
+        compiler_params=pltpu.CompilerParams(vmem_limit_bytes=2 << 20),
+        cost_estimate=pl.CostEstimate(flops=0, bytes_accessed=1 << 20, transcendentals=0),
+    )(shard)
+
+
+def placed_items(pieces):
+    return pl.pallas_call(
+        place_kernel,
+        out_shape=jax.ShapeDtypeStruct(pieces.shape, BF16),
+        in_specs=[pl.BlockSpec(memory_space=pl.ANY)],
+        out_specs=in_hbm(),
+        scratch_shapes=[pltpu.SemaphoreType.DMA((pieces.shape[0],))],
+        compiler_params=pltpu.CompilerParams(vmem_limit_bytes=2 << 20),
+        cost_estimate=pl.CostEstimate(flops=0, bytes_accessed=2 << 20, transcendentals=0),
+    )(pieces)
+
+
 def exchanged(pieces, axis):
     return lax.all_to_all(pieces, axis, 0, 0)
 
@@ -199,16 +283,14 @@
         rating_tiles.T, rating_counts, tag_tiles.T, core[None], u, v, w, ratings, tag_values
     )
     item_pieces = exchanged(item_part.reshape(n_tag, -1, rank), "tag")
+    new_users = updated_users(err, u, v)
     tag_total = tag_sum_in_plane(tag_send, tag_own, x_hi)
-    item_pieces, _ = lax.optimization_barrier((item_pieces, tag_total))
-    shard = part_of(v, lax.axis_index("tag"), v.shape[0] // n_tag)
-    shard = updated(shard, jnp.sum(item_pieces.astype(F32), axis=0))
+    item_pieces, _, _ = lax.optimization_barrier((item_pieces, tag_total, new_users))
+    shard = updated_items(lax.axis_index("tag")[None], v, item_pieces)
     shard = lax.ppermute(shard, "rot", [(i, (i + 1) % n_rot) for i in range(n_rot)])
     tag_total = added(tag_total, 8)
-    shard, err, _ = lax.optimization_barrier((shard, err, tag_total))
-    new_users = updated_users(err, u, v)
-    copies = jnp.broadcast_to(shard, (n_tag,) + shard.shape)
-    rotated_items = exchanged(copies, "tag").reshape(v.shape)
+    shard, _ = lax.optimization_barrier((shard, tag_total))
+    rotated_items = placed_items(exchanged(spread(shard, n_tag), "tag")).reshape(v.shape)
     new_tags = new_tag_rows(added(tag_total, 16), w, core, x_hi)
     return (new_users, rotated_items, new_tags)
 

time: 99.9 us -> 98.8 us (0.989)
  Pallas kernels: 7.14 us -> 10.5 us
  local copies, waits for them, and re-layouts: 3.35 us -> 0.01 us
  other arithmetic: 3.57 us -> 2.16 us
    pallas_call x0 -> x3, Pallas kernels: none -> 3.47 us  [the longest x1 1.3 us: updated_items(): pl.pallas_call(item_kernel, out_shape=jax.ShapeDtypeStruct((size, rank),...]
    unnamed x5 -> x4, local copies, waits for them, and re-layouts: 2.27 us -> 0.01 us
    all_to_all x2, starting transfers between devices: 16.3 us -> 18.2 us  [exchanged(): return lax.all_to_all(pieces, axis, 0, 0)]
    reduce_sum x1 -> x0, other arithmetic: 1.38 us -> none  [on_device(): shard = updated(shard, jnp.sum(item_pieces.astype(F32), axis=0))]
    broadcast_in_dim x1 -> x0, local copies, waits for them, and re-layouts: 1.07 us -> none  [on_device(): copies = jnp.broadcast_to(shard, (n_tag,) + shard.shape)]
  transfers between devices with their start and end apart: 10 -> 10, of which waited for: 8 -> 7; matrix products, arithmetic and copies ran while one was open for 4% -> 2% of each run, Pallas kernels for 2% -> 3%
where the time goes in v6:
time: 98.8 us; the launch traced here: 98.2 us
  starting transfers between devices  56.4 us (57%)
  waiting for transfers between devices  27.7 us (28%)
  Pallas kernels  10.5 us (11%)
  other arithmetic  2.16 us (2%)
  between operations  1.46 us (1%)
    ppermute x7, starting transfers between devices, swapped(): return lax.ppermute(block, 'rot', [(i, i ^ mask) for i in range(n)])  31 us
    ppermute x7, waiting for transfers between devices, swapped(): return lax.ppermute(block, 'rot', [(i, i ^ mask) for i in range(n)])  26.4 us
    all_to_all x2, starting transfers between devices, exchanged(): return lax.all_to_all(pieces, axis, 0, 0)  18.2 us
    ppermute x1, starting transfers between devices, on_device(): lax.ppermute(shard, 'rot', [(i, (i + 1) % n_rot) for i in range(n_rot)])  7.23 us
    pallas_call x1, Pallas kernels, partials(): pl.pallas_call(grads_kernel, out_shape=(jax.ShapeDtypeStruct((items, rank...  5.43 us
  transfers between devices with their start and end apart: 10, of which 7 were waited for; matrix products, arithmetic and copies ran while one was open for 2% of the time, Pallas kernels for 3%

profile of v6, /device:TPU:15, one launch (start us, length us, event | category | flops | bytes accessed | tf_op | source)
XLA Modules:
  0.0 98.2 jit_solution(15232827770953144438)
XLA Ops:
  1.3 5.4 %shard_map.103 = (bf16[1024,512]{1,0:T(8,128)(2,1)}, bf16[256,512]{1,0:T(8,128)(2,1)S(1)}, f32[256,512]{1,0:T(8,128)S(1)}, bf16[512,1024]{1,0:T(8,128)(2,1)S(1)}) custom-call(s32[1]{0:T(128)S(6)} %copy.11.rc_ref, s32[1]{0:T(128)} %bitcast.core_ref, s32[2,16]{1,0:T(2,128)} %bitcast.8, s32[2,16]{1,0:T(2,128)} %bitcast.9, bf16[512,512]{1,0:T(8,128)(2,1)} %u_ref.1, ...), custom_call_target="tpu_custom_call" | custom-call | flops 3221225472 | bytes 6291456 | tf_op jit(solution)/shard_map/pallas_call | solution.py:149
  6.7 11.2 %all-to-all-start = ((bf16[16,64,512]{2,1,0:T(8,128)(2,1)}), bf16[16,64,512]{2,1,0:T(8,128)(2,1)}, u32[]{:S(2)}, u32[]{:S(2)}) async-start(bf16[16,64,512]{2,1,0:T(8,128)(2,1)} %bitcast.4), calls=%async_computation | async-start | bytes 2097152 | tf_op jit(solution)/shard_map/all_to_all | solution.py:238
  18.0 3.1 %collective-permute-start = (bf16[256,512]{1,0:T(8,128)(2,1)S(1)}, bf16[256,512]{1,0:T(8,128)(2,1)S(1)}, u32[]{:S(2)}, u32[]{:S(2)}) collective-permute-start(bf16[256,512]{1,0:T(8,128)(2,1)S(1)} %get-tuple-element.14), channel_id=1, source_target_pairs={{0,16},{16,0},{32,48},{48,32},{64,80},{80,64},{96,112},{112,96},{1... | collective-permute-start | bytes 786440 | tf_op jit(solution)/shard_map/ppermute | solution.py:252
  21.1 1.1 %collective-permute-done.arrived_ref = bf16[256,512]{1,0:T(8,128)(2,1)S(1)} collective-permute-done((bf16[256,512]{1,0:T(8,128)(2,1)S(1)}, bf16[256,512]{1,0:T(8,128)(2,1)S(1)}, u32[]{:S(2)}, u32[]{:S(2)}) %collective-permute-start) | collective-permute-done | bytes 262176 | tf_op jit(solution)/shard_map/ppermute | solution.py:252
  22.2 0.0 copy-start
  22.3 3.2 %collective-permute-start.1 = (bf16[128,512]{1,0:T(8,128)(2,1)S(1)}, bf16[128,512]{1,0:T(8,128)(2,1)S(1)}, u32[]{:S(2)}, u32[]{:S(2)}) collective-permute-start(bf16[128,512]{1,0:T(8,128)(2,1)S(1)} %get-tuple-element.16), channel_id=1, source_target_pairs={{0,32},{16,48},{32,0},{48,16},{64,96},{80,112},{96,64},{112,80},{1... | collective-permute-start | bytes 393224 | tf_op jit(solution)/shard_map/ppermute | solution.py:252
  25.5 5.6 %collective-permute-done.1 = bf16[128,512]{1,0:T(8,128)(2,1)S(1)} collective-permute-done((bf16[128,512]{1,0:T(8,128)(2,1)S(1)}, bf16[128,512]{1,0:T(8,128)(2,1)S(1)}, u32[]{:S(2)}, u32[]{:S(2)}) %collective-permute-start.1) | collective-permute-done | bytes 131104 | tf_op jit(solution)/shard_map/ppermute | solution.py:252
  31.1 0.0 copy-start.1
  31.1 2.2 %collective-permute-start.2 = (bf16[128,512]{1,0:T(8,128)(2,1)S(1)}, bf16[128,512]{1,0:T(8,128)(2,1)S(1)}, u32[]{:S(2)}, u32[]{:S(2)}) collective-permute-start(bf16[128,512]{1,0:T(8,128)(2,1)S(1)} %fusion.3), channel_id=1, source_target_pairs={{0,64},{16,80},{32,96},{48,112},{64,0},{80,16},{96,32},{112,48},{1... | collective-permute-start | bytes 393224 | tf_op jit(solution)/shard_map/ppermute | solution.py:252
  33.3 4.0 %collective-permute-done.2 = bf16[128,512]{1,0:T(8,128)(2,1)S(1)} collective-permute-done((bf16[128,512]{1,0:T(8,128)(2,1)S(1)}, bf16[128,512]{1,0:T(8,128)(2,1)S(1)}, u32[]{:S(2)}, u32[]{:S(2)}) %collective-permute-start.2) | collective-permute-done | bytes 131104 | tf_op jit(solution)/shard_map/ppermute | solution.py:252
  37.3 0.1 reduce-precision_convert_fusion.1
  37.4 4.2 %collective-permute-start.4 = (bf16[128,512]{1,0:T(8,128)(2,1)S(1)}, bf16[128,512]{1,0:T(8,128)(2,1)S(1)}, u32[]{:S(2)}, u32[]{:S(2)}) collective-permute-start(bf16[128,512]{1,0:T(8,128)(2,1)S(1)} %get-tuple-element.21), channel_id=1, source_target_pairs={{0,128},{16,144},{32,160},{48,176},{64,192},{80,208},{96,224},{112... | collective-permute-start | bytes 393224 | tf_op jit(solution)/shard_map/ppermute | solution.py:252
  41.6 0.0 copy-done
  41.6 0.0 copy-done.1
  41.7 1.6 %shard_map.104 = bf16[512,512]{1,0:T(8,128)(2,1)} custom-call(bf16[512,1024]{1,0:T(8,128)(2,1)S(1)} %get-tuple-element.11.err_ref, bf16[512,512]{1,0:T(8,128)(2,1)S(1)} %copy-done.1, bf16[1024,512]{1,0:T(8,128)(2,1)S(1)} %copy-done), custom_call_target="tpu_custom_call" | custom-call | flops 1073741824 | bytes 4194304 | tf_op jit(solution)/shard_map/pallas_call | solution.py:171
  43.2 0.0 all-to-all-done.pieces_hbm
  43.2 1.3 %shard_map.106 = bf16[64,512]{1,0:T(8,128)(2,1)S(1)} custom-call(s32[1]{0:T(128)} %bitcast.3.tag_ref, bf16[1024,512]{1,0:T(8,128)(2,1)} %v_hbm.3, bf16[16,64,512]{2,1,0:T(8,128)(2,1)} %all-to-all-done.pieces_hbm), custom_call_target="tpu_custom_call" | custom-call | flops 524288 | bytes 1048576 | tf_op jit(solution)/shard_map/pallas_call | solution.py:198
  44.5 7.2 %collective-permute-start.3 = (bf16[64,512]{1,0:T(8,128)(2,1)S(1)}, bf16[64,512]{1,0:T(8,128)(2,1)S(1)}, u32[]{:S(2)}, u32[]{:S(2)}) collective-permute-start(bf16[64,512]{1,0:T(8,128)(2,1)S(1)} %shard_map.106), channel_id=1, source_target_pairs={{0,16},{16,32},{32,48},{48,64},{64,80},{80,96},{96,112},{112,128},... | collective-permute-start | bytes 196616 | tf_op jit(solution)/shard_map/ppermute | solution.py:290
  51.8 0.0 collective-permute-done.4
  51.8 1.3 %collective-permute-done.3.shard_ref = bf16[64,512]{1,0:T(8,128)(2,1)S(1)} collective-permute-done((bf16[64,512]{1,0:T(8,128)(2,1)S(1)}, bf16[64,512]{1,0:T(8,128)(2,1)S(1)}, u32[]{:S(2)}, u32[]{:S(2)}) %collective-permute-start.3) | collective-permute-done | bytes 65568 | tf_op jit(solution)/shard_map/ppermute | solution.py:290
  53.1 1.1 %shard_map.107 = bf16[16,64,512]{2,1,0:T(8,128)(2,1)} custom-call(bf16[64,512]{1,0:T(8,128)(2,1)S(1)} %collective-permute-done.3.shard_ref), custom_call_target="tpu_custom_call" | custom-call | bytes 1048576 | tf_op jit(solution)/shard_map/pallas_call | solution.py:214
  54.2 7.0 %all-to-all-start.1 = ((bf16[16,64,512]{2,1,0:T(8,128)(2,1)}), bf16[16,64,512]{2,1,0:T(8,128)(2,1)S(1)}, u32[]{:S(2)}, u32[]{:S(2)}) async-start(bf16[16,64,512]{2,1,0:T(8,128)(2,1)} %shard_map.107), calls=%async_computation.1 | async-start | bytes 2097152 | tf_op jit(solution)/shard_map/all_to_all | solution.py:238
  61.1 5.0 %collective-permute-start.5 = (bf16[128,512]{1,0:T(8,128)(2,1)S(1)}, bf16[128,512]{1,0:T(8,128)(2,1)S(1)}, u32[]{:S(2)}, u32[]{:S(2)}) collective-permute-start(bf16[128,512]{1,0:T(8,128)(2,1)S(1)} %get-tuple-element.19), channel_id=1, source_target_pairs={{0,256},{16,272},{32,288},{48,304},{64,320},{80,336},{96,352},{112... | collective-permute-start | bytes 393224 | tf_op jit(solution)/shard_map/ppermute | solution.py:252
  66.2 4.7 %collective-permute-done.5 = bf16[128,512]{1,0:T(8,128)(2,1)S(1)} collective-permute-done((bf16[128,512]{1,0:T(8,128)(2,1)S(1)}, bf16[128,512]{1,0:T(8,128)(2,1)S(1)}, u32[]{:S(2)}, u32[]{:S(2)}) %collective-permute-start.5) | collective-permute-done | bytes 131104 | tf_op jit(solution)/shard_map/ppermute | solution.py:252
  70.9 1.0 fusion.2
  71.8 10.0 %collective-permute-start.6 = (bf16[128,512]{1,0:T(8,128)(2,1)S(1)}, bf16[128,512]{1,0:T(8,128)(2,1)S(1)}, u32[]{:S(2)}, u32[]{:S(2)}) collective-permute-start(bf16[128,512]{1,0:T(8,128)(2,1)S(1)} %fusion.2), channel_id=1, source_target_pairs={{0,32},{16,48},{32,0},{48,16},{64,96},{80,112},{96,64},{112,80},{1... | collective-permute-start | bytes 393224 | tf_op jit(solution)/shard_map/ppermute | solution.py:252
  81.9 9.9 %collective-permute-done.6 = bf16[128,512]{1,0:T(8,128)(2,1)S(1)} collective-permute-done((bf16[128,512]{1,0:T(8,128)(2,1)S(1)}, bf16[128,512]{1,0:T(8,128)(2,1)S(1)}, u32[]{:S(2)}, u32[]{:S(2)}) %collective-permute-start.6) | collective-permute-done | bytes 131104 | tf_op jit(solution)/shard_map/ppermute | solution.py:252
  91.8 0.1 maximum_select_fusion.1
  91.8 3.2 %collective-permute-start.7 = (bf16[256,512]{1,0:T(8,128)(2,1)S(1)}, bf16[256,512]{1,0:T(8,128)(2,1)S(1)}, u32[]{:S(2)}, u32[]{:S(2)}) collective-permute-start(bf16[256,512]{1,0:T(8,128)(2,1)S(1)} %maximum_select_fusion.1), channel_id=1, source_target_pairs={{0,16},{16,0},{32,48},{48,32},{64,80},{80,64},{96,112},{112,96},{1... | collective-permute-start | bytes 786440 | tf_op jit(solution)/shard_map/ppermute | solution.py:252
  95.0 1.1 %collective-permute-done.7 = bf16[256,512]{1,0:T(8,128)(2,1)S(1)} collective-permute-done((bf16[256,512]{1,0:T(8,128)(2,1)S(1)}, bf16[256,512]{1,0:T(8,128)(2,1)S(1)}, u32[]{:S(2)}, u32[]{:S(2)}) %collective-permute-start.7) | collective-permute-done | bytes 262176 | tf_op jit(solution)/shard_map/ppermute | solution.py:252
  96.1 1.0 %maximum_select_fusion = bf16[512,512]{1,0:T(8,128)(2,1)} fusion(bf16[256,512]{1,0:T(8,128)(2,1)S(1)} %collective-permute-done.7, bf16[256,512]{1,0:T(8,128)(2,1)S(1)} %maximum_select_fusion.1, pred[]{:T(512)S(6)} %eq.6), kind=kLoop, calls=%fused_computation | loop fusion | flops 2359296 | bytes 1048577 | tf_op jit(solution)/shard_map/jit(_where)/select_n | solution.py:256
  97.1 0.0 all-to-all-done.1.in_ref
  97.1 1.1 %shard_map.108 = bf16[16,64,512]{2,1,0:T(8,128)(2,1)} custom-call(bf16[16,64,512]{2,1,0:T(8,128)(2,1)S(1)} %all-to-all-done.1.in_ref), custom_call_target="tpu_custom_call" | custom-call | bytes 2097152 | tf_op jit(solution)/shard_map/pallas_call | solution.py:226
  (3 shorter events, 0.1 us)
Async XLA Ops:
  6.7 36.5 %all-to-all-start = ((bf16[16,64,512]{2,1,0:T(8,128)(2,1)}), bf16[16,64,512]{2,1,0:T(8,128)(2,1)}, u32[]{:S(2)}, u32[]{:S(2)}) async-start(bf16[16,64,512]{2,1,0:T(8,128)(2,1)} %bitcast.4), calls=%async_computation | async-start | bytes 2097152 | tf_op jit(solution)/shard_map/all_to_all | solution.py:238
  18.0 4.3 %collective-permute-start = (bf16[256,512]{1,0:T(8,128)(2,1)S(1)}, bf16[256,512]{1,0:T(8,128)(2,1)S(1)}, u32[]{:S(2)}, u32[]{:S(2)}) collective-permute-start(bf16[256,512]{1,0:T(8,128)(2,1)S(1)} %get-tuple-element.14), channel_id=1, source_target_pairs={{0,16},{16,0},{32,48},{48,32},{64,80},{80,64},{96,112},{112,96},{1... | collective-permute-start | bytes 786440 | tf_op jit(solution)/shard_map/ppermute | solution.py:252
  22.2 19.4 %copy-start = (bf16[1024,512]{1,0:T(8,128)(2,1)S(1)}, bf16[1024,512]{1,0:T(8,128)(2,1)}, u32[]{:S(2)}) copy-start(bf16[1024,512]{1,0:T(8,128)(2,1)} %v_hbm.3) | copy-start | bytes 3145732
  22.3 8.8 %collective-permute-start.1 = (bf16[128,512]{1,0:T(8,128)(2,1)S(1)}, bf16[128,512]{1,0:T(8,128)(2,1)S(1)}, u32[]{:S(2)}, u32[]{:S(2)}) collective-permute-start(bf16[128,512]{1,0:T(8,128)(2,1)S(1)} %get-tuple-element.16), channel_id=1, source_target_pairs={{0,32},{16,48},{32,0},{48,16},{64,96},{80,112},{96,64},{112,80},{1... | collective-permute-start | bytes 393224 | tf_op jit(solution)/shard_map/ppermute | solution.py:252
  31.1 10.6 %copy-start.1 = (bf16[512,512]{1,0:T(8,128)(2,1)S(1)}, bf16[512,512]{1,0:T(8,128)(2,1)}, u32[]{:S(2)}) copy-start(bf16[512,512]{1,0:T(8,128)(2,1)} %u_ref.1) | copy-start | bytes 1572868
  31.1 6.2 %collective-permute-start.2 = (bf16[128,512]{1,0:T(8,128)(2,1)S(1)}, bf16[128,512]{1,0:T(8,128)(2,1)S(1)}, u32[]{:S(2)}, u32[]{:S(2)}) collective-permute-start(bf16[128,512]{1,0:T(8,128)(2,1)S(1)} %fusion.3), channel_id=1, source_target_pairs={{0,64},{16,80},{32,96},{48,112},{64,0},{80,16},{96,32},{112,48},{1... | collective-permute-start | bytes 393224 | tf_op jit(solution)/shard_map/ppermute | solution.py:252
  37.4 14.4 %collective-permute-start.4 = (bf16[128,512]{1,0:T(8,128)(2,1)S(1)}, bf16[128,512]{1,0:T(8,128)(2,1)S(1)}, u32[]{:S(2)}, u32[]{:S(2)}) collective-permute-start(bf16[128,512]{1,0:T(8,128)(2,1)S(1)} %get-tuple-element.21), channel_id=1, source_target_pairs={{0,128},{16,144},{32,160},{48,176},{64,192},{80,208},{96,224},{112... | collective-permute-start | bytes 393224 | tf_op jit(solution)/shard_map/ppermute | solution.py:252
  44.5 8.5 %collective-permute-start.3 = (bf16[64,512]{1,0:T(8,128)(2,1)S(1)}, bf16[64,512]{1,0:T(8,128)(2,1)S(1)}, u32[]{:S(2)}, u32[]{:S(2)}) collective-permute-start(bf16[64,512]{1,0:T(8,128)(2,1)S(1)} %shard_map.106), channel_id=1, source_target_pairs={{0,16},{16,32},{32,48},{48,64},{64,80},{80,96},{96,112},{112,128},... | collective-permute-start | bytes 196616 | tf_op jit(solution)/shard_map/ppermute | solution.py:290
  54.2 43.0 %all-to-all-start.1 = ((bf16[16,64,512]{2,1,0:T(8,128)(2,1)}), bf16[16,64,512]{2,1,0:T(8,128)(2,1)S(1)}, u32[]{:S(2)}, u32[]{:S(2)}) async-start(bf16[16,64,512]{2,1,0:T(8,128)(2,1)} %shard_map.107), calls=%async_computation.1 | async-start | bytes 2097152 | tf_op jit(solution)/shard_map/all_to_all | solution.py:238
  61.1 9.7 %collective-permute-start.5 = (bf16[128,512]{1,0:T(8,128)(2,1)S(1)}, bf16[128,512]{1,0:T(8,128)(2,1)S(1)}, u32[]{:S(2)}, u32[]{:S(2)}) collective-permute-start(bf16[128,512]{1,0:T(8,128)(2,1)S(1)} %get-tuple-element.19), channel_id=1, source_target_pairs={{0,256},{16,272},{32,288},{48,304},{64,320},{80,336},{96,352},{112... | collective-permute-start | bytes 393224 | tf_op jit(solution)/shard_map/ppermute | solution.py:252
  71.8 19.9 %collective-permute-start.6 = (bf16[128,512]{1,0:T(8,128)(2,1)S(1)}, bf16[128,512]{1,0:T(8,128)(2,1)S(1)}, u32[]{:S(2)}, u32[]{:S(2)}) collective-permute-start(bf16[128,512]{1,0:T(8,128)(2,1)S(1)} %fusion.2), channel_id=1, source_target_pairs={{0,32},{16,48},{32,0},{48,16},{64,96},{80,112},{96,64},{112,80},{1... | collective-permute-start | bytes 393224 | tf_op jit(solution)/shard_map/ppermute | solution.py:252
  91.8 4.3 %collective-permute-start.7 = (bf16[256,512]{1,0:T(8,128)(2,1)S(1)}, bf16[256,512]{1,0:T(8,128)(2,1)S(1)}, u32[]{:S(2)}, u32[]{:S(2)}) collective-permute-start(bf16[256,512]{1,0:T(8,128)(2,1)S(1)} %maximum_select_fusion.1), channel_id=1, source_target_pairs={{0,16},{16,0},{32,48},{48,32},{64,80},{80,64},{96,112},{112,96},{1... | collective-permute-start | bytes 786440 | tf_op jit(solution)/shard_map/ppermute | solution.py:252

commit v7 on v6

--- a/solution.py
+++ b/solution.py
@@ -263,14 +263,14 @@
     return own + swapped(own.astype(BF16), mask).astype(F32)
 
 
-def tag_sum_in_plane(send, own, x_hi):
-    own, send = split_sum(x_hi[None], own, swapped(send, 1))
-    return added(own + swapped(send, 2).astype(F32), 4)
-
-
-def new_tag_rows(total, w, core, x_hi):
-    shard = updated(part_of(w, core * 2 + x_hi, total.shape[0]), total)
-    half = joined(shard, swapped(shard, 2), x_hi)
+def tag_sum_nearby(send, own, y_bit):
+    own, send = split_sum(y_bit[None], own, swapped(send, 1))
+    return added(own + swapped(send, 4).astype(F32), 2)
+
+
+def new_tag_rows(total, w, core, y_bit):
+    shard = updated(part_of(w, core * 2 + y_bit, total.shape[0]), total)
+    half = joined(shard, swapped(shard, 4), y_bit)
     return joined(half, swapped(half, 1), core)
 
 
@@ -278,20 +278,20 @@
     rank = u.shape[1]
     n_rot, n_tag = lax.axis_size("rot"), lax.axis_size("tag")
     rot = lax.axis_index("rot")
-    core, x_hi = rot & 1, (rot >> 1) & 1
+    core, y_bit = rot & 1, (rot >> 2) & 1
     item_part, tag_send, tag_own, err = partials(
         rating_tiles.T, rating_counts, tag_tiles.T, core[None], u, v, w, ratings, tag_values
     )
     item_pieces = exchanged(item_part.reshape(n_tag, -1, rank), "tag")
     new_users = updated_users(err, u, v)
-    tag_total = tag_sum_in_plane(tag_send, tag_own, x_hi)
+    tag_total = tag_sum_nearby(tag_send, tag_own, y_bit)
     item_pieces, _, _ = lax.optimization_barrier((item_pieces, tag_total, new_users))
     shard = updated_items(lax.axis_index("tag")[None], v, item_pieces)
     shard = lax.ppermute(shard, "rot", [(i, (i + 1) % n_rot) for i in range(n_rot)])
     tag_total = added(tag_total, 8)
     shard, _ = lax.optimization_barrier((shard, tag_total))
     rotated_items = placed_items(exchanged(spread(shard, n_tag), "tag")).reshape(v.shape)
-    new_tags = new_tag_rows(added(tag_total, 16), w, core, x_hi)
+    new_tags = new_tag_rows(added(tag_total, 16), w, core, y_bit)
     return (new_users, rotated_items, new_tags)
 
 

time: 98.8 us -> 97.1 us (0.983)
  the two profiles are of different devices: /device:TPU:15 before, /device:TPU:1 now
where the time goes in v7:
time: 97.1 us; the launch traced here: 96.2 us
  starting transfers between devices  59.9 us (62%)
  waiting for transfers between devices  22.1 us (23%)
  Pallas kernels  10.5 us (11%)
  other arithmetic  2.16 us (2%)
  between operations  1.47 us (2%)
    ppermute x7, starting transfers between devices, swapped(): return lax.ppermute(block, 'rot', [(i, i ^ mask) for i in range(n)])  33.1 us
    ppermute x7, waiting for transfers between devices, swapped(): return lax.ppermute(block, 'rot', [(i, i ^ mask) for i in range(n)])  20.8 us
    all_to_all x2, starting transfers between devices, exchanged(): return lax.all_to_all(pieces, axis, 0, 0)  18.6 us
    ppermute x1, starting transfers between devices, on_device(): lax.ppermute(shard, 'rot', [(i, (i + 1) % n_rot) for i in range(n_rot)])  8.19 us
    pallas_call x1, Pallas kernels, partials(): pl.pallas_call(grads_kernel, out_shape=(jax.ShapeDtypeStruct((items, rank...  5.44 us
  transfers between devices with their start and end apart: 10, of which 7 were waited for; matrix products, arithmetic and copies ran while one was open for 2% of the time, Pallas kernels for 3%

profile of v7, /device:TPU:1, one launch (start us, length us, event | category | flops | bytes accessed | tf_op | source)
XLA Modules:
  0.0 96.2 jit_solution(17901641712471610928)
XLA Ops:
  1.3 5.4 %shard_map.103 = (bf16[1024,512]{1,0:T(8,128)(2,1)}, bf16[256,512]{1,0:T(8,128)(2,1)S(1)}, f32[256,512]{1,0:T(8,128)S(1)}, bf16[512,1024]{1,0:T(8,128)(2,1)S(1)}) custom-call(s32[1]{0:T(128)S(6)} %copy.11.rc_ref, s32[1]{0:T(128)} %bitcast.core_ref, s32[2,16]{1,0:T(2,128)} %bitcast.8, s32[2,16]{1,0:T(2,128)} %bitcast.9, bf16[512,512]{1,0:T(8,128)(2,1)} %u_ref.1, ...), custom_call_target="tpu_custom_call" | custom-call | flops 3221225472 | bytes 6291456 | tf_op jit(solution)/shard_map/pallas_call | solution.py:149
  6.7 12.0 %all-to-all-start = ((bf16[16,64,512]{2,1,0:T(8,128)(2,1)}), bf16[16,64,512]{2,1,0:T(8,128)(2,1)}, u32[]{:S(2)}, u32[]{:S(2)}) async-start(bf16[16,64,512]{2,1,0:T(8,128)(2,1)} %bitcast.4), calls=%async_computation | async-start | bytes 2097152 | tf_op jit(solution)/shard_map/all_to_all | solution.py:238
  18.7 2.9 %collective-permute-start = (bf16[256,512]{1,0:T(8,128)(2,1)S(1)}, bf16[256,512]{1,0:T(8,128)(2,1)S(1)}, u32[]{:S(2)}, u32[]{:S(2)}) collective-permute-start(bf16[256,512]{1,0:T(8,128)(2,1)S(1)} %get-tuple-element.14), channel_id=1, source_target_pairs={{0,16},{16,0},{32,48},{48,32},{64,80},{80,64},{96,112},{112,96},{1... | collective-permute-start | bytes 786440 | tf_op jit(solution)/shard_map/ppermute | solution.py:252
  21.6 1.1 %collective-permute-done.arrived_ref = bf16[256,512]{1,0:T(8,128)(2,1)S(1)} collective-permute-done((bf16[256,512]{1,0:T(8,128)(2,1)S(1)}, bf16[256,512]{1,0:T(8,128)(2,1)S(1)}, u32[]{:S(2)}, u32[]{:S(2)}) %collective-permute-start) | collective-permute-done | bytes 262176 | tf_op jit(solution)/shard_map/ppermute | solution.py:252
  22.7 0.0 copy-start
  22.8 3.3 %collective-permute-start.1 = (bf16[128,512]{1,0:T(8,128)(2,1)S(1)}, bf16[128,512]{1,0:T(8,128)(2,1)S(1)}, u32[]{:S(2)}, u32[]{:S(2)}) collective-permute-start(bf16[128,512]{1,0:T(8,128)(2,1)S(1)} %get-tuple-element.16), channel_id=1, source_target_pairs={{0,64},{16,80},{32,96},{48,112},{64,0},{80,16},{96,32},{112,48},{1... | collective-permute-start | bytes 393224 | tf_op jit(solution)/shard_map/ppermute | solution.py:252
  26.1 3.5 %collective-permute-done.1 = bf16[128,512]{1,0:T(8,128)(2,1)S(1)} collective-permute-done((bf16[128,512]{1,0:T(8,128)(2,1)S(1)}, bf16[128,512]{1,0:T(8,128)(2,1)S(1)}, u32[]{:S(2)}, u32[]{:S(2)}) %collective-permute-start.1) | collective-permute-done | bytes 131104 | tf_op jit(solution)/shard_map/ppermute | solution.py:252
  29.6 0.0 copy-start.1
  29.6 4.5 %collective-permute-start.2 = (bf16[128,512]{1,0:T(8,128)(2,1)S(1)}, bf16[128,512]{1,0:T(8,128)(2,1)S(1)}, u32[]{:S(2)}, u32[]{:S(2)}) collective-permute-start(bf16[128,512]{1,0:T(8,128)(2,1)S(1)} %fusion.3), channel_id=1, source_target_pairs={{0,32},{16,48},{32,0},{48,16},{64,96},{80,112},{96,64},{112,80},{1... | collective-permute-start | bytes 393224 | tf_op jit(solution)/shard_map/ppermute | solution.py:252
  34.1 8.5 %collective-permute-done.2 = bf16[128,512]{1,0:T(8,128)(2,1)S(1)} collective-permute-done((bf16[128,512]{1,0:T(8,128)(2,1)S(1)}, bf16[128,512]{1,0:T(8,128)(2,1)S(1)}, u32[]{:S(2)}, u32[]{:S(2)}) %collective-permute-start.2) | collective-permute-done | bytes 131104 | tf_op jit(solution)/shard_map/ppermute | solution.py:252
  42.6 0.1 reduce-precision_convert_fusion.1
  42.7 4.2 %collective-permute-start.4 = (bf16[128,512]{1,0:T(8,128)(2,1)S(1)}, bf16[128,512]{1,0:T(8,128)(2,1)S(1)}, u32[]{:S(2)}, u32[]{:S(2)}) collective-permute-start(bf16[128,512]{1,0:T(8,128)(2,1)S(1)} %get-tuple-element.21), channel_id=1, source_target_pairs={{0,128},{16,144},{32,160},{48,176},{64,192},{80,208},{96,224},{112... | collective-permute-start | bytes 393224 | tf_op jit(solution)/shard_map/ppermute | solution.py:252
  46.9 0.0 copy-done
  46.9 0.0 copy-done.1
  46.9 1.6 %shard_map.104 = bf16[512,512]{1,0:T(8,128)(2,1)} custom-call(bf16[512,1024]{1,0:T(8,128)(2,1)S(1)} %get-tuple-element.11.err_ref, bf16[512,512]{1,0:T(8,128)(2,1)S(1)} %copy-done.1, bf16[1024,512]{1,0:T(8,128)(2,1)S(1)} %copy-done), custom_call_target="tpu_custom_call" | custom-call | flops 1073741824 | bytes 4194304 | tf_op jit(solution)/shard_map/pallas_call | solution.py:171
  48.5 0.0 all-to-all-done.pieces_hbm
  48.5 1.3 %shard_map.106 = bf16[64,512]{1,0:T(8,128)(2,1)S(1)} custom-call(s32[1]{0:T(128)} %bitcast.3.tag_ref, bf16[1024,512]{1,0:T(8,128)(2,1)} %v_hbm.3, bf16[16,64,512]{2,1,0:T(8,128)(2,1)} %all-to-all-done.pieces_hbm), custom_call_target="tpu_custom_call" | custom-call | flops 524288 | bytes 1048576 | tf_op jit(solution)/shard_map/pallas_call | solution.py:198
  49.8 8.2 %collective-permute-start.3 = (bf16[64,512]{1,0:T(8,128)(2,1)S(1)}, bf16[64,512]{1,0:T(8,128)(2,1)S(1)}, u32[]{:S(2)}, u32[]{:S(2)}) collective-permute-start(bf16[64,512]{1,0:T(8,128)(2,1)S(1)} %shard_map.106), channel_id=1, source_target_pairs={{0,16},{16,32},{32,48},{48,64},{64,80},{80,96},{96,112},{112,128},... | collective-permute-start | bytes 196616 | tf_op jit(solution)/shard_map/ppermute | solution.py:290
  58.0 0.0 collective-permute-done.4
  58.1 1.3 %collective-permute-done.3.shard_ref = bf16[64,512]{1,0:T(8,128)(2,1)S(1)} collective-permute-done((bf16[64,512]{1,0:T(8,128)(2,1)S(1)}, bf16[64,512]{1,0:T(8,128)(2,1)S(1)}, u32[]{:S(2)}, u32[]{:S(2)}) %collective-permute-start.3) | collective-permute-done | bytes 65568 | tf_op jit(solution)/shard_map/ppermute | solution.py:290
  59.3 1.1 %shard_map.107 = bf16[16,64,512]{2,1,0:T(8,128)(2,1)} custom-call(bf16[64,512]{1,0:T(8,128)(2,1)S(1)} %collective-permute-done.3.shard_ref), custom_call_target="tpu_custom_call" | custom-call | bytes 1048576 | tf_op jit(solution)/shard_map/pallas_call | solution.py:214
  60.4 6.7 %all-to-all-start.1 = ((bf16[16,64,512]{2,1,0:T(8,128)(2,1)}), bf16[16,64,512]{2,1,0:T(8,128)(2,1)S(1)}, u32[]{:S(2)}, u32[]{:S(2)}) async-start(bf16[16,64,512]{2,1,0:T(8,128)(2,1)} %shard_map.107), calls=%async_computation.1 | async-start | bytes 2097152 | tf_op jit(solution)/shard_map/all_to_all | solution.py:238
  67.1 5.7 %collective-permute-start.5 = (bf16[128,512]{1,0:T(8,128)(2,1)S(1)}, bf16[128,512]{1,0:T(8,128)(2,1)S(1)}, u32[]{:S(2)}, u32[]{:S(2)}) collective-permute-start(bf16[128,512]{1,0:T(8,128)(2,1)S(1)} %get-tuple-element.19), channel_id=1, source_target_pairs={{0,256},{16,272},{32,288},{48,304},{64,320},{80,336},{96,352},{112... | collective-permute-start | bytes 393224 | tf_op jit(solution)/shard_map/ppermute | solution.py:252
  72.8 3.9 %collective-permute-done.5 = bf16[128,512]{1,0:T(8,128)(2,1)S(1)} collective-permute-done((bf16[128,512]{1,0:T(8,128)(2,1)S(1)}, bf16[128,512]{1,0:T(8,128)(2,1)S(1)}, u32[]{:S(2)}, u32[]{:S(2)}) %collective-permute-start.5) | collective-permute-done | bytes 131104 | tf_op jit(solution)/shard_map/ppermute | solution.py:252
  76.7 1.0 %fusion.2 = bf16[128,512]{1,0:T(8,128)(2,1)S(1)} fusion(bf16[128,512]{1,0:T(8,128)(2,1)S(1)} %collective-permute-done.5, f32[128,512]{1,0:T(8,128)S(1)} %get-tuple-element.20, bf16[512,512]{1,0:T(8,128)(2,1)} %w_hbm.1, s32[]{:T(128)S(6)} %select_n.21), kind=kLoop, calls=%fused_computation.5 | loop fusion | flops 589824 | bytes 655364 | tf_op jit(solution)/shard_map/convert_element_type | solution.py:243
  77.7 4.4 %collective-permute-start.6 = (bf16[128,512]{1,0:T(8,128)(2,1)S(1)}, bf16[128,512]{1,0:T(8,128)(2,1)S(1)}, u32[]{:S(2)}, u32[]{:S(2)}) collective-permute-start(bf16[128,512]{1,0:T(8,128)(2,1)S(1)} %fusion.2), channel_id=1, source_target_pairs={{0,64},{16,80},{32,96},{48,112},{64,0},{80,16},{96,32},{112,48},{1... | collective-permute-start | bytes 393224 | tf_op jit(solution)/shard_map/ppermute | solution.py:252
  82.2 2.6 %collective-permute-done.6 = bf16[128,512]{1,0:T(8,128)(2,1)S(1)} collective-permute-done((bf16[128,512]{1,0:T(8,128)(2,1)S(1)}, bf16[128,512]{1,0:T(8,128)(2,1)S(1)}, u32[]{:S(2)}, u32[]{:S(2)}) %collective-permute-start.6) | collective-permute-done | bytes 131104 | tf_op jit(solution)/shard_map/ppermute | solution.py:252
  84.8 0.1 maximum_select_fusion.1
  84.9 8.1 %collective-permute-start.7 = (bf16[256,512]{1,0:T(8,128)(2,1)S(1)}, bf16[256,512]{1,0:T(8,128)(2,1)S(1)}, u32[]{:S(2)}, u32[]{:S(2)}) collective-permute-start(bf16[256,512]{1,0:T(8,128)(2,1)S(1)} %maximum_select_fusion.1), channel_id=1, source_target_pairs={{0,16},{16,0},{32,48},{48,32},{64,80},{80,64},{96,112},{112,96},{1... | collective-permute-start | bytes 786440 | tf_op jit(solution)/shard_map/ppermute | solution.py:252
  92.9 1.1 %collective-permute-done.7 = bf16[256,512]{1,0:T(8,128)(2,1)S(1)} collective-permute-done((bf16[256,512]{1,0:T(8,128)(2,1)S(1)}, bf16[256,512]{1,0:T(8,128)(2,1)S(1)}, u32[]{:S(2)}, u32[]{:S(2)}) %collective-permute-start.7) | collective-permute-done | bytes 262176 | tf_op jit(solution)/shard_map/ppermute | solution.py:252
  94.1 1.0 %maximum_select_fusion = bf16[512,512]{1,0:T(8,128)(2,1)} fusion(bf16[256,512]{1,0:T(8,128)(2,1)S(1)} %collective-permute-done.7, bf16[256,512]{1,0:T(8,128)(2,1)S(1)} %maximum_select_fusion.1, pred[]{:T(512)S(6)} %eq.6), kind=kLoop, calls=%fused_computation | loop fusion | flops 2359296 | bytes 1048577 | tf_op jit(solution)/shard_map/jit(_where)/select_n | solution.py:256
  95.1 0.0 all-to-all-done.1.in_ref
  95.1 1.1 %shard_map.108 = bf16[16,64,512]{2,1,0:T(8,128)(2,1)} custom-call(bf16[16,64,512]{2,1,0:T(8,128)(2,1)S(1)} %all-to-all-done.1.in_ref), custom_call_target="tpu_custom_call" | custom-call | bytes 2097152 | tf_op jit(solution)/shard_map/pallas_call | solution.py:226
  (3 shorter events, 0.1 us)
Async XLA Ops:
  6.7 41.8 %all-to-all-start = ((bf16[16,64,512]{2,1,0:T(8,128)(2,1)}), bf16[16,64,512]{2,1,0:T(8,128)(2,1)}, u32[]{:S(2)}, u32[]{:S(2)}) async-start(bf16[16,64,512]{2,1,0:T(8,128)(2,1)} %bitcast.4), calls=%async_computation | async-start | bytes 2097152 | tf_op jit(solution)/shard_map/all_to_all | solution.py:238
  18.7 4.0 %collective-permute-start = (bf16[256,512]{1,0:T(8,128)(2,1)S(1)}, bf16[256,512]{1,0:T(8,128)(2,1)S(1)}, u32[]{:S(2)}, u32[]{:S(2)}) collective-permute-start(bf16[256,512]{1,0:T(8,128)(2,1)S(1)} %get-tuple-element.14), channel_id=1, source_target_pairs={{0,16},{16,0},{32,48},{48,32},{64,80},{80,64},{96,112},{112,96},{1... | collective-permute-start | bytes 786440 | tf_op jit(solution)/shard_map/ppermute | solution.py:252
  22.7 24.2 %copy-start = (bf16[1024,512]{1,0:T(8,128)(2,1)S(1)}, bf16[1024,512]{1,0:T(8,128)(2,1)}, u32[]{:S(2)}) copy-start(bf16[1024,512]{1,0:T(8,128)(2,1)} %v_hbm.3) | copy-start | bytes 3145732
  22.8 6.8 %collective-permute-start.1 = (bf16[128,512]{1,0:T(8,128)(2,1)S(1)}, bf16[128,512]{1,0:T(8,128)(2,1)S(1)}, u32[]{:S(2)}, u32[]{:S(2)}) collective-permute-start(bf16[128,512]{1,0:T(8,128)(2,1)S(1)} %get-tuple-element.16), channel_id=1, source_target_pairs={{0,64},{16,80},{32,96},{48,112},{64,0},{80,16},{96,32},{112,48},{1... | collective-permute-start | bytes 393224 | tf_op jit(solution)/shard_map/ppermute | solution.py:252
  29.6 17.3 %copy-start.1 = (bf16[512,512]{1,0:T(8,128)(2,1)S(1)}, bf16[512,512]{1,0:T(8,128)(2,1)}, u32[]{:S(2)}) copy-start(bf16[512,512]{1,0:T(8,128)(2,1)} %u_ref.1) | copy-start | bytes 1572868
  29.6 13.0 %collective-permute-start.2 = (bf16[128,512]{1,0:T(8,128)(2,1)S(1)}, bf16[128,512]{1,0:T(8,128)(2,1)S(1)}, u32[]{:S(2)}, u32[]{:S(2)}) collective-permute-start(bf16[128,512]{1,0:T(8,128)(2,1)S(1)} %fusion.3), channel_id=1, source_target_pairs={{0,32},{16,48},{32,0},{48,16},{64,96},{80,112},{96,64},{112,80},{1... | collective-permute-start | bytes 393224 | tf_op jit(solution)/shard_map/ppermute | solution.py:252
  42.7 15.3 %collective-permute-start.4 = (bf16[128,512]{1,0:T(8,128)(2,1)S(1)}, bf16[128,512]{1,0:T(8,128)(2,1)S(1)}, u32[]{:S(2)}, u32[]{:S(2)}) collective-permute-start(bf16[128,512]{1,0:T(8,128)(2,1)S(1)} %get-tuple-element.21), channel_id=1, source_target_pairs={{0,128},{16,144},{32,160},{48,176},{64,192},{80,208},{96,224},{112... | collective-permute-start | bytes 393224 | tf_op jit(solution)/shard_map/ppermute | solution.py:252
  49.8 9.5 %collective-permute-start.3 = (bf16[64,512]{1,0:T(8,128)(2,1)S(1)}, bf16[64,512]{1,0:T(8,128)(2,1)S(1)}, u32[]{:S(2)}, u32[]{:S(2)}) collective-permute-start(bf16[64,512]{1,0:T(8,128)(2,1)S(1)} %shard_map.106), channel_id=1, source_target_pairs={{0,16},{16,32},{32,48},{48,64},{64,80},{80,96},{96,112},{112,128},... | collective-permute-start | bytes 196616 | tf_op jit(solution)/shard_map/ppermute | solution.py:290
  60.4 34.7 %all-to-all-start.1 = ((bf16[16,64,512]{2,1,0:T(8,128)(2,1)}), bf16[16,64,512]{2,1,0:T(8,128)(2,1)S(1)}, u32[]{:S(2)}, u32[]{:S(2)}) async-start(bf16[16,64,512]{2,1,0:T(8,128)(2,1)} %shard_map.107), calls=%async_computation.1 | async-start | bytes 2097152 | tf_op jit(solution)/shard_map/all_to_all | solution.py:238
  67.1 9.6 %collective-permute-start.5 = (bf16[128,512]{1,0:T(8,128)(2,1)S(1)}, bf16[128,512]{1,0:T(8,128)(2,1)S(1)}, u32[]{:S(2)}, u32[]{:S(2)}) collective-permute-start(bf16[128,512]{1,0:T(8,128)(2,1)S(1)} %get-tuple-element.19), channel_id=1, source_target_pairs={{0,256},{16,272},{32,288},{48,304},{64,320},{80,336},{96,352},{112... | collective-permute-start | bytes 393224 | tf_op jit(solution)/shard_map/ppermute | solution.py:252
  77.7 7.1 %collective-permute-start.6 = (bf16[128,512]{1,0:T(8,128)(2,1)S(1)}, bf16[128,512]{1,0:T(8,128)(2,1)S(1)}, u32[]{:S(2)}, u32[]{:S(2)}) collective-permute-start(bf16[128,512]{1,0:T(8,128)(2,1)S(1)} %fusion.2), channel_id=1, source_target_pairs={{0,64},{16,80},{32,96},{48,112},{64,0},{80,16},{96,32},{112,48},{1... | collective-permute-start | bytes 393224 | tf_op jit(solution)/shard_map/ppermute | solution.py:252
  84.9 9.2 %collective-permute-start.7 = (bf16[256,512]{1,0:T(8,128)(2,1)S(1)}, bf16[256,512]{1,0:T(8,128)(2,1)S(1)}, u32[]{:S(2)}, u32[]{:S(2)}) collective-permute-start(bf16[256,512]{1,0:T(8,128)(2,1)S(1)} %maximum_select_fusion.1), channel_id=1, source_target_pairs={{0,16},{16,0},{32,48},{48,32},{64,80},{80,64},{96,112},{112,96},{1... | collective-permute-start | bytes 786440 | tf_op jit(solution)/shard_map/ppermute | solution.py:252

commit v8 on v7

--- a/solution.py
+++ b/solution.py
@@ -265,7 +265,7 @@
 
 def tag_sum_nearby(send, own, y_bit):
     own, send = split_sum(y_bit[None], own, swapped(send, 1))
-    return added(own + swapped(send, 4).astype(F32), 2)
+    return added(own + swapped(send, 4).astype(F32), 8)
 
 
 def new_tag_rows(total, w, core, y_bit):
@@ -288,7 +288,7 @@
     item_pieces, _, _ = lax.optimization_barrier((item_pieces, tag_total, new_users))
     shard = updated_items(lax.axis_index("tag")[None], v, item_pieces)
     shard = lax.ppermute(shard, "rot", [(i, (i + 1) % n_rot) for i in range(n_rot)])
-    tag_total = added(tag_total, 8)
+    tag_total = added(tag_total, 2)
     shard, _ = lax.optimization_barrier((shard, tag_total))
     rotated_items = placed_items(exchanged(spread(shard, n_tag), "tag")).reshape(v.shape)
     new_tags = new_tag_rows(added(tag_total, 16), w, core, y_bit)

time: 97.1 us -> 93 us (0.958)
  waiting for transfers between devices: 22.1 us -> 19.6 us
  starting transfers between devices: 59.9 us -> 58.1 us
    ppermute x7, waiting for transfers between devices: 20.8 us -> 18.3 us  [swapped(): return lax.ppermute(block, 'rot', [(i, i ^ mask) for i in range(n)])]
    all_to_all x2, starting transfers between devices: 18.6 us -> 17 us  [exchanged(): return lax.all_to_all(pieces, axis, 0, 0)]
    ppermute x1, starting transfers between devices: 8.19 us -> 6.78 us  [on_device(): lax.ppermute(shard, 'rot', [(i, (i + 1) % n_rot) for i in range(n_rot)])]
    ppermute x7, starting transfers between devices: 33.1 us -> 34.3 us  [swapped(): return lax.ppermute(block, 'rot', [(i, i ^ mask) for i in range(n)])]
where the time goes in v8:
time: 93 us; the launch traced here: 91.9 us
  starting transfers between devices  58.1 us (62%)
  waiting for transfers between devices  19.6 us (21%)
  Pallas kernels  10.5 us (11%)
  other arithmetic  2.16 us (2%)
  between operations  1.47 us (2%)
    ppermute x7, starting transfers between devices, swapped(): return lax.ppermute(block, 'rot', [(i, i ^ mask) for i in range(n)])  34.3 us
    ppermute x7, waiting for transfers between devices, swapped(): return lax.ppermute(block, 'rot', [(i, i ^ mask) for i in range(n)])  18.3 us
    all_to_all x2, starting transfers between devices, exchanged(): return lax.all_to_all(pieces, axis, 0, 0)  17 us
    ppermute x1, starting transfers between devices, on_device(): lax.ppermute(shard, 'rot', [(i, (i + 1) % n_rot) for i in range(n_rot)])  6.78 us
    pallas_call x1, Pallas kernels, partials(): pl.pallas_call(grads_kernel, out_shape=(jax.ShapeDtypeStruct((items, rank...  5.44 us
  transfers between devices with their start and end apart: 10, of which 7 were waited for; matrix products, arithmetic and copies ran while one was open for 2% of the time, Pallas kernels for 3%

profile of v8, /device:TPU:1, one launch (start us, length us, event | category | flops | bytes accessed | tf_op | source)
XLA Modules:
  0.0 91.9 jit_solution(3282133498255546719)
XLA Ops:
  1.3 5.4 %shard_map.103 = (bf16[1024,512]{1,0:T(8,128)(2,1)}, bf16[256,512]{1,0:T(8,128)(2,1)S(1)}, f32[256,512]{1,0:T(8,128)S(1)}, bf16[512,1024]{1,0:T(8,128)(2,1)S(1)}) custom-call(s32[1]{0:T(128)S(6)} %copy.11.rc_ref, s32[1]{0:T(128)} %bitcast.core_ref, s32[2,16]{1,0:T(2,128)} %bitcast.8, s32[2,16]{1,0:T(2,128)} %bitcast.9, bf16[512,512]{1,0:T(8,128)(2,1)} %u_ref.1, ...), custom_call_target="tpu_custom_call" | custom-call | flops 3221225472 | bytes 6291456 | tf_op jit(solution)/shard_map/pallas_call | solution.py:149
  6.7 12.0 %all-to-all-start = ((bf16[16,64,512]{2,1,0:T(8,128)(2,1)}), bf16[16,64,512]{2,1,0:T(8,128)(2,1)}, u32[]{:S(2)}, u32[]{:S(2)}) async-start(bf16[16,64,512]{2,1,0:T(8,128)(2,1)} %bitcast.4), calls=%async_computation | async-start | bytes 2097152 | tf_op jit(solution)/shard_map/all_to_all | solution.py:238
  18.7 2.8 %collective-permute-start = (bf16[256,512]{1,0:T(8,128)(2,1)S(1)}, bf16[256,512]{1,0:T(8,128)(2,1)S(1)}, u32[]{:S(2)}, u32[]{:S(2)}) collective-permute-start(bf16[256,512]{1,0:T(8,128)(2,1)S(1)} %get-tuple-element.14), channel_id=1, source_target_pairs={{0,16},{16,0},{32,48},{48,32},{64,80},{80,64},{96,112},{112,96},{1... | collective-permute-start | bytes 786440 | tf_op jit(solution)/shard_map/ppermute | solution.py:252
  21.6 1.1 %collective-permute-done.arrived_ref = bf16[256,512]{1,0:T(8,128)(2,1)S(1)} collective-permute-done((bf16[256,512]{1,0:T(8,128)(2,1)S(1)}, bf16[256,512]{1,0:T(8,128)(2,1)S(1)}, u32[]{:S(2)}, u32[]{:S(2)}) %collective-permute-start) | collective-permute-done | bytes 262176 | tf_op jit(solution)/shard_map/ppermute | solution.py:252
  22.7 0.0 copy-start
  22.8 3.3 %collective-permute-start.1 = (bf16[128,512]{1,0:T(8,128)(2,1)S(1)}, bf16[128,512]{1,0:T(8,128)(2,1)S(1)}, u32[]{:S(2)}, u32[]{:S(2)}) collective-permute-start(bf16[128,512]{1,0:T(8,128)(2,1)S(1)} %get-tuple-element.16), channel_id=1, source_target_pairs={{0,64},{16,80},{32,96},{48,112},{64,0},{80,16},{96,32},{112,48},{1... | collective-permute-start | bytes 393224 | tf_op jit(solution)/shard_map/ppermute | solution.py:252
  26.1 3.5 %collective-permute-done.1 = bf16[128,512]{1,0:T(8,128)(2,1)S(1)} collective-permute-done((bf16[128,512]{1,0:T(8,128)(2,1)S(1)}, bf16[128,512]{1,0:T(8,128)(2,1)S(1)}, u32[]{:S(2)}, u32[]{:S(2)}) %collective-permute-start.1) | collective-permute-done | bytes 131104 | tf_op jit(solution)/shard_map/ppermute | solution.py:252
  29.6 0.0 copy-start.1
  29.6 4.3 %collective-permute-start.2 = (bf16[128,512]{1,0:T(8,128)(2,1)S(1)}, bf16[128,512]{1,0:T(8,128)(2,1)S(1)}, u32[]{:S(2)}, u32[]{:S(2)}) collective-permute-start(bf16[128,512]{1,0:T(8,128)(2,1)S(1)} %fusion.3), channel_id=1, source_target_pairs={{0,128},{16,144},{32,160},{48,176},{64,192},{80,208},{96,224},{112... | collective-permute-start | bytes 393224 | tf_op jit(solution)/shard_map/ppermute | solution.py:252
  34.0 5.8 %collective-permute-done.2 = bf16[128,512]{1,0:T(8,128)(2,1)S(1)} collective-permute-done((bf16[128,512]{1,0:T(8,128)(2,1)S(1)}, bf16[128,512]{1,0:T(8,128)(2,1)S(1)}, u32[]{:S(2)}, u32[]{:S(2)}) %collective-permute-start.2) | collective-permute-done | bytes 131104 | tf_op jit(solution)/shard_map/ppermute | solution.py:252
  39.8 0.1 reduce-precision_convert_fusion.1
  39.9 4.4 %collective-permute-start.4 = (bf16[128,512]{1,0:T(8,128)(2,1)S(1)}, bf16[128,512]{1,0:T(8,128)(2,1)S(1)}, u32[]{:S(2)}, u32[]{:S(2)}) collective-permute-start(bf16[128,512]{1,0:T(8,128)(2,1)S(1)} %get-tuple-element.21), channel_id=1, source_target_pairs={{0,32},{16,48},{32,0},{48,16},{64,96},{80,112},{96,64},{112,80},{1... | collective-permute-start | bytes 393224 | tf_op jit(solution)/shard_map/ppermute | solution.py:252
  44.3 0.0 copy-done
  44.3 0.0 copy-done.1
  44.3 1.6 %shard_map.104 = bf16[512,512]{1,0:T(8,128)(2,1)} custom-call(bf16[512,1024]{1,0:T(8,128)(2,1)S(1)} %get-tuple-element.11.err_ref, bf16[512,512]{1,0:T(8,128)(2,1)S(1)} %copy-done.1, bf16[1024,512]{1,0:T(8,128)(2,1)S(1)} %copy-done), custom_call_target="tpu_custom_call" | custom-call | flops 1073741824 | bytes 4194304 | tf_op jit(solution)/shard_map/pallas_call | solution.py:171
  45.9 0.0 all-to-all-done.pieces_hbm
  45.9 1.3 %shard_map.106 = bf16[64,512]{1,0:T(8,128)(2,1)S(1)} custom-call(s32[1]{0:T(128)} %bitcast.3.tag_ref, bf16[1024,512]{1,0:T(8,128)(2,1)} %v_hbm.3, bf16[16,64,512]{2,1,0:T(8,128)(2,1)} %all-to-all-done.pieces_hbm), custom_call_target="tpu_custom_call" | custom-call | flops 524288 | bytes 1048576 | tf_op jit(solution)/shard_map/pallas_call | solution.py:198
  47.2 6.8 %collective-permute-start.3 = (bf16[64,512]{1,0:T(8,128)(2,1)S(1)}, bf16[64,512]{1,0:T(8,128)(2,1)S(1)}, u32[]{:S(2)}, u32[]{:S(2)}) collective-permute-start(bf16[64,512]{1,0:T(8,128)(2,1)S(1)} %shard_map.106), channel_id=1, source_target_pairs={{0,16},{16,32},{32,48},{48,64},{64,80},{80,96},{96,112},{112,128},... | collective-permute-start | bytes 196616 | tf_op jit(solution)/shard_map/ppermute | solution.py:290
  53.9 0.0 collective-permute-done.4
  54.0 1.3 %collective-permute-done.3.shard_ref = bf16[64,512]{1,0:T(8,128)(2,1)S(1)} collective-permute-done((bf16[64,512]{1,0:T(8,128)(2,1)S(1)}, bf16[64,512]{1,0:T(8,128)(2,1)S(1)}, u32[]{:S(2)}, u32[]{:S(2)}) %collective-permute-start.3) | collective-permute-done | bytes 65568 | tf_op jit(solution)/shard_map/ppermute | solution.py:290
  55.3 1.1 %shard_map.107 = bf16[16,64,512]{2,1,0:T(8,128)(2,1)} custom-call(bf16[64,512]{1,0:T(8,128)(2,1)S(1)} %collective-permute-done.3.shard_ref), custom_call_target="tpu_custom_call" | custom-call | bytes 1048576 | tf_op jit(solution)/shard_map/pallas_call | solution.py:214
  56.4 5.0 %all-to-all-start.1 = ((bf16[16,64,512]{2,1,0:T(8,128)(2,1)}), bf16[16,64,512]{2,1,0:T(8,128)(2,1)S(1)}, u32[]{:S(2)}, u32[]{:S(2)}) async-start(bf16[16,64,512]{2,1,0:T(8,128)(2,1)} %shard_map.107), calls=%async_computation.1 | async-start | bytes 2097152 | tf_op jit(solution)/shard_map/all_to_all | solution.py:238
  61.4 7.5 %collective-permute-start.5 = (bf16[128,512]{1,0:T(8,128)(2,1)S(1)}, bf16[128,512]{1,0:T(8,128)(2,1)S(1)}, u32[]{:S(2)}, u32[]{:S(2)}) collective-permute-start(bf16[128,512]{1,0:T(8,128)(2,1)S(1)} %get-tuple-element.19), channel_id=1, source_target_pairs={{0,256},{16,272},{32,288},{48,304},{64,320},{80,336},{96,352},{112... | collective-permute-start | bytes 393224 | tf_op jit(solution)/shard_map/ppermute | solution.py:252
  68.9 2.4 %collective-permute-done.5 = bf16[128,512]{1,0:T(8,128)(2,1)S(1)} collective-permute-done((bf16[128,512]{1,0:T(8,128)(2,1)S(1)}, bf16[128,512]{1,0:T(8,128)(2,1)S(1)}, u32[]{:S(2)}, u32[]{:S(2)}) %collective-permute-start.5) | collective-permute-done | bytes 131104 | tf_op jit(solution)/shard_map/ppermute | solution.py:252
  71.3 1.0 %fusion.2 = bf16[128,512]{1,0:T(8,128)(2,1)S(1)} fusion(bf16[128,512]{1,0:T(8,128)(2,1)S(1)} %collective-permute-done.5, f32[128,512]{1,0:T(8,128)S(1)} %get-tuple-element.20, bf16[512,512]{1,0:T(8,128)(2,1)} %w_hbm.1, s32[]{:T(128)S(6)} %select_n.21), kind=kLoop, calls=%fused_computation.5 | loop fusion | flops 589824 | bytes 655364 | tf_op jit(solution)/shard_map/convert_element_type | solution.py:243
  72.3 2.1 %collective-permute-start.6 = (bf16[128,512]{1,0:T(8,128)(2,1)S(1)}, bf16[128,512]{1,0:T(8,128)(2,1)S(1)}, u32[]{:S(2)}, u32[]{:S(2)}) collective-permute-start(bf16[128,512]{1,0:T(8,128)(2,1)S(1)} %fusion.2), channel_id=1, source_target_pairs={{0,64},{16,80},{32,96},{48,112},{64,0},{80,16},{96,32},{112,48},{1... | collective-permute-start | bytes 393224 | tf_op jit(solution)/shard_map/ppermute | solution.py:252
  74.4 4.3 %collective-permute-done.6 = bf16[128,512]{1,0:T(8,128)(2,1)S(1)} collective-permute-done((bf16[128,512]{1,0:T(8,128)(2,1)S(1)}, bf16[128,512]{1,0:T(8,128)(2,1)S(1)}, u32[]{:S(2)}, u32[]{:S(2)}) %collective-permute-start.6) | collective-permute-done | bytes 131104 | tf_op jit(solution)/shard_map/ppermute | solution.py:252
  78.7 0.1 maximum_select_fusion.1
  78.8 9.8 %collective-permute-start.7 = (bf16[256,512]{1,0:T(8,128)(2,1)S(1)}, bf16[256,512]{1,0:T(8,128)(2,1)S(1)}, u32[]{:S(2)}, u32[]{:S(2)}) collective-permute-start(bf16[256,512]{1,0:T(8,128)(2,1)S(1)} %maximum_select_fusion.1), channel_id=1, source_target_pairs={{0,16},{16,0},{32,48},{48,32},{64,80},{80,64},{96,112},{112,96},{1... | collective-permute-start | bytes 786440 | tf_op jit(solution)/shard_map/ppermute | solution.py:252
  88.7 1.1 %collective-permute-done.7 = bf16[256,512]{1,0:T(8,128)(2,1)S(1)} collective-permute-done((bf16[256,512]{1,0:T(8,128)(2,1)S(1)}, bf16[256,512]{1,0:T(8,128)(2,1)S(1)}, u32[]{:S(2)}, u32[]{:S(2)}) %collective-permute-start.7) | collective-permute-done | bytes 262176 | tf_op jit(solution)/shard_map/ppermute | solution.py:252
  89.8 1.0 %maximum_select_fusion = bf16[512,512]{1,0:T(8,128)(2,1)} fusion(bf16[256,512]{1,0:T(8,128)(2,1)S(1)} %collective-permute-done.7, bf16[256,512]{1,0:T(8,128)(2,1)S(1)} %maximum_select_fusion.1, pred[]{:T(512)S(6)} %eq.6), kind=kLoop, calls=%fused_computation | loop fusion | flops 2359296 | bytes 1048577 | tf_op jit(solution)/shard_map/jit(_where)/select_n | solution.py:256
  90.8 0.0 all-to-all-done.1.in_ref
  90.8 1.1 %shard_map.108 = bf16[16,64,512]{2,1,0:T(8,128)(2,1)} custom-call(bf16[16,64,512]{2,1,0:T(8,128)(2,1)S(1)} %all-to-all-done.1.in_ref), custom_call_target="tpu_custom_call" | custom-call | bytes 2097152 | tf_op jit(solution)/shard_map/pallas_call | solution.py:226
  (3 shorter events, 0.1 us)
Async XLA Ops:
  6.7 39.1 %all-to-all-start = ((bf16[16,64,512]{2,1,0:T(8,128)(2,1)}), bf16[16,64,512]{2,1,0:T(8,128)(2,1)}, u32[]{:S(2)}, u32[]{:S(2)}) async-start(bf16[16,64,512]{2,1,0:T(8,128)(2,1)} %bitcast.4), calls=%async_computation | async-start | bytes 2097152 | tf_op jit(solution)/shard_map/all_to_all | solution.py:238
  18.7 4.0 %collective-permute-start = (bf16[256,512]{1,0:T(8,128)(2,1)S(1)}, bf16[256,512]{1,0:T(8,128)(2,1)S(1)}, u32[]{:S(2)}, u32[]{:S(2)}) collective-permute-start(bf16[256,512]{1,0:T(8,128)(2,1)S(1)} %get-tuple-element.14), channel_id=1, source_target_pairs={{0,16},{16,0},{32,48},{48,32},{64,80},{80,64},{96,112},{112,96},{1... | collective-permute-start | bytes 786440 | tf_op jit(solution)/shard_map/ppermute | solution.py:252
  22.7 21.6 %copy-start = (bf16[1024,512]{1,0:T(8,128)(2,1)S(1)}, bf16[1024,512]{1,0:T(8,128)(2,1)}, u32[]{:S(2)}) copy-start(bf16[1024,512]{1,0:T(8,128)(2,1)} %v_hbm.3) | copy-start | bytes 3145732
  22.8 6.8 %collective-permute-start.1 = (bf16[128,512]{1,0:T(8,128)(2,1)S(1)}, bf16[128,512]{1,0:T(8,128)(2,1)S(1)}, u32[]{:S(2)}, u32[]{:S(2)}) collective-permute-start(bf16[128,512]{1,0:T(8,128)(2,1)S(1)} %get-tuple-element.16), channel_id=1, source_target_pairs={{0,64},{16,80},{32,96},{48,112},{64,0},{80,16},{96,32},{112,48},{1... | collective-permute-start | bytes 393224 | tf_op jit(solution)/shard_map/ppermute | solution.py:252
  29.6 14.6 %copy-start.1 = (bf16[512,512]{1,0:T(8,128)(2,1)S(1)}, bf16[512,512]{1,0:T(8,128)(2,1)}, u32[]{:S(2)}) copy-start(bf16[512,512]{1,0:T(8,128)(2,1)} %u_ref.1) | copy-start | bytes 1572868
  29.6 10.2 %collective-permute-start.2 = (bf16[128,512]{1,0:T(8,128)(2,1)S(1)}, bf16[128,512]{1,0:T(8,128)(2,1)S(1)}, u32[]{:S(2)}, u32[]{:S(2)}) collective-permute-start(bf16[128,512]{1,0:T(8,128)(2,1)S(1)} %fusion.3), channel_id=1, source_target_pairs={{0,128},{16,144},{32,160},{48,176},{64,192},{80,208},{96,224},{112... | collective-permute-start | bytes 393224 | tf_op jit(solution)/shard_map/ppermute | solution.py:252
  39.9 14.1 %collective-permute-start.4 = (bf16[128,512]{1,0:T(8,128)(2,1)S(1)}, bf16[128,512]{1,0:T(8,128)(2,1)S(1)}, u32[]{:S(2)}, u32[]{:S(2)}) collective-permute-start(bf16[128,512]{1,0:T(8,128)(2,1)S(1)} %get-tuple-element.21), channel_id=1, source_target_pairs={{0,32},{16,48},{32,0},{48,16},{64,96},{80,112},{96,64},{112,80},{1... | collective-permute-start | bytes 393224 | tf_op jit(solution)/shard_map/ppermute | solution.py:252
  47.2 8.1 %collective-permute-start.3 = (bf16[64,512]{1,0:T(8,128)(2,1)S(1)}, bf16[64,512]{1,0:T(8,128)(2,1)S(1)}, u32[]{:S(2)}, u32[]{:S(2)}) collective-permute-start(bf16[64,512]{1,0:T(8,128)(2,1)S(1)} %shard_map.106), channel_id=1, source_target_pairs={{0,16},{16,32},{32,48},{48,64},{64,80},{80,96},{96,112},{112,128},... | collective-permute-start | bytes 196616 | tf_op jit(solution)/shard_map/ppermute | solution.py:290
  56.4 34.5 %all-to-all-start.1 = ((bf16[16,64,512]{2,1,0:T(8,128)(2,1)}), bf16[16,64,512]{2,1,0:T(8,128)(2,1)S(1)}, u32[]{:S(2)}, u32[]{:S(2)}) async-start(bf16[16,64,512]{2,1,0:T(8,128)(2,1)} %shard_map.107), calls=%async_computation.1 | async-start | bytes 2097152 | tf_op jit(solution)/shard_map/all_to_all | solution.py:238
  61.4 9.9 %collective-permute-start.5 = (bf16[128,512]{1,0:T(8,128)(2,1)S(1)}, bf16[128,512]{1,0:T(8,128)(2,1)S(1)}, u32[]{:S(2)}, u32[]{:S(2)}) collective-permute-start(bf16[128,512]{1,0:T(8,128)(2,1)S(1)} %get-tuple-element.19), channel_id=1, source_target_pairs={{0,256},{16,272},{32,288},{48,304},{64,320},{80,336},{96,352},{112... | collective-permute-start | bytes 393224 | tf_op jit(solution)/shard_map/ppermute | solution.py:252
  72.3 6.5 %collective-permute-start.6 = (bf16[128,512]{1,0:T(8,128)(2,1)S(1)}, bf16[128,512]{1,0:T(8,128)(2,1)S(1)}, u32[]{:S(2)}, u32[]{:S(2)}) collective-permute-start(bf16[128,512]{1,0:T(8,128)(2,1)S(1)} %fusion.2), channel_id=1, source_target_pairs={{0,64},{16,80},{32,96},{48,112},{64,0},{80,16},{96,32},{112,48},{1... | collective-permute-start | bytes 393224 | tf_op jit(solution)/shard_map/ppermute | solution.py:252
  78.8 11.0 %collective-permute-start.7 = (bf16[256,512]{1,0:T(8,128)(2,1)S(1)}, bf16[256,512]{1,0:T(8,128)(2,1)S(1)}, u32[]{:S(2)}, u32[]{:S(2)}) collective-permute-start(bf16[256,512]{1,0:T(8,128)(2,1)S(1)} %maximum_select_fusion.1), channel_id=1, source_target_pairs={{0,16},{16,0},{32,48},{48,32},{64,80},{80,64},{96,112},{112,96},{1... | collective-permute-start | bytes 786440 | tf_op jit(solution)/shard_map/ppermute | solution.py:252

commit v9 on v8

--- a/solution.py
+++ b/solution.py
@@ -265,7 +265,7 @@
 
 def tag_sum_nearby(send, own, y_bit):
     own, send = split_sum(y_bit[None], own, swapped(send, 1))
-    return added(own + swapped(send, 4).astype(F32), 8)
+    return added(own + swapped(send, 4).astype(F32), 16)
 
 
 def new_tag_rows(total, w, core, y_bit):
@@ -291,7 +291,7 @@
     tag_total = added(tag_total, 2)
     shard, _ = lax.optimization_barrier((shard, tag_total))
     rotated_items = placed_items(exchanged(spread(shard, n_tag), "tag")).reshape(v.shape)
-    new_tags = new_tag_rows(added(tag_total, 16), w, core, y_bit)
+    new_tags = new_tag_rows(added(tag_total, 8), w, core, y_bit)
     return (new_users, rotated_items, new_tags)
 
 

time: 93 us -> 95.7 us (1.029)
  the two profiles are of different devices: /device:TPU:1 before, /device:TPU:28 now
where the time goes in v9:
time: 95.7 us; the launch traced here: 95.2 us
  waiting for transfers between devices  40.8 us (43%)
  starting transfers between devices  40.2 us (42%)
  Pallas kernels  10.5 us (11%)
  other arithmetic  2.16 us (2%)
  between operations  1.47 us (2%)
    ppermute x7, waiting for transfers between devices, swapped(): return lax.ppermute(block, 'rot', [(i, i ^ mask) for i in range(n)])  29.8 us
    all_to_all x2, starting transfers between devices, exchanged(): return lax.all_to_all(pieces, axis, 0, 0)  19.6 us
    ppermute x7, starting transfers between devices, swapped(): return lax.ppermute(block, 'rot', [(i, i ^ mask) for i in range(n)])  18.7 us
    all_to_all x2, waiting for transfers between devices, exchanged(): return lax.all_to_all(pieces, axis, 0, 0)  6.55 us
    pallas_call x1, Pallas kernels, partials(): pl.pallas_call(grads_kernel, out_shape=(jax.ShapeDtypeStruct((items, rank...  5.44 us
    ppermute x1, waiting for transfers between devices, on_device(): lax.ppermute(shard, 'rot', [(i, (i + 1) % n_rot) for i in range(n_rot)])  4.46 us
    ppermute x1, starting transfers between devices, on_device(): lax.ppermute(shard, 'rot', [(i, (i + 1) % n_rot) for i in range(n_rot)])  1.92 us
  transfers between devices with their start and end apart: 10, of which 10 were waited for; matrix products, arithmetic and copies ran while one was open for 2% of the time, Pallas kernels for 3%

profile of v9, /device:TPU:28, one launch (start us, length us, event | category | flops | bytes accessed | tf_op | source)
XLA Modules:
  0.0 95.2 jit_solution(13951872618247389525)
XLA Ops:
  1.3 5.4 %shard_map.103 = (bf16[1024,512]{1,0:T(8,128)(2,1)}, bf16[256,512]{1,0:T(8,128)(2,1)S(1)}, f32[256,512]{1,0:T(8,128)S(1)}, bf16[512,1024]{1,0:T(8,128)(2,1)S(1)}) custom-call(s32[1]{0:T(128)S(6)} %copy.11.rc_ref, s32[1]{0:T(128)} %bitcast.core_ref, s32[2,16]{1,0:T(2,128)} %bitcast.8, s32[2,16]{1,0:T(2,128)} %bitcast.9, bf16[512,512]{1,0:T(8,128)(2,1)} %u_ref.1, ...), custom_call_target="tpu_custom_call" | custom-call | flops 3221225472 | bytes 6291456 | tf_op jit(solution)/shard_map/pallas_call | solution.py:149
  6.7 11.1 %all-to-all-start = ((bf16[16,64,512]{2,1,0:T(8,128)(2,1)}), bf16[16,64,512]{2,1,0:T(8,128)(2,1)}, u32[]{:S(2)}, u32[]{:S(2)}) async-start(bf16[16,64,512]{2,1,0:T(8,128)(2,1)} %bitcast.4), calls=%async_computation | async-start | bytes 2097152 | tf_op jit(solution)/shard_map/all_to_all | solution.py:238
  17.8 1.9 %collective-permute-start = (bf16[256,512]{1,0:T(8,128)(2,1)S(1)}, bf16[256,512]{1,0:T(8,128)(2,1)S(1)}, u32[]{:S(2)}, u32[]{:S(2)}) collective-permute-start(bf16[256,512]{1,0:T(8,128)(2,1)S(1)} %get-tuple-element.14), channel_id=1, source_target_pairs={{0,16},{16,0},{32,48},{48,32},{64,80},{80,64},{96,112},{112,96},{1... | collective-permute-start | bytes 786440 | tf_op jit(solution)/shard_map/ppermute | solution.py:252
  19.8 1.5 %collective-permute-done.arrived_ref = bf16[256,512]{1,0:T(8,128)(2,1)S(1)} collective-permute-done((bf16[256,512]{1,0:T(8,128)(2,1)S(1)}, bf16[256,512]{1,0:T(8,128)(2,1)S(1)}, u32[]{:S(2)}, u32[]{:S(2)}) %collective-permute-start) | collective-permute-done | bytes 262176 | tf_op jit(solution)/shard_map/ppermute | solution.py:252
  21.3 0.0 copy-start
  21.3 2.5 %collective-permute-start.1 = (bf16[128,512]{1,0:T(8,128)(2,1)S(1)}, bf16[128,512]{1,0:T(8,128)(2,1)S(1)}, u32[]{:S(2)}, u32[]{:S(2)}) collective-permute-start(bf16[128,512]{1,0:T(8,128)(2,1)S(1)} %get-tuple-element.16), channel_id=1, source_target_pairs={{0,64},{16,80},{32,96},{48,112},{64,0},{80,16},{96,32},{112,48},{1... | collective-permute-start | bytes 393224 | tf_op jit(solution)/shard_map/ppermute | solution.py:252
  23.8 5.1 %collective-permute-done.1 = bf16[128,512]{1,0:T(8,128)(2,1)S(1)} collective-permute-done((bf16[128,512]{1,0:T(8,128)(2,1)S(1)}, bf16[128,512]{1,0:T(8,128)(2,1)S(1)}, u32[]{:S(2)}, u32[]{:S(2)}) %collective-permute-start.1) | collective-permute-done | bytes 131104 | tf_op jit(solution)/shard_map/ppermute | solution.py:252
  28.9 0.0 copy-start.1
  28.9 5.2 %collective-permute-start.2 = (bf16[128,512]{1,0:T(8,128)(2,1)S(1)}, bf16[128,512]{1,0:T(8,128)(2,1)S(1)}, u32[]{:S(2)}, u32[]{:S(2)}) collective-permute-start(bf16[128,512]{1,0:T(8,128)(2,1)S(1)} %fusion.3), channel_id=1, source_target_pairs={{0,256},{16,272},{32,288},{48,304},{64,320},{80,336},{96,352},{112... | collective-permute-start | bytes 393224 | tf_op jit(solution)/shard_map/ppermute | solution.py:252
  34.1 7.9 %collective-permute-done.2 = bf16[128,512]{1,0:T(8,128)(2,1)S(1)} collective-permute-done((bf16[128,512]{1,0:T(8,128)(2,1)S(1)}, bf16[128,512]{1,0:T(8,128)(2,1)S(1)}, u32[]{:S(2)}, u32[]{:S(2)}) %collective-permute-start.2) | collective-permute-done | bytes 131104 | tf_op jit(solution)/shard_map/ppermute | solution.py:252
  42.1 0.1 reduce-precision_convert_fusion.1
  42.1 2.7 %collective-permute-start.4 = (bf16[128,512]{1,0:T(8,128)(2,1)S(1)}, bf16[128,512]{1,0:T(8,128)(2,1)S(1)}, u32[]{:S(2)}, u32[]{:S(2)}) collective-permute-start(bf16[128,512]{1,0:T(8,128)(2,1)S(1)} %get-tuple-element.21), channel_id=1, source_target_pairs={{0,32},{16,48},{32,0},{48,16},{64,96},{80,112},{96,64},{112,80},{1... | collective-permute-start | bytes 393224 | tf_op jit(solution)/shard_map/ppermute | solution.py:252
  44.8 0.0 copy-done
  44.8 0.0 copy-done.1
  44.8 1.6 %shard_map.104 = bf16[512,512]{1,0:T(8,128)(2,1)} custom-call(bf16[512,1024]{1,0:T(8,128)(2,1)S(1)} %get-tuple-element.11.err_ref, bf16[512,512]{1,0:T(8,128)(2,1)S(1)} %copy-done.1, bf16[1024,512]{1,0:T(8,128)(2,1)S(1)} %copy-done), custom_call_target="tpu_custom_call" | custom-call | flops 1073741824 | bytes 4194304 | tf_op jit(solution)/shard_map/pallas_call | solution.py:171
  46.4 0.2 all-to-all-done.pieces_hbm
  46.6 1.3 %shard_map.106 = bf16[64,512]{1,0:T(8,128)(2,1)S(1)} custom-call(s32[1]{0:T(128)} %bitcast.3.tag_ref, bf16[1024,512]{1,0:T(8,128)(2,1)} %v_hbm.3, bf16[16,64,512]{2,1,0:T(8,128)(2,1)} %all-to-all-done.pieces_hbm), custom_call_target="tpu_custom_call" | custom-call | flops 524288 | bytes 1048576 | tf_op jit(solution)/shard_map/pallas_call | solution.py:198
  47.9 1.9 %collective-permute-start.3 = (bf16[64,512]{1,0:T(8,128)(2,1)S(1)}, bf16[64,512]{1,0:T(8,128)(2,1)S(1)}, u32[]{:S(2)}, u32[]{:S(2)}) collective-permute-start(bf16[64,512]{1,0:T(8,128)(2,1)S(1)} %shard_map.106), channel_id=1, source_target_pairs={{0,16},{16,32},{32,48},{48,64},{64,80},{80,96},{96,112},{112,128},... | collective-permute-start | bytes 196616 | tf_op jit(solution)/shard_map/ppermute | solution.py:290
  49.8 0.7 collective-permute-done.4
  50.5 4.5 %collective-permute-done.3.shard_ref = bf16[64,512]{1,0:T(8,128)(2,1)S(1)} collective-permute-done((bf16[64,512]{1,0:T(8,128)(2,1)S(1)}, bf16[64,512]{1,0:T(8,128)(2,1)S(1)}, u32[]{:S(2)}, u32[]{:S(2)}) %collective-permute-start.3) | collective-permute-done | bytes 65568 | tf_op jit(solution)/shard_map/ppermute | solution.py:290
  55.0 1.1 %shard_map.107 = bf16[16,64,512]{2,1,0:T(8,128)(2,1)} custom-call(bf16[64,512]{1,0:T(8,128)(2,1)S(1)} %collective-permute-done.3.shard_ref), custom_call_target="tpu_custom_call" | custom-call | bytes 1048576 | tf_op jit(solution)/shard_map/pallas_call | solution.py:214
  56.1 8.5 %all-to-all-start.1 = ((bf16[16,64,512]{2,1,0:T(8,128)(2,1)}), bf16[16,64,512]{2,1,0:T(8,128)(2,1)S(1)}, u32[]{:S(2)}, u32[]{:S(2)}) async-start(bf16[16,64,512]{2,1,0:T(8,128)(2,1)} %shard_map.107), calls=%async_computation.1 | async-start | bytes 2097152 | tf_op jit(solution)/shard_map/all_to_all | solution.py:238
  64.6 2.5 %collective-permute-start.5 = (bf16[128,512]{1,0:T(8,128)(2,1)S(1)}, bf16[128,512]{1,0:T(8,128)(2,1)S(1)}, u32[]{:S(2)}, u32[]{:S(2)}) collective-permute-start(bf16[128,512]{1,0:T(8,128)(2,1)S(1)} %get-tuple-element.19), channel_id=1, source_target_pairs={{0,128},{16,144},{32,160},{48,176},{64,192},{80,208},{96,224},{112... | collective-permute-start | bytes 393224 | tf_op jit(solution)/shard_map/ppermute | solution.py:252
  67.1 7.9 %collective-permute-done.5 = bf16[128,512]{1,0:T(8,128)(2,1)S(1)} collective-permute-done((bf16[128,512]{1,0:T(8,128)(2,1)S(1)}, bf16[128,512]{1,0:T(8,128)(2,1)S(1)}, u32[]{:S(2)}, u32[]{:S(2)}) %collective-permute-start.5) | collective-permute-done | bytes 131104 | tf_op jit(solution)/shard_map/ppermute | solution.py:252
  75.0 1.0 %fusion.2 = bf16[128,512]{1,0:T(8,128)(2,1)S(1)} fusion(bf16[128,512]{1,0:T(8,128)(2,1)S(1)} %collective-permute-done.5, f32[128,512]{1,0:T(8,128)S(1)} %get-tuple-element.20, bf16[512,512]{1,0:T(8,128)(2,1)} %w_hbm.1, s32[]{:T(128)S(6)} %select_n.21), kind=kLoop, calls=%fused_computation.5 | loop fusion | flops 589824 | bytes 655364 | tf_op jit(solution)/shard_map/convert_element_type | solution.py:243
  76.0 1.9 %collective-permute-start.6 = (bf16[128,512]{1,0:T(8,128)(2,1)S(1)}, bf16[128,512]{1,0:T(8,128)(2,1)S(1)}, u32[]{:S(2)}, u32[]{:S(2)}) collective-permute-start(bf16[128,512]{1,0:T(8,128)(2,1)S(1)} %fusion.2), channel_id=1, source_target_pairs={{0,64},{16,80},{32,96},{48,112},{64,0},{80,16},{96,32},{112,48},{1... | collective-permute-start | bytes 393224 | tf_op jit(solution)/shard_map/ppermute | solution.py:252
  77.9 5.3 %collective-permute-done.6 = bf16[128,512]{1,0:T(8,128)(2,1)S(1)} collective-permute-done((bf16[128,512]{1,0:T(8,128)(2,1)S(1)}, bf16[128,512]{1,0:T(8,128)(2,1)S(1)}, u32[]{:S(2)}, u32[]{:S(2)}) %collective-permute-start.6) | collective-permute-done | bytes 131104 | tf_op jit(solution)/shard_map/ppermute | solution.py:252
  83.2 0.1 maximum_select_fusion.1
  83.3 1.9 %collective-permute-start.7 = (bf16[256,512]{1,0:T(8,128)(2,1)S(1)}, bf16[256,512]{1,0:T(8,128)(2,1)S(1)}, u32[]{:S(2)}, u32[]{:S(2)}) collective-permute-start(bf16[256,512]{1,0:T(8,128)(2,1)S(1)} %maximum_select_fusion.1), channel_id=1, source_target_pairs={{0,16},{16,0},{32,48},{48,32},{64,80},{80,64},{96,112},{112,96},{1... | collective-permute-start | bytes 786440 | tf_op jit(solution)/shard_map/ppermute | solution.py:252
  85.2 1.5 %collective-permute-done.7 = bf16[256,512]{1,0:T(8,128)(2,1)S(1)} collective-permute-done((bf16[256,512]{1,0:T(8,128)(2,1)S(1)}, bf16[256,512]{1,0:T(8,128)(2,1)S(1)}, u32[]{:S(2)}, u32[]{:S(2)}) %collective-permute-start.7) | collective-permute-done | bytes 262176 | tf_op jit(solution)/shard_map/ppermute | solution.py:252
  86.7 1.0 %maximum_select_fusion = bf16[512,512]{1,0:T(8,128)(2,1)} fusion(bf16[256,512]{1,0:T(8,128)(2,1)S(1)} %collective-permute-done.7, bf16[256,512]{1,0:T(8,128)(2,1)S(1)} %maximum_select_fusion.1, pred[]{:T(512)S(6)} %eq.6), kind=kLoop, calls=%fused_computation | loop fusion | flops 2359296 | bytes 1048577 | tf_op jit(solution)/shard_map/jit(_where)/select_n | solution.py:256
  87.7 6.4 %all-to-all-done.1.in_ref = bf16[16,64,512]{2,1,0:T(8,128)(2,1)S(1)} async-done(((bf16[16,64,512]{2,1,0:T(8,128)(2,1)}), bf16[16,64,512]{2,1,0:T(8,128)(2,1)S(1)}, u32[]{:S(2)}, u32[]{:S(2)}) %all-to-all-start.1) | async-done | bytes 1048608 | tf_op jit(solution)/shard_map/all_to_all | solution.py:238
  94.1 1.1 %shard_map.108 = bf16[16,64,512]{2,1,0:T(8,128)(2,1)} custom-call(bf16[16,64,512]{2,1,0:T(8,128)(2,1)S(1)} %all-to-all-done.1.in_ref), custom_call_target="tpu_custom_call" | custom-call | bytes 2097152 | tf_op jit(solution)/shard_map/pallas_call | solution.py:226
  (3 shorter events, 0.1 us)
Async XLA Ops:
  6.7 39.9 %all-to-all-start = ((bf16[16,64,512]{2,1,0:T(8,128)(2,1)}), bf16[16,64,512]{2,1,0:T(8,128)(2,1)}, u32[]{:S(2)}, u32[]{:S(2)}) async-start(bf16[16,64,512]{2,1,0:T(8,128)(2,1)} %bitcast.4), calls=%async_computation | async-start | bytes 2097152 | tf_op jit(solution)/shard_map/all_to_all | solution.py:238
  17.8 3.4 %collective-permute-start = (bf16[256,512]{1,0:T(8,128)(2,1)S(1)}, bf16[256,512]{1,0:T(8,128)(2,1)S(1)}, u32[]{:S(2)}, u32[]{:S(2)}) collective-permute-start(bf16[256,512]{1,0:T(8,128)(2,1)S(1)} %get-tuple-element.14), channel_id=1, source_target_pairs={{0,16},{16,0},{32,48},{48,32},{64,80},{80,64},{96,112},{112,96},{1... | collective-permute-start | bytes 786440 | tf_op jit(solution)/shard_map/ppermute | solution.py:252
  21.3 23.6 %copy-start = (bf16[1024,512]{1,0:T(8,128)(2,1)S(1)}, bf16[1024,512]{1,0:T(8,128)(2,1)}, u32[]{:S(2)}) copy-start(bf16[1024,512]{1,0:T(8,128)(2,1)} %v_hbm.3) | copy-start | bytes 3145732
  21.3 7.6 %collective-permute-start.1 = (bf16[128,512]{1,0:T(8,128)(2,1)S(1)}, bf16[128,512]{1,0:T(8,128)(2,1)S(1)}, u32[]{:S(2)}, u32[]{:S(2)}) collective-permute-start(bf16[128,512]{1,0:T(8,128)(2,1)S(1)} %get-tuple-element.16), channel_id=1, source_target_pairs={{0,64},{16,80},{32,96},{48,112},{64,0},{80,16},{96,32},{112,48},{1... | collective-permute-start | bytes 393224 | tf_op jit(solution)/shard_map/ppermute | solution.py:252
  28.9 15.9 %copy-start.1 = (bf16[512,512]{1,0:T(8,128)(2,1)S(1)}, bf16[512,512]{1,0:T(8,128)(2,1)}, u32[]{:S(2)}) copy-start(bf16[512,512]{1,0:T(8,128)(2,1)} %u_ref.1) | copy-start | bytes 1572868
  28.9 13.1 %collective-permute-start.2 = (bf16[128,512]{1,0:T(8,128)(2,1)S(1)}, bf16[128,512]{1,0:T(8,128)(2,1)S(1)}, u32[]{:S(2)}, u32[]{:S(2)}) collective-permute-start(bf16[128,512]{1,0:T(8,128)(2,1)S(1)} %fusion.3), channel_id=1, source_target_pairs={{0,256},{16,272},{32,288},{48,304},{64,320},{80,336},{96,352},{112... | collective-permute-start | bytes 393224 | tf_op jit(solution)/shard_map/ppermute | solution.py:252
  42.1 8.4 %collective-permute-start.4 = (bf16[128,512]{1,0:T(8,128)(2,1)S(1)}, bf16[128,512]{1,0:T(8,128)(2,1)S(1)}, u32[]{:S(2)}, u32[]{:S(2)}) collective-permute-start(bf16[128,512]{1,0:T(8,128)(2,1)S(1)} %get-tuple-element.21), channel_id=1, source_target_pairs={{0,32},{16,48},{32,0},{48,16},{64,96},{80,112},{96,64},{112,80},{1... | collective-permute-start | bytes 393224 | tf_op jit(solution)/shard_map/ppermute | solution.py:252
  47.9 7.1 %collective-permute-start.3 = (bf16[64,512]{1,0:T(8,128)(2,1)S(1)}, bf16[64,512]{1,0:T(8,128)(2,1)S(1)}, u32[]{:S(2)}, u32[]{:S(2)}) collective-permute-start(bf16[64,512]{1,0:T(8,128)(2,1)S(1)} %shard_map.106), channel_id=1, source_target_pairs={{0,16},{16,32},{32,48},{48,64},{64,80},{80,96},{96,112},{112,128},... | collective-permute-start | bytes 196616 | tf_op jit(solution)/shard_map/ppermute | solution.py:290
  56.1 38.0 %all-to-all-start.1 = ((bf16[16,64,512]{2,1,0:T(8,128)(2,1)}), bf16[16,64,512]{2,1,0:T(8,128)(2,1)S(1)}, u32[]{:S(2)}, u32[]{:S(2)}) async-start(bf16[16,64,512]{2,1,0:T(8,128)(2,1)} %shard_map.107), calls=%async_computation.1 | async-start | bytes 2097152 | tf_op jit(solution)/shard_map/all_to_all | solution.py:238
  64.6 10.4 %collective-permute-start.5 = (bf16[128,512]{1,0:T(8,128)(2,1)S(1)}, bf16[128,512]{1,0:T(8,128)(2,1)S(1)}, u32[]{:S(2)}, u32[]{:S(2)}) collective-permute-start(bf16[128,512]{1,0:T(8,128)(2,1)S(1)} %get-tuple-element.19), channel_id=1, source_target_pairs={{0,128},{16,144},{32,160},{48,176},{64,192},{80,208},{96,224},{112... | collective-permute-start | bytes 393224 | tf_op jit(solution)/shard_map/ppermute | solution.py:252
  76.0 7.3 %collective-permute-start.6 = (bf16[128,512]{1,0:T(8,128)(2,1)S(1)}, bf16[128,512]{1,0:T(8,128)(2,1)S(1)}, u32[]{:S(2)}, u32[]{:S(2)}) collective-permute-start(bf16[128,512]{1,0:T(8,128)(2,1)S(1)} %fusion.2), channel_id=1, source_target_pairs={{0,64},{16,80},{32,96},{48,112},{64,0},{80,16},{96,32},{112,48},{1... | collective-permute-start | bytes 393224 | tf_op jit(solution)/shard_map/ppermute | solution.py:252
  83.3 3.4 %collective-permute-start.7 = (bf16[256,512]{1,0:T(8,128)(2,1)S(1)}, bf16[256,512]{1,0:T(8,128)(2,1)S(1)}, u32[]{:S(2)}, u32[]{:S(2)}) collective-permute-start(bf16[256,512]{1,0:T(8,128)(2,1)S(1)} %maximum_select_fusion.1), channel_id=1, source_target_pairs={{0,16},{16,0},{32,48},{48,32},{64,80},{80,64},{96,112},{112,96},{1... | collective-permute-start | bytes 786440 | tf_op jit(solution)/shard_map/ppermute | solution.py:252

commit v10 on v8

--- a/solution.py
+++ b/solution.py
@@ -24,8 +24,8 @@
 
 def grads_kernel(
     rc_ref, core_ref, xt_hbm, rt_hbm, u_hbm, v_hbm, w_hbm, r_hbm, x_hbm,
-    item_ref, send_ref, own_ref, err_ref,
-    xt_ref, rt_ref, u_ref, v_ref, w_ref, r_ref, x_ref, tag_err, sems,
+    item_hbm, send_ref, own_ref, err_ref,
+    xt_ref, rt_ref, u_ref, v_ref, w_ref, r_ref, x_ref, tag_err, item_ref, sems, out_sems,
 ):
     copies = [
         pltpu.make_async_copy(src, dst, sems.at[i])
@@ -55,17 +55,24 @@
         e = jnp.where(s < count, e, 0.0)
         err_ref[a, c] = e.astype(BF16)
     step = 256
+    leaving = []
     for i in range(0, item_ref.shape[0], step):
         rows = pl.ds(i, step)
         part = dot_cols(err_ref[:, rows], u_ref[...])
         part += jnp.dot(tag_err[rows, :], w_ref[...], preferred_element_type=F32)
         item_ref[rows, :] = part.astype(BF16)
+        leaving.append(
+            pltpu.make_async_copy(item_ref.at[rows], item_hbm.at[rows], out_sems.at[i // step])
+        )
+        leaving[-1].start()
     half = own_ref.shape[0]
     core = core_ref[0]
     mine, other = (pl.ds(pl.multiple_of(h * half, half), half) for h in (core, 1 - core))
     own_ref[...] = dot_cols(tag_err[:, mine], v_ref[...])
     part = dot_cols(tag_err[:, other], v_ref[...])
     send_ref[...] = part.astype(BF16)
+    for copy in leaving:
+        copy.wait()
 
 
 def users_kernel(err_ref, u_ref, v_ref, out_ref):
@@ -155,12 +162,14 @@
             jax.ShapeDtypeStruct((users, items), BF16),
         ),
         in_specs=[scalars()] * 2 + [in_hbm()] * 7,
-        out_specs=(whole(),) * 4,
+        out_specs=(in_hbm(),) + (whole(),) * 3,
         scratch_shapes=[pltpu.SMEM(a.shape, a.dtype) for a in (xt, rt)]
         + [pltpu.VMEM(a.shape, BF16) for a in (u, v, w, r, x)]
         + [
             pltpu.VMEM((items, tags), BF16),
+            pltpu.VMEM((items, rank), BF16),
             pltpu.SemaphoreType.DMA((7,)),
+            pltpu.SemaphoreType.DMA((items // 256,)),
         ],
         compiler_params=pltpu.CompilerParams(vmem_limit_bytes=14 << 20),
         cost_estimate=pl.CostEstimate(flops=3 << 30, bytes_accessed=6 << 20, transcendentals=0),

time: 93 us -> 92.5 us (level)
  no operation moved by 1% of the time
where the time goes in v10:
time: 92.5 us; the launch traced here: 91.4 us
  starting transfers between devices  58.2 us (63%)
  waiting for transfers between devices  19.6 us (21%)
  Pallas kernels  10 us (11%)
  other arithmetic  2.16 us (2%)
  between operations  1.47 us (2%)
    ppermute x7, starting transfers between devices, swapped(): return lax.ppermute(block, 'rot', [(i, i ^ mask) for i in range(n)])  34.4 us
    ppermute x7, waiting for transfers between devices, swapped(): return lax.ppermute(block, 'rot', [(i, i ^ mask) for i in range(n)])  18.3 us
    all_to_all x2, starting transfers between devices, exchanged(): return lax.all_to_all(pieces, axis, 0, 0)  17 us
    ppermute x1, starting transfers between devices, on_device(): lax.ppermute(shard, 'rot', [(i, (i + 1) % n_rot) for i in range(n_rot)])  6.79 us
    pallas_call x1, Pallas kernels, partials(): pl.pallas_call(grads_kernel, out_shape=(jax.ShapeDtypeStruct((items, rank...  4.93 us
  transfers between devices with their start and end apart: 10, of which 7 were waited for; matrix products, arithmetic and copies ran while one was open for 2% of the time, Pallas kernels for 3%

profile of v10, /device:TPU:1, one launch (start us, length us, event | category | flops | bytes accessed | tf_op | source)
XLA Modules:
  0.0 91.4 jit_solution(19900519950871474)
XLA Ops:
  1.3 4.9 %shard_map.103 = (bf16[1024,512]{1,0:T(8,128)(2,1)}, bf16[256,512]{1,0:T(8,128)(2,1)S(1)}, f32[256,512]{1,0:T(8,128)S(1)}, bf16[512,1024]{1,0:T(8,128)(2,1)S(1)}) custom-call(s32[1]{0:T(128)S(6)} %copy.11.rc_ref, s32[1]{0:T(128)} %bitcast.core_ref, s32[2,16]{1,0:T(2,128)} %bitcast.8, s32[2,16]{1,0:T(2,128)} %bitcast.9, bf16[512,512]{1,0:T(8,128)(2,1)} %u_ref.1, ...), custom_call_target="tpu_custom_call" | custom-call | flops 3221225472 | bytes 6291456 | tf_op jit(solution)/shard_map/pallas_call | solution.py:156
  6.2 12.0 %all-to-all-start = ((bf16[16,64,512]{2,1,0:T(8,128)(2,1)}), bf16[16,64,512]{2,1,0:T(8,128)(2,1)}, u32[]{:S(2)}, u32[]{:S(2)}) async-start(bf16[16,64,512]{2,1,0:T(8,128)(2,1)} %bitcast.4), calls=%async_computation | async-start | bytes 2097152 | tf_op jit(solution)/shard_map/all_to_all | solution.py:247
  18.2 2.9 %collective-permute-start = (bf16[256,512]{1,0:T(8,128)(2,1)S(1)}, bf16[256,512]{1,0:T(8,128)(2,1)S(1)}, u32[]{:S(2)}, u32[]{:S(2)}) collective-permute-start(bf16[256,512]{1,0:T(8,128)(2,1)S(1)} %get-tuple-element.14), channel_id=1, source_target_pairs={{0,16},{16,0},{32,48},{48,32},{64,80},{80,64},{96,112},{112,96},{1... | collective-permute-start | bytes 786440 | tf_op jit(solution)/shard_map/ppermute | solution.py:261
  21.1 1.1 %collective-permute-done.arrived_ref = bf16[256,512]{1,0:T(8,128)(2,1)S(1)} collective-permute-done((bf16[256,512]{1,0:T(8,128)(2,1)S(1)}, bf16[256,512]{1,0:T(8,128)(2,1)S(1)}, u32[]{:S(2)}, u32[]{:S(2)}) %collective-permute-start) | collective-permute-done | bytes 262176 | tf_op jit(solution)/shard_map/ppermute | solution.py:261
  22.2 0.0 copy-start
  22.3 3.3 %collective-permute-start.1 = (bf16[128,512]{1,0:T(8,128)(2,1)S(1)}, bf16[128,512]{1,0:T(8,128)(2,1)S(1)}, u32[]{:S(2)}, u32[]{:S(2)}) collective-permute-start(bf16[128,512]{1,0:T(8,128)(2,1)S(1)} %get-tuple-element.16), channel_id=1, source_target_pairs={{0,64},{16,80},{32,96},{48,112},{64,0},{80,16},{96,32},{112,48},{1... | collective-permute-start | bytes 393224 | tf_op jit(solution)/shard_map/ppermute | solution.py:261
  25.6 3.5 %collective-permute-done.1 = bf16[128,512]{1,0:T(8,128)(2,1)S(1)} collective-permute-done((bf16[128,512]{1,0:T(8,128)(2,1)S(1)}, bf16[128,512]{1,0:T(8,128)(2,1)S(1)}, u32[]{:S(2)}, u32[]{:S(2)}) %collective-permute-start.1) | collective-permute-done | bytes 131104 | tf_op jit(solution)/shard_map/ppermute | solution.py:261
  29.1 0.0 copy-start.1
  29.1 4.4 %collective-permute-start.2 = (bf16[128,512]{1,0:T(8,128)(2,1)S(1)}, bf16[128,512]{1,0:T(8,128)(2,1)S(1)}, u32[]{:S(2)}, u32[]{:S(2)}) collective-permute-start(bf16[128,512]{1,0:T(8,128)(2,1)S(1)} %fusion.3), channel_id=1, source_target_pairs={{0,128},{16,144},{32,160},{48,176},{64,192},{80,208},{96,224},{112... | collective-permute-start | bytes 393224 | tf_op jit(solution)/shard_map/ppermute | solution.py:261
  33.5 5.8 %collective-permute-done.2 = bf16[128,512]{1,0:T(8,128)(2,1)S(1)} collective-permute-done((bf16[128,512]{1,0:T(8,128)(2,1)S(1)}, bf16[128,512]{1,0:T(8,128)(2,1)S(1)}, u32[]{:S(2)}, u32[]{:S(2)}) %collective-permute-start.2) | collective-permute-done | bytes 131104 | tf_op jit(solution)/shard_map/ppermute | solution.py:261
  39.3 0.1 reduce-precision_convert_fusion.1
  39.4 4.4 %collective-permute-start.4 = (bf16[128,512]{1,0:T(8,128)(2,1)S(1)}, bf16[128,512]{1,0:T(8,128)(2,1)S(1)}, u32[]{:S(2)}, u32[]{:S(2)}) collective-permute-start(bf16[128,512]{1,0:T(8,128)(2,1)S(1)} %get-tuple-element.21), channel_id=1, source_target_pairs={{0,32},{16,48},{32,0},{48,16},{64,96},{80,112},{96,64},{112,80},{1... | collective-permute-start | bytes 393224 | tf_op jit(solution)/shard_map/ppermute | solution.py:261
  43.7 0.0 copy-done
  43.8 0.0 copy-done.1
  43.8 1.6 %shard_map.104 = bf16[512,512]{1,0:T(8,128)(2,1)} custom-call(bf16[512,1024]{1,0:T(8,128)(2,1)S(1)} %get-tuple-element.11.err_ref, bf16[512,512]{1,0:T(8,128)(2,1)S(1)} %copy-done.1, bf16[1024,512]{1,0:T(8,128)(2,1)S(1)} %copy-done), custom_call_target="tpu_custom_call" | custom-call | flops 1073741824 | bytes 4194304 | tf_op jit(solution)/shard_map/pallas_call | solution.py:180
  45.3 0.0 all-to-all-done.pieces_hbm
  45.3 1.3 %shard_map.106 = bf16[64,512]{1,0:T(8,128)(2,1)S(1)} custom-call(s32[1]{0:T(128)} %bitcast.3.tag_ref, bf16[1024,512]{1,0:T(8,128)(2,1)} %v_hbm.3, bf16[16,64,512]{2,1,0:T(8,128)(2,1)} %all-to-all-done.pieces_hbm), custom_call_target="tpu_custom_call" | custom-call | flops 524288 | bytes 1048576 | tf_op jit(solution)/shard_map/pallas_call | solution.py:207
  46.6 6.8 %collective-permute-start.3 = (bf16[64,512]{1,0:T(8,128)(2,1)S(1)}, bf16[64,512]{1,0:T(8,128)(2,1)S(1)}, u32[]{:S(2)}, u32[]{:S(2)}) collective-permute-start(bf16[64,512]{1,0:T(8,128)(2,1)S(1)} %shard_map.106), channel_id=1, source_target_pairs={{0,16},{16,32},{32,48},{48,64},{64,80},{80,96},{96,112},{112,128},... | collective-permute-start | bytes 196616 | tf_op jit(solution)/shard_map/ppermute | solution.py:299
  53.4 0.0 collective-permute-done.4
  53.5 1.3 %collective-permute-done.3.shard_ref = bf16[64,512]{1,0:T(8,128)(2,1)S(1)} collective-permute-done((bf16[64,512]{1,0:T(8,128)(2,1)S(1)}, bf16[64,512]{1,0:T(8,128)(2,1)S(1)}, u32[]{:S(2)}, u32[]{:S(2)}) %collective-permute-start.3) | collective-permute-done | bytes 65568 | tf_op jit(solution)/shard_map/ppermute | solution.py:299
  54.7 1.1 %shard_map.107 = bf16[16,64,512]{2,1,0:T(8,128)(2,1)} custom-call(bf16[64,512]{1,0:T(8,128)(2,1)S(1)} %collective-permute-done.3.shard_ref), custom_call_target="tpu_custom_call" | custom-call | bytes 1048576 | tf_op jit(solution)/shard_map/pallas_call | solution.py:223
  55.8 5.1 %all-to-all-start.1 = ((bf16[16,64,512]{2,1,0:T(8,128)(2,1)}), bf16[16,64,512]{2,1,0:T(8,128)(2,1)S(1)}, u32[]{:S(2)}, u32[]{:S(2)}) async-start(bf16[16,64,512]{2,1,0:T(8,128)(2,1)} %shard_map.107), calls=%async_computation.1 | async-start | bytes 2097152 | tf_op jit(solution)/shard_map/all_to_all | solution.py:247
  60.9 7.5 %collective-permute-start.5 = (bf16[128,512]{1,0:T(8,128)(2,1)S(1)}, bf16[128,512]{1,0:T(8,128)(2,1)S(1)}, u32[]{:S(2)}, u32[]{:S(2)}) collective-permute-start(bf16[128,512]{1,0:T(8,128)(2,1)S(1)} %get-tuple-element.19), channel_id=1, source_target_pairs={{0,256},{16,272},{32,288},{48,304},{64,320},{80,336},{96,352},{112... | collective-permute-start | bytes 393224 | tf_op jit(solution)/shard_map/ppermute | solution.py:261
  68.4 2.4 %collective-permute-done.5 = bf16[128,512]{1,0:T(8,128)(2,1)S(1)} collective-permute-done((bf16[128,512]{1,0:T(8,128)(2,1)S(1)}, bf16[128,512]{1,0:T(8,128)(2,1)S(1)}, u32[]{:S(2)}, u32[]{:S(2)}) %collective-permute-start.5) | collective-permute-done | bytes 131104 | tf_op jit(solution)/shard_map/ppermute | solution.py:261
  70.8 1.0 %fusion.2 = bf16[128,512]{1,0:T(8,128)(2,1)S(1)} fusion(bf16[128,512]{1,0:T(8,128)(2,1)S(1)} %collective-permute-done.5, f32[128,512]{1,0:T(8,128)S(1)} %get-tuple-element.20, bf16[512,512]{1,0:T(8,128)(2,1)} %w_hbm.1, s32[]{:T(128)S(6)} %select_n.21), kind=kLoop, calls=%fused_computation.5 | loop fusion | flops 589824 | bytes 655364 | tf_op jit(solution)/shard_map/convert_element_type | solution.py:252
  71.8 2.1 %collective-permute-start.6 = (bf16[128,512]{1,0:T(8,128)(2,1)S(1)}, bf16[128,512]{1,0:T(8,128)(2,1)S(1)}, u32[]{:S(2)}, u32[]{:S(2)}) collective-permute-start(bf16[128,512]{1,0:T(8,128)(2,1)S(1)} %fusion.2), channel_id=1, source_target_pairs={{0,64},{16,80},{32,96},{48,112},{64,0},{80,16},{96,32},{112,48},{1... | collective-permute-start | bytes 393224 | tf_op jit(solution)/shard_map/ppermute | solution.py:261
  73.9 4.3 %collective-permute-done.6 = bf16[128,512]{1,0:T(8,128)(2,1)S(1)} collective-permute-done((bf16[128,512]{1,0:T(8,128)(2,1)S(1)}, bf16[128,512]{1,0:T(8,128)(2,1)S(1)}, u32[]{:S(2)}, u32[]{:S(2)}) %collective-permute-start.6) | collective-permute-done | bytes 131104 | tf_op jit(solution)/shard_map/ppermute | solution.py:261
  78.2 0.1 maximum_select_fusion.1
  78.3 9.9 %collective-permute-start.7 = (bf16[256,512]{1,0:T(8,128)(2,1)S(1)}, bf16[256,512]{1,0:T(8,128)(2,1)S(1)}, u32[]{:S(2)}, u32[]{:S(2)}) collective-permute-start(bf16[256,512]{1,0:T(8,128)(2,1)S(1)} %maximum_select_fusion.1), channel_id=1, source_target_pairs={{0,16},{16,0},{32,48},{48,32},{64,80},{80,64},{96,112},{112,96},{1... | collective-permute-start | bytes 786440 | tf_op jit(solution)/shard_map/ppermute | solution.py:261
  88.2 1.1 %collective-permute-done.7 = bf16[256,512]{1,0:T(8,128)(2,1)S(1)} collective-permute-done((bf16[256,512]{1,0:T(8,128)(2,1)S(1)}, bf16[256,512]{1,0:T(8,128)(2,1)S(1)}, u32[]{:S(2)}, u32[]{:S(2)}) %collective-permute-start.7) | collective-permute-done | bytes 262176 | tf_op jit(solution)/shard_map/ppermute | solution.py:261
  89.3 1.0 %maximum_select_fusion = bf16[512,512]{1,0:T(8,128)(2,1)} fusion(bf16[256,512]{1,0:T(8,128)(2,1)S(1)} %collective-permute-done.7, bf16[256,512]{1,0:T(8,128)(2,1)S(1)} %maximum_select_fusion.1, pred[]{:T(512)S(6)} %eq.6), kind=kLoop, calls=%fused_computation | loop fusion | flops 2359296 | bytes 1048577 | tf_op jit(solution)/shard_map/jit(_where)/select_n | solution.py:265
  90.3 0.0 all-to-all-done.1.in_ref
  90.3 1.1 %shard_map.108 = bf16[16,64,512]{2,1,0:T(8,128)(2,1)} custom-call(bf16[16,64,512]{2,1,0:T(8,128)(2,1)S(1)} %all-to-all-done.1.in_ref), custom_call_target="tpu_custom_call" | custom-call | bytes 2097152 | tf_op jit(solution)/shard_map/pallas_call | solution.py:235
  (3 shorter events, 0.1 us)
Async XLA Ops:
  6.2 39.1 %all-to-all-start = ((bf16[16,64,512]{2,1,0:T(8,128)(2,1)}), bf16[16,64,512]{2,1,0:T(8,128)(2,1)}, u32[]{:S(2)}, u32[]{:S(2)}) async-start(bf16[16,64,512]{2,1,0:T(8,128)(2,1)} %bitcast.4), calls=%async_computation | async-start | bytes 2097152 | tf_op jit(solution)/shard_map/all_to_all | solution.py:247
  18.2 4.0 %collective-permute-start = (bf16[256,512]{1,0:T(8,128)(2,1)S(1)}, bf16[256,512]{1,0:T(8,128)(2,1)S(1)}, u32[]{:S(2)}, u32[]{:S(2)}) collective-permute-start(bf16[256,512]{1,0:T(8,128)(2,1)S(1)} %get-tuple-element.14), channel_id=1, source_target_pairs={{0,16},{16,0},{32,48},{48,32},{64,80},{80,64},{96,112},{112,96},{1... | collective-permute-start | bytes 786440 | tf_op jit(solution)/shard_map/ppermute | solution.py:261
  22.2 21.5 %copy-start = (bf16[1024,512]{1,0:T(8,128)(2,1)S(1)}, bf16[1024,512]{1,0:T(8,128)(2,1)}, u32[]{:S(2)}) copy-start(bf16[1024,512]{1,0:T(8,128)(2,1)} %v_hbm.3) | copy-start | bytes 3145732
  22.3 6.8 %collective-permute-start.1 = (bf16[128,512]{1,0:T(8,128)(2,1)S(1)}, bf16[128,512]{1,0:T(8,128)(2,1)S(1)}, u32[]{:S(2)}, u32[]{:S(2)}) collective-permute-start(bf16[128,512]{1,0:T(8,128)(2,1)S(1)} %get-tuple-element.16), channel_id=1, source_target_pairs={{0,64},{16,80},{32,96},{48,112},{64,0},{80,16},{96,32},{112,48},{1... | collective-permute-start | bytes 393224 | tf_op jit(solution)/shard_map/ppermute | solution.py:261
  29.1 14.6 %copy-start.1 = (bf16[512,512]{1,0:T(8,128)(2,1)S(1)}, bf16[512,512]{1,0:T(8,128)(2,1)}, u32[]{:S(2)}) copy-start(bf16[512,512]{1,0:T(8,128)(2,1)} %u_ref.1) | copy-start | bytes 1572868
  29.1 10.2 %collective-permute-start.2 = (bf16[128,512]{1,0:T(8,128)(2,1)S(1)}, bf16[128,512]{1,0:T(8,128)(2,1)S(1)}, u32[]{:S(2)}, u32[]{:S(2)}) collective-permute-start(bf16[128,512]{1,0:T(8,128)(2,1)S(1)} %fusion.3), channel_id=1, source_target_pairs={{0,128},{16,144},{32,160},{48,176},{64,192},{80,208},{96,224},{112... | collective-permute-start | bytes 393224 | tf_op jit(solution)/shard_map/ppermute | solution.py:261
  39.4 14.1 %collective-permute-start.4 = (bf16[128,512]{1,0:T(8,128)(2,1)S(1)}, bf16[128,512]{1,0:T(8,128)(2,1)S(1)}, u32[]{:S(2)}, u32[]{:S(2)}) collective-permute-start(bf16[128,512]{1,0:T(8,128)(2,1)S(1)} %get-tuple-element.21), channel_id=1, source_target_pairs={{0,32},{16,48},{32,0},{48,16},{64,96},{80,112},{96,64},{112,80},{1... | collective-permute-start | bytes 393224 | tf_op jit(solution)/shard_map/ppermute | solution.py:261
  46.6 8.1 %collective-permute-start.3 = (bf16[64,512]{1,0:T(8,128)(2,1)S(1)}, bf16[64,512]{1,0:T(8,128)(2,1)S(1)}, u32[]{:S(2)}, u32[]{:S(2)}) collective-permute-start(bf16[64,512]{1,0:T(8,128)(2,1)S(1)} %shard_map.106), channel_id=1, source_target_pairs={{0,16},{16,32},{32,48},{48,64},{64,80},{80,96},{96,112},{112,128},... | collective-permute-start | bytes 196616 | tf_op jit(solution)/shard_map/ppermute | solution.py:299
  55.8 34.5 %all-to-all-start.1 = ((bf16[16,64,512]{2,1,0:T(8,128)(2,1)}), bf16[16,64,512]{2,1,0:T(8,128)(2,1)S(1)}, u32[]{:S(2)}, u32[]{:S(2)}) async-start(bf16[16,64,512]{2,1,0:T(8,128)(2,1)} %shard_map.107), calls=%async_computation.1 | async-start | bytes 2097152 | tf_op jit(solution)/shard_map/all_to_all | solution.py:247
  60.9 9.9 %collective-permute-start.5 = (bf16[128,512]{1,0:T(8,128)(2,1)S(1)}, bf16[128,512]{1,0:T(8,128)(2,1)S(1)}, u32[]{:S(2)}, u32[]{:S(2)}) collective-permute-start(bf16[128,512]{1,0:T(8,128)(2,1)S(1)} %get-tuple-element.19), channel_id=1, source_target_pairs={{0,256},{16,272},{32,288},{48,304},{64,320},{80,336},{96,352},{112... | collective-permute-start | bytes 393224 | tf_op jit(solution)/shard_map/ppermute | solution.py:261
  71.8 6.5 %collective-permute-start.6 = (bf16[128,512]{1,0:T(8,128)(2,1)S(1)}, bf16[128,512]{1,0:T(8,128)(2,1)S(1)}, u32[]{:S(2)}, u32[]{:S(2)}) collective-permute-start(bf16[128,512]{1,0:T(8,128)(2,1)S(1)} %fusion.2), channel_id=1, source_target_pairs={{0,64},{16,80},{32,96},{48,112},{64,0},{80,16},{96,32},{112,48},{1... | collective-permute-start | bytes 393224 | tf_op jit(solution)/shard_map/ppermute | solution.py:261
  78.3 11.0 %collective-permute-start.7 = (bf16[256,512]{1,0:T(8,128)(2,1)S(1)}, bf16[256,512]{1,0:T(8,128)(2,1)S(1)}, u32[]{:S(2)}, u32[]{:S(2)}) collective-permute-start(bf16[256,512]{1,0:T(8,128)(2,1)S(1)} %maximum_select_fusion.1), channel_id=1, source_target_pairs={{0,16},{16,0},{32,48},{48,32},{64,80},{80,64},{96,112},{112,96},{1... | collective-permute-start | bytes 786440 | tf_op jit(solution)/shard_map/ppermute | solution.py:261

commit v11 on v10

--- a/solution.py
+++ b/solution.py
@@ -138,6 +138,17 @@
         copy.wait()
 
 
+def join_kernel(bit_ref, mine_ref, other_ref, out_hbm, sems):
+    size = mine_ref.shape[0]
+    copies = []
+    for k, (ref, index) in enumerate([(mine_ref, bit_ref[0]), (other_ref, 1 - bit_ref[0])]):
+        rows = pl.ds(pl.multiple_of(index * size, size), size)
+        copies.append(pltpu.make_async_copy(ref, out_hbm.at[rows], sems.at[k]))
+        copies[-1].start()
+    for copy in copies:
+        copy.wait()
+
+
 def whole():
     return pl.BlockSpec(memory_space=pltpu.VMEM)
 
@@ -243,6 +254,19 @@
     )(pieces)
 
 
+def placed_halves(bit, mine, other):
+    size, rank = mine.shape
+    return pl.pallas_call(
+        join_kernel,
+        out_shape=jax.ShapeDtypeStruct((2 * size, rank), BF16),
+        in_specs=[scalars(), whole(), whole()],
+        out_specs=in_hbm(),
+        scratch_shapes=[pltpu.SemaphoreType.DMA((2,))],
+        compiler_params=pltpu.CompilerParams(vmem_limit_bytes=2 << 20),
+        cost_estimate=pl.CostEstimate(flops=0, bytes_accessed=1 << 20, transcendentals=0),
+    )(bit, mine, other)
+
+
 def exchanged(pieces, axis):
     return lax.all_to_all(pieces, axis, 0, 0)
 
@@ -280,7 +304,7 @@
 def new_tag_rows(total, w, core, y_bit):
     shard = updated(part_of(w, core * 2 + y_bit, total.shape[0]), total)
     half = joined(shard, swapped(shard, 4), y_bit)
-    return joined(half, swapped(half, 1), core)
+    return placed_halves(core[None], half, swapped(half, 1))
 
 
 def on_device(u, v, w, rating_tiles, rating_counts, ratings, tag_tiles, tag_values):

time: 92.5 us -> 92.5 us (level)
  other arithmetic: 2.16 us -> 1.15 us
    select_n x2 -> x1, other arithmetic: 1.06 us -> 0.06 us  [joined(): jnp.where(bit == 0, jnp.concatenate([mine, other], 0), jnp.concatenate([o...]
  transfers between devices with their start and end apart: 10 -> 10, of which waited for: 7 -> 7; matrix products, arithmetic and copies ran while one was open for 2% -> 1% of each run, Pallas kernels for 3% -> 4%
where the time goes in v11:
time: 92.5 us; the launch traced here: 91.2 us
  starting transfers between devices  58.1 us (63%)
  waiting for transfers between devices  19.6 us (21%)
  Pallas kernels  10.8 us (12%)
  between operations  1.49 us (2%)
  other arithmetic  1.15 us (1%)
    ppermute x7, starting transfers between devices, swapped(): return lax.ppermute(block, 'rot', [(i, i ^ mask) for i in range(n)])  34.3 us
    ppermute x7, waiting for transfers between devices, swapped(): return lax.ppermute(block, 'rot', [(i, i ^ mask) for i in range(n)])  18.3 us
    all_to_all x2, starting transfers between devices, exchanged(): return lax.all_to_all(pieces, axis, 0, 0)  17 us
    ppermute x1, starting transfers between devices, on_device(): lax.ppermute(shard, 'rot', [(i, (i + 1) % n_rot) for i in range(n_rot)])  6.79 us
    pallas_call x1, Pallas kernels, partials(): pl.pallas_call(grads_kernel, out_shape=(jax.ShapeDtypeStruct((items, rank...  4.94 us
  transfers between devices with their start and end apart: 10, of which 7 were waited for; matrix products, arithmetic and copies ran while one was open for 1% of the time, Pallas kernels for 4%

profile of v11, /device:TPU:1, one launch (start us, length us, event | category | flops | bytes accessed | tf_op | source)
XLA Modules:
  0.0 91.2 jit_solution(2983777969287218503)
XLA Ops:
  1.3 4.9 %shard_map.103 = (bf16[1024,512]{1,0:T(8,128)(2,1)}, bf16[256,512]{1,0:T(8,128)(2,1)S(1)}, f32[256,512]{1,0:T(8,128)S(1)}, bf16[512,1024]{1,0:T(8,128)(2,1)S(1)}) custom-call(s32[1]{0:T(128)S(6)} %copy.11.rc_ref, s32[1]{0:T(128)} %bitcast.core_ref.bit_ref, s32[2,16]{1,0:T(2,128)} %bitcast.8, s32[2,16]{1,0:T(2,128)} %bitcast.9, bf16[512,512]{1,0:T(8,128)(2,1)} %u_ref.1, ...), custom_call_target="tpu_custom_call" | custom-call | flops 3221225472 | bytes 6291456 | tf_op jit(solution)/shard_map/pallas_call | solution.py:167
  6.2 12.0 %all-to-all-start = ((bf16[16,64,512]{2,1,0:T(8,128)(2,1)}), bf16[16,64,512]{2,1,0:T(8,128)(2,1)}, u32[]{:S(2)}, u32[]{:S(2)}) async-start(bf16[16,64,512]{2,1,0:T(8,128)(2,1)} %bitcast.4), calls=%async_computation | async-start | bytes 2097152 | tf_op jit(solution)/shard_map/all_to_all | solution.py:271
  18.2 2.9 %collective-permute-start = (bf16[256,512]{1,0:T(8,128)(2,1)S(1)}, bf16[256,512]{1,0:T(8,128)(2,1)S(1)}, u32[]{:S(2)}, u32[]{:S(2)}) collective-permute-start(bf16[256,512]{1,0:T(8,128)(2,1)S(1)} %get-tuple-element.14), channel_id=1, source_target_pairs={{0,16},{16,0},{32,48},{48,32},{64,80},{80,64},{96,112},{112,96},{1... | collective-permute-start | bytes 786440 | tf_op jit(solution)/shard_map/ppermute | solution.py:285
  21.1 1.1 %collective-permute-done.arrived_ref = bf16[256,512]{1,0:T(8,128)(2,1)S(1)} collective-permute-done((bf16[256,512]{1,0:T(8,128)(2,1)S(1)}, bf16[256,512]{1,0:T(8,128)(2,1)S(1)}, u32[]{:S(2)}, u32[]{:S(2)}) %collective-permute-start) | collective-permute-done | bytes 262176 | tf_op jit(solution)/shard_map/ppermute | solution.py:285
  22.2 0.0 copy-start
  22.3 3.3 %collective-permute-start.1 = (bf16[128,512]{1,0:T(8,128)(2,1)S(1)}, bf16[128,512]{1,0:T(8,128)(2,1)S(1)}, u32[]{:S(2)}, u32[]{:S(2)}) collective-permute-start(bf16[128,512]{1,0:T(8,128)(2,1)S(1)} %get-tuple-element.16), channel_id=1, source_target_pairs={{0,64},{16,80},{32,96},{48,112},{64,0},{80,16},{96,32},{112,48},{1... | collective-permute-start | bytes 393224 | tf_op jit(solution)/shard_map/ppermute | solution.py:285
  25.6 3.5 %collective-permute-done.1 = bf16[128,512]{1,0:T(8,128)(2,1)S(1)} collective-permute-done((bf16[128,512]{1,0:T(8,128)(2,1)S(1)}, bf16[128,512]{1,0:T(8,128)(2,1)S(1)}, u32[]{:S(2)}, u32[]{:S(2)}) %collective-permute-start.1) | collective-permute-done | bytes 131104 | tf_op jit(solution)/shard_map/ppermute | solution.py:285
  29.1 0.0 copy-start.1
  29.1 4.3 %collective-permute-start.2 = (bf16[128,512]{1,0:T(8,128)(2,1)S(1)}, bf16[128,512]{1,0:T(8,128)(2,1)S(1)}, u32[]{:S(2)}, u32[]{:S(2)}) collective-permute-start(bf16[128,512]{1,0:T(8,128)(2,1)S(1)} %fusion.3), channel_id=1, source_target_pairs={{0,128},{16,144},{32,160},{48,176},{64,192},{80,208},{96,224},{112... | collective-permute-start | bytes 393224 | tf_op jit(solution)/shard_map/ppermute | solution.py:285
  33.5 5.8 %collective-permute-done.2 = bf16[128,512]{1,0:T(8,128)(2,1)S(1)} collective-permute-done((bf16[128,512]{1,0:T(8,128)(2,1)S(1)}, bf16[128,512]{1,0:T(8,128)(2,1)S(1)}, u32[]{:S(2)}, u32[]{:S(2)}) %collective-permute-start.2) | collective-permute-done | bytes 131104 | tf_op jit(solution)/shard_map/ppermute | solution.py:285
  39.3 0.1 reduce-precision_convert_fusion.1
  39.4 4.4 %collective-permute-start.4 = (bf16[128,512]{1,0:T(8,128)(2,1)S(1)}, bf16[128,512]{1,0:T(8,128)(2,1)S(1)}, u32[]{:S(2)}, u32[]{:S(2)}) collective-permute-start(bf16[128,512]{1,0:T(8,128)(2,1)S(1)} %get-tuple-element.21), channel_id=1, source_target_pairs={{0,32},{16,48},{32,0},{48,16},{64,96},{80,112},{96,64},{112,80},{1... | collective-permute-start | bytes 393224 | tf_op jit(solution)/shard_map/ppermute | solution.py:285
  43.7 0.0 copy-done
  43.8 0.0 copy-done.1
  43.8 1.6 %shard_map.104 = bf16[512,512]{1,0:T(8,128)(2,1)} custom-call(bf16[512,1024]{1,0:T(8,128)(2,1)S(1)} %get-tuple-element.11.err_ref, bf16[512,512]{1,0:T(8,128)(2,1)S(1)} %copy-done.1, bf16[1024,512]{1,0:T(8,128)(2,1)S(1)} %copy-done), custom_call_target="tpu_custom_call" | custom-call | flops 1073741824 | bytes 4194304 | tf_op jit(solution)/shard_map/pallas_call | solution.py:191
  45.3 0.0 all-to-all-done.pieces_hbm
  45.3 1.3 %shard_map.106 = bf16[64,512]{1,0:T(8,128)(2,1)S(1)} custom-call(s32[1]{0:T(128)} %bitcast.3.tag_ref, bf16[1024,512]{1,0:T(8,128)(2,1)} %v_hbm.3, bf16[16,64,512]{2,1,0:T(8,128)(2,1)} %all-to-all-done.pieces_hbm), custom_call_target="tpu_custom_call" | custom-call | flops 524288 | bytes 1048576 | tf_op jit(solution)/shard_map/pallas_call | solution.py:218
  46.6 6.8 %collective-permute-start.3 = (bf16[64,512]{1,0:T(8,128)(2,1)S(1)}, bf16[64,512]{1,0:T(8,128)(2,1)S(1)}, u32[]{:S(2)}, u32[]{:S(2)}) collective-permute-start(bf16[64,512]{1,0:T(8,128)(2,1)S(1)} %shard_map.106), channel_id=1, source_target_pairs={{0,16},{16,32},{32,48},{48,64},{64,80},{80,96},{96,112},{112,128},... | collective-permute-start | bytes 196616 | tf_op jit(solution)/shard_map/ppermute | solution.py:323
  53.4 0.0 collective-permute-done.4
  53.5 1.3 %collective-permute-done.3.shard_ref = bf16[64,512]{1,0:T(8,128)(2,1)S(1)} collective-permute-done((bf16[64,512]{1,0:T(8,128)(2,1)S(1)}, bf16[64,512]{1,0:T(8,128)(2,1)S(1)}, u32[]{:S(2)}, u32[]{:S(2)}) %collective-permute-start.3) | collective-permute-done | bytes 65568 | tf_op jit(solution)/shard_map/ppermute | solution.py:323
  54.8 1.1 %shard_map.107 = bf16[16,64,512]{2,1,0:T(8,128)(2,1)} custom-call(bf16[64,512]{1,0:T(8,128)(2,1)S(1)} %collective-permute-done.3.shard_ref), custom_call_target="tpu_custom_call" | custom-call | bytes 1048576 | tf_op jit(solution)/shard_map/pallas_call | solution.py:234
  55.8 5.0 %all-to-all-start.1 = ((bf16[16,64,512]{2,1,0:T(8,128)(2,1)}), bf16[16,64,512]{2,1,0:T(8,128)(2,1)S(1)}, u32[]{:S(2)}, u32[]{:S(2)}) async-start(bf16[16,64,512]{2,1,0:T(8,128)(2,1)} %shard_map.107), calls=%async_computation.1 | async-start | bytes 2097152 | tf_op jit(solution)/shard_map/all_to_all | solution.py:271
  60.9 7.5 %collective-permute-start.5 = (bf16[128,512]{1,0:T(8,128)(2,1)S(1)}, bf16[128,512]{1,0:T(8,128)(2,1)S(1)}, u32[]{:S(2)}, u32[]{:S(2)}) collective-permute-start(bf16[128,512]{1,0:T(8,128)(2,1)S(1)} %get-tuple-element.19), channel_id=1, source_target_pairs={{0,256},{16,272},{32,288},{48,304},{64,320},{80,336},{96,352},{112... | collective-permute-start | bytes 393224 | tf_op jit(solution)/shard_map/ppermute | solution.py:285
  68.4 2.4 %collective-permute-done.5 = bf16[128,512]{1,0:T(8,128)(2,1)S(1)} collective-permute-done((bf16[128,512]{1,0:T(8,128)(2,1)S(1)}, bf16[128,512]{1,0:T(8,128)(2,1)S(1)}, u32[]{:S(2)}, u32[]{:S(2)}) %collective-permute-start.5) | collective-permute-done | bytes 131104 | tf_op jit(solution)/shard_map/ppermute | solution.py:285
  70.8 1.0 %fusion.2 = bf16[128,512]{1,0:T(8,128)(2,1)S(1)} fusion(bf16[128,512]{1,0:T(8,128)(2,1)S(1)} %collective-permute-done.5, f32[128,512]{1,0:T(8,128)S(1)} %get-tuple-element.20, bf16[512,512]{1,0:T(8,128)(2,1)} %w_hbm.1, s32[]{:T(128)S(6)} %select_n.12), kind=kLoop, calls=%fused_computation.4 | loop fusion | flops 589824 | bytes 655364 | tf_op jit(solution)/shard_map/convert_element_type | solution.py:276
  71.8 2.1 %collective-permute-start.6 = (bf16[128,512]{1,0:T(8,128)(2,1)S(1)}, bf16[128,512]{1,0:T(8,128)(2,1)S(1)}, u32[]{:S(2)}, u32[]{:S(2)}) collective-permute-start(bf16[128,512]{1,0:T(8,128)(2,1)S(1)} %fusion.2), channel_id=1, source_target_pairs={{0,64},{16,80},{32,96},{48,112},{64,0},{80,16},{96,32},{112,48},{1... | collective-permute-start | bytes 393224 | tf_op jit(solution)/shard_map/ppermute | solution.py:285
  73.9 4.3 %collective-permute-done.6 = bf16[128,512]{1,0:T(8,128)(2,1)S(1)} collective-permute-done((bf16[128,512]{1,0:T(8,128)(2,1)S(1)}, bf16[128,512]{1,0:T(8,128)(2,1)S(1)}, u32[]{:S(2)}, u32[]{:S(2)}) %collective-permute-start.6) | collective-permute-done | bytes 131104 | tf_op jit(solution)/shard_map/ppermute | solution.py:285
  78.2 0.1 maximum_select_fusion.mine_ref
  78.3 9.9 %collective-permute-start.7 = (bf16[256,512]{1,0:T(8,128)(2,1)S(1)}, bf16[256,512]{1,0:T(8,128)(2,1)S(1)}, u32[]{:S(2)}, u32[]{:S(2)}) collective-permute-start(bf16[256,512]{1,0:T(8,128)(2,1)S(1)} %maximum_select_fusion.mine_ref), channel_id=1, source_target_pairs={{0,16},{16,0},{32,48},{48,32},{64,80},{80,64},{96,112},{112,96},{1... | collective-permute-start | bytes 786440 | tf_op jit(solution)/shard_map/ppermute | solution.py:285
  88.2 1.1 %collective-permute-done.7.other_ref = bf16[256,512]{1,0:T(8,128)(2,1)S(1)} collective-permute-done((bf16[256,512]{1,0:T(8,128)(2,1)S(1)}, bf16[256,512]{1,0:T(8,128)(2,1)S(1)}, u32[]{:S(2)}, u32[]{:S(2)}) %collective-permute-start.7) | collective-permute-done | bytes 262176 | tf_op jit(solution)/shard_map/ppermute | solution.py:285
  89.3 0.8 shard_map.109
  90.1 0.0 all-to-all-done.1.in_ref
  90.1 1.1 %shard_map.108 = bf16[16,64,512]{2,1,0:T(8,128)(2,1)} custom-call(bf16[16,64,512]{2,1,0:T(8,128)(2,1)S(1)} %all-to-all-done.1.in_ref), custom_call_target="tpu_custom_call" | custom-call | bytes 2097152 | tf_op jit(solution)/shard_map/pallas_call | solution.py:246
  (3 shorter events, 0.1 us)
Async XLA Ops:
  6.2 39.1 %all-to-all-start = ((bf16[16,64,512]{2,1,0:T(8,128)(2,1)}), bf16[16,64,512]{2,1,0:T(8,128)(2,1)}, u32[]{:S(2)}, u32[]{:S(2)}) async-start(bf16[16,64,512]{2,1,0:T(8,128)(2,1)} %bitcast.4), calls=%async_computation | async-start | bytes 2097152 | tf_op jit(solution)/shard_map/all_to_all | solution.py:271
  18.2 4.0 %collective-permute-start = (bf16[256,512]{1,0:T(8,128)(2,1)S(1)}, bf16[256,512]{1,0:T(8,128)(2,1)S(1)}, u32[]{:S(2)}, u32[]{:S(2)}) collective-permute-start(bf16[256,512]{1,0:T(8,128)(2,1)S(1)} %get-tuple-element.14), channel_id=1, source_target_pairs={{0,16},{16,0},{32,48},{48,32},{64,80},{80,64},{96,112},{112,96},{1... | collective-permute-start | bytes 786440 | tf_op jit(solution)/shard_map/ppermute | solution.py:285
  22.2 21.6 %copy-start = (bf16[1024,512]{1,0:T(8,128)(2,1)S(1)}, bf16[1024,512]{1,0:T(8,128)(2,1)}, u32[]{:S(2)}) copy-start(bf16[1024,512]{1,0:T(8,128)(2,1)} %v_hbm.3) | copy-start | bytes 3145732
  22.3 6.8 %collective-permute-start.1 = (bf16[128,512]{1,0:T(8,128)(2,1)S(1)}, bf16[128,512]{1,0:T(8,128)(2,1)S(1)}, u32[]{:S(2)}, u32[]{:S(2)}) collective-permute-start(bf16[128,512]{1,0:T(8,128)(2,1)S(1)} %get-tuple-element.16), channel_id=1, source_target_pairs={{0,64},{16,80},{32,96},{48,112},{64,0},{80,16},{96,32},{112,48},{1... | collective-permute-start | bytes 393224 | tf_op jit(solution)/shard_map/ppermute | solution.py:285
  29.1 14.6 %copy-start.1 = (bf16[512,512]{1,0:T(8,128)(2,1)S(1)}, bf16[512,512]{1,0:T(8,128)(2,1)}, u32[]{:S(2)}) copy-start(bf16[512,512]{1,0:T(8,128)(2,1)} %u_ref.1) | copy-start | bytes 1572868
  29.1 10.2 %collective-permute-start.2 = (bf16[128,512]{1,0:T(8,128)(2,1)S(1)}, bf16[128,512]{1,0:T(8,128)(2,1)S(1)}, u32[]{:S(2)}, u32[]{:S(2)}) collective-permute-start(bf16[128,512]{1,0:T(8,128)(2,1)S(1)} %fusion.3), channel_id=1, source_target_pairs={{0,128},{16,144},{32,160},{48,176},{64,192},{80,208},{96,224},{112... | collective-permute-start | bytes 393224 | tf_op jit(solution)/shard_map/ppermute | solution.py:285
  39.4 14.1 %collective-permute-start.4 = (bf16[128,512]{1,0:T(8,128)(2,1)S(1)}, bf16[128,512]{1,0:T(8,128)(2,1)S(1)}, u32[]{:S(2)}, u32[]{:S(2)}) collective-permute-start(bf16[128,512]{1,0:T(8,128)(2,1)S(1)} %get-tuple-element.21), channel_id=1, source_target_pairs={{0,32},{16,48},{32,0},{48,16},{64,96},{80,112},{96,64},{112,80},{1... | collective-permute-start | bytes 393224 | tf_op jit(solution)/shard_map/ppermute | solution.py:285
  46.6 8.1 %collective-permute-start.3 = (bf16[64,512]{1,0:T(8,128)(2,1)S(1)}, bf16[64,512]{1,0:T(8,128)(2,1)S(1)}, u32[]{:S(2)}, u32[]{:S(2)}) collective-permute-start(bf16[64,512]{1,0:T(8,128)(2,1)S(1)} %shard_map.106), channel_id=1, source_target_pairs={{0,16},{16,32},{32,48},{48,64},{64,80},{80,96},{96,112},{112,128},... | collective-permute-start | bytes 196616 | tf_op jit(solution)/shard_map/ppermute | solution.py:323
  55.8 34.3 %all-to-all-start.1 = ((bf16[16,64,512]{2,1,0:T(8,128)(2,1)}), bf16[16,64,512]{2,1,0:T(8,128)(2,1)S(1)}, u32[]{:S(2)}, u32[]{:S(2)}) async-start(bf16[16,64,512]{2,1,0:T(8,128)(2,1)} %shard_map.107), calls=%async_computation.1 | async-start | bytes 2097152 | tf_op jit(solution)/shard_map/all_to_all | solution.py:271
  60.9 9.9 %collective-permute-start.5 = (bf16[128,512]{1,0:T(8,128)(2,1)S(1)}, bf16[128,512]{1,0:T(8,128)(2,1)S(1)}, u32[]{:S(2)}, u32[]{:S(2)}) collective-permute-start(bf16[128,512]{1,0:T(8,128)(2,1)S(1)} %get-tuple-element.19), channel_id=1, source_target_pairs={{0,256},{16,272},{32,288},{48,304},{64,320},{80,336},{96,352},{112... | collective-permute-start | bytes 393224 | tf_op jit(solution)/shard_map/ppermute | solution.py:285
  71.8 6.5 %collective-permute-start.6 = (bf16[128,512]{1,0:T(8,128)(2,1)S(1)}, bf16[128,512]{1,0:T(8,128)(2,1)S(1)}, u32[]{:S(2)}, u32[]{:S(2)}) collective-permute-start(bf16[128,512]{1,0:T(8,128)(2,1)S(1)} %fusion.2), channel_id=1, source_target_pairs={{0,64},{16,80},{32,96},{48,112},{64,0},{80,16},{96,32},{112,48},{1... | collective-permute-start | bytes 393224 | tf_op jit(solution)/shard_map/ppermute | solution.py:285
  78.3 11.0 %collective-permute-start.7 = (bf16[256,512]{1,0:T(8,128)(2,1)S(1)}, bf16[256,512]{1,0:T(8,128)(2,1)S(1)}, u32[]{:S(2)}, u32[]{:S(2)}) collective-permute-start(bf16[256,512]{1,0:T(8,128)(2,1)S(1)} %maximum_select_fusion.mine_ref), channel_id=1, source_target_pairs={{0,16},{16,0},{32,48},{48,32},{64,80},{80,64},{96,112},{112,96},{1... | collective-permute-start | bytes 786440 | tf_op jit(solution)/shard_map/ppermute | solution.py:285
